TPU v7x, 32 devices: a whole 2x2x4 slice. The times are simulated.
32 devices in a mesh: groups: 2 (over x), gx: 4 (over y, core), gy: 4 (over z).
Axes of the slice: x: 2, y: 2, z: 4, core: 2. Of those that a mesh axis runs over, the one named last changes fastest.
Arguments:
- stay_feats: bfloat16 [16, 4, 4, 12288], P(None, 'gx', 'gy', 'groups'), parts along dimension 3, may hold values from -6 to 6
- stay_slots: int32 [4, 4, 12288], P('gx', 'gy', 'groups'), parts along dimension 2, may hold values from 0 to 32767, as said below
- move_feats: bfloat16 [16, 4, 4, 8, 1024], P(None, 'gx', 'gy', None, 'groups'), parts along dimension 4, may hold values from -6 to 6
- move_slots: int32 [4, 4, 8, 1024], P('gx', 'gy', None, 'groups'), parts along dimension 3, may hold values from 0 to 32767, as said below
- move_counts: int32 [4, 4, 16], P('gx', 'gy', 'groups'), parts along dimension 2, may hold values from 85 to 512
- encoder: bfloat16 [32, 16], replicated, may hold values from -1.5 to 1.5
- conv_weights: bfloat16 [3, 32, 864], replicated, may hold values from -0.21875 to 0.21875
- conv_biases: float32 [3, 32], replicated, may hold values from -3 to 3
- decoder: bfloat16 [3, 32], replicated, may hold values from -1 to 1
- self_weight: bfloat16 [3, 16], replicated, may hold values from -1.5 to 1.5
Outputs:
- velocity: float32 [3, 4, 4, 20480], P(None, 'gx', 'gy', 'groups'), parts along dimension 3
There are 2 independent parts, one for each index of `groups`. A program takes and returns all parts, laid end to end along the dimension named above; an argument that names none is the same for every part. Nothing has to cross between parts.
Inputs may be any that keep to these rules, and one draw needn't show every extreme that they name: `stay_slots`: A slot s of a device belongs to its local cell s mod 8192. On each device the slots of its staying rows and of all rows sent to it by its eight neighbours are distinct. `move_slots`: slots at the destination device, distinct there together with its staying rows.
All inputs are finite; a program needn't handle non-finite values.
Results may differ from a plain program's by a relative error of at most 0.0055.
Values may be sent and summed in bfloat16 or wider, within the bound.
No kernel may reach another device: no remote copies, remote signals or barrier semaphores. Data moves between devices by JAX's collectives and lax.ppermute only.
A program may use at most 64 MiB of HBM per device.

v0:
```python
import jax
import jax.numpy as jnp
from jax import lax
from jax.sharding import PartitionSpec as P

Z = 8
SLOT_CELL = 4
CX = 8
CY = 128


def passed_along(x, axis, by):
    length = lax.axis_size(axis)
    return lax.ppermute(x, axis, [(i, (i + by) % length) for i in range(length)])


def as_sent(x):

    def short(part):
        return part.astype(jnp.bfloat16) if part.dtype == jnp.float32 else part

    return jax.tree.map(short, x)


def extended(cells, sides, width):
    for axis, dim in sides:
        count = lax.axis_size(axis)
        head = lax.slice_in_dim(cells, 0, width, axis=dim)
        tail = lax.slice_in_dim(cells, cells.shape[dim] - width, cells.shape[dim], axis=dim)
        cells = jnp.concatenate(
            [
                lax.ppermute(tail, axis, [(i, (i + 1) % count) for i in range(count)]),
                cells,
                lax.ppermute(head, axis, [((i + 1) % count, i) for i in range(count)]),
            ],
            axis=dim,
        )
    return cells


def stack_buckets(feat_list, slot_list):
    return (jnp.stack(feat_list, 1), jnp.stack(slot_list, 0))


def local_means(feature_rows, slot_rows, slot_total, cell_total):
    feat_dim = feature_rows.shape[0]
    placed = (
        jnp.zeros((feat_dim, slot_total), feature_rows.dtype)
        .at[:, slot_rows]
        .set(feature_rows, mode="drop")
    )
    filled = jnp.zeros((slot_total,), jnp.float32).at[slot_rows].set(1.0, mode="drop")
    summed = jnp.sum(
        placed.reshape(feat_dim, slot_total // cell_total, cell_total).astype(jnp.float32), axis=1
    )
    occupied = jnp.sum(filled.reshape(slot_total // cell_total, cell_total), axis=0)
    return (summed / jnp.maximum(occupied, 1.0)).astype(jnp.bfloat16)


def conv_layer(volume, weight, width_x, width_y):
    layer_count = volume.shape[0]
    padded = jnp.pad(volume, ((1, 1), (0, 0), (0, 0), (0, 0)))

    def one_block(z_start):
        window = lax.dynamic_slice_in_dim(padded, z_start, 4, 0)
        pieces = []
        for depth_off in range(3):
            for x_off in range(3):
                for y_off in range(3):
                    pieces.append(
                        window[
                            depth_off : depth_off + 2,
                            :,
                            x_off : x_off + width_x,
                            y_off : y_off + width_y,
                        ]
                    )
        columns = jnp.concatenate(pieces, 1)
        flat_columns = columns.reshape(2, columns.shape[1], width_x * width_y)
        return jnp.einsum("ok,zkp->zop", weight, flat_columns, preferred_element_type=jnp.float32)

    blocks = lax.map(one_block, jnp.arange(layer_count // 2, dtype=jnp.int32) * 2)
    return blocks.reshape(layer_count, weight.shape[0], width_x, width_y)


def on_device(
    stay_feats,
    stay_slots,
    move_feats,
    move_slots,
    move_counts,
    encoder,
    conv_weights,
    conv_biases,
    decoder,
    self_weight,
):
    feat_dim = stay_feats.shape[0]
    stay_count = stay_feats.shape[3]
    capacity = move_feats.shape[4]
    channels = encoder.shape[0]
    cell_total = Z * CX * CY
    slot_total = SLOT_CELL * cell_total
    own_feats = stay_feats.reshape(feat_dim, stay_count)
    own_slots = stay_slots.reshape(stay_count)
    bucket_feats = move_feats.reshape(feat_dim, 8, capacity)
    live_rows = jnp.arange(capacity, dtype=jnp.int32)[None, :] < move_counts.reshape(8)[:, None]
    bucket_slots = jnp.where(live_rows, move_slots.reshape(8, capacity), jnp.int32(slot_total))
    west_in = passed_along((bucket_feats[:, 0:3], bucket_slots[0:3]), "gx", -1)
    east_in = passed_along((bucket_feats[:, 5:8], bucket_slots[5:8]), "gx", 1)
    lowered = passed_along(
        as_sent(
            stack_buckets(
                [west_in[0][:, 0], bucket_feats[:, 3], east_in[0][:, 0]],
                [west_in[1][0], bucket_slots[3], east_in[1][0]],
            )
        ),
        "gy",
        -1,
    )
    raised = passed_along(
        as_sent(
            stack_buckets(
                [west_in[0][:, 2], bucket_feats[:, 4], east_in[0][:, 2]],
                [west_in[1][2], bucket_slots[4], east_in[1][2]],
            )
        ),
        "gy",
        1,
    )
    arrived = [
        (lowered, 0),
        (west_in, 1),
        (raised, 0),
        (lowered, 1),
        (raised, 1),
        (lowered, 2),
        (east_in, 1),
        (raised, 2),
    ]
    held_feats = jnp.concatenate(
        [own_feats] + [source[0][:, place] for source, place in arrived], 1
    )
    held_slots = jnp.concatenate([own_slots] + [source[1][place] for source, place in arrived], 0)
    cell_mean = local_means(held_feats, held_slots, slot_total, cell_total).reshape(
        feat_dim, Z, CX, CY
    )
    grid_in = jnp.einsum(
        "cf,fzxy->zcxy", encoder, cell_mean, preferred_element_type=jnp.float32
    ).astype(jnp.bfloat16)

    def activate(summed, layer):
        return jax.nn.gelu(summed + conv_biases[layer][None, :, None, None]).astype(jnp.bfloat16)

    def widened(volume):
        return extended(volume, (("gx", 2), ("gy", 3)), 1)

    hidden_one = activate(conv_layer(widened(grid_in), conv_weights[0], CX, CY), 0)
    hidden_two = activate(conv_layer(widened(hidden_one), conv_weights[1], CX, CY), 1)
    last_sum = conv_layer(widened(hidden_two), conv_weights[2], CX, CY)
    grid_out = (
        last_sum + conv_biases[2][None, :, None, None] + grid_in.astype(jnp.float32)
    ).astype(jnp.bfloat16)
    flat_out = grid_out.transpose(1, 0, 2, 3).reshape(channels, cell_total)
    picked = jnp.take(flat_out, held_slots % cell_total, axis=1)
    moving = jnp.dot(decoder, picked, preferred_element_type=jnp.float32)
    moving = moving + jnp.dot(self_weight, held_feats, preferred_element_type=jnp.float32)
    moving = jnp.where(held_slots[None, :] < slot_total, moving, jnp.zeros_like(moving))
    return moving.reshape(3, 1, 1, held_slots.shape[0])


def solution(mesh):
    placed = (
        P(None, "gx", "gy", "groups"),
        P("gx", "gy", "groups"),
        P(None, "gx", "gy", None, "groups"),
        P("gx", "gy", None, "groups"),
        P("gx", "gy", "groups"),
        P(),
        P(),
        P(),
        P(),
        P(),
    )
    return jax.shard_map(
        on_device,
        mesh=mesh,
        in_specs=placed,
        out_specs=P(None, "gx", "gy", "groups"),
        check_vma=False,
    )
```

profile of v0, /device:TPU:0, one launch (start us, length us, event | category | flops | bytes accessed | tf_op | source)
XLA Modules:
  0.0 627.3 jit_solution(8771275527013593866)
XLA Ops:
  21.0 38.0 %scatter_custom_fusion.1 = f32[32768]{0:T(1024)S(1)} fusion(s32[10240]{0:T(1024)S(1)} %bitcast.204, f32[10240]{0:T(1024)S(1)} %broadcast.138, f32[]{:T(128)} %constant.52.clone.1), kind=kCustom, calls=%fused_computation.241 | custom fusion | bytes 131076 | tf_op jit(solution)/shard_map/scatter | solution.py:52
  67.2 31.0 %scatter_custom_fusion = bf16[16,32768]{0,1:T(8,128)(2,1)} fusion(s32[10240]{0:T(1024)S(1)} %bitcast.205, bf16[10240,16]{1,0:T(8,128)(2,1)S(1)} %copy.92, bf16[]{:T(256)} %constant.54.clone.1), kind=kCustom, calls=%fused_computation.178 | custom fusion | bytes 1048578 | tf_op jit(solution)/shard_map/scatter | solution.py:50
  98.3 7.6 %convert_reduce_fusion = f32[16,8192]{0,1:T(8,128)} fusion(bf16[16,4,8192]{0,2,1:T(8,128)(2,1)} %bitcast.190), kind=kLoop, calls=%fused_computation.174 | loop fusion | flops 917504 | bytes 1572864 | tf_op jit(solution)/shard_map/reduce_sum | solution.py:53
  124.1 138.6 %while.30 = (s32[]{:T(128)}, f32[4,2,32,1024]{3,2,1,0:T(8,128)}, s32[4]{0:T(128)}, bf16[10,32,10,130]{3,1,2,0:T(8,128)(2,1)}, bf16[32,864]{1,0:T(8,128)(2,1)}, /...) while((s32[]{:T(128)}, f32[4,2,32,1024]{3,2,1,0:T(8,128)}, s32[4]{0:T(128)}, ...), condition=%wide.region_5.6_spmd, body=%wide.region_4.5_spmd.sunk | while | flops 113246216 | bytes 25092824 | solution.py:82
  127.3 4.7 constant_dynamic-slice_fusion.84
  151.3 5.0 reshape.905
  161.8 4.9 constant_dynamic-slice_fusion.84
  185.9 5.0 reshape.905
  196.4 4.7 constant_dynamic-slice_fusion.84
  220.4 5.0 reshape.905
  230.9 5.3 constant_dynamic-slice_fusion.84
  255.4 5.0 reshape.905
  282.5 138.3 %while.31 = (s32[]{:T(128)}, f32[4,2,32,1024]{3,2,1,0:T(8,128)}, s32[4]{0:T(128)}, bf16[10,32,10,130]{3,1,2,0:T(8,128)(2,1)}, bf16[32,864]{1,0:T(8,128)(2,1)}, /...) while((s32[]{:T(128)}, f32[4,2,32,1024]{3,2,1,0:T(8,128)}, s32[4]{0:T(128)}, ...), condition=%wide.region_7.8_spmd, body=%wide.region_6.7_spmd.sunk | while | flops 113246216 | bytes 25092824 | solution.py:82
  285.7 4.7 constant_dynamic-slice_fusion.85
  309.6 5.0 reshape.906
  320.1 4.9 constant_dynamic-slice_fusion.85
  344.2 5.0 reshape.906
  354.6 4.7 constant_dynamic-slice_fusion.85
  378.6 5.0 reshape.906
  389.0 5.3 constant_dynamic-slice_fusion.85
  413.6 5.0 reshape.906
  440.4 138.6 %while.32 = (s32[]{:T(128)}, f32[4,2,32,1024]{3,2,1,0:T(8,128)}, s32[4]{0:T(128)}, bf16[10,32,10,130]{3,1,2,0:T(8,128)(2,1)}, bf16[32,864]{1,0:T(8,128)(2,1)}, /...) while((s32[]{:T(128)}, f32[4,2,32,1024]{3,2,1,0:T(8,128)}, s32[4]{0:T(128)}, ...), condition=%wide.region_9.10_spmd, body=%wide.region_8.9_spmd.sunk | while | flops 113246216 | bytes 25092824 | solution.py:82
  443.6 4.7 constant_dynamic-slice_fusion.86
  467.5 5.0 reshape.907
  478.0 4.9 constant_dynamic-slice_fusion.86
  502.2 5.0 reshape.907
  512.7 4.7 constant_dynamic-slice_fusion.86
  536.6 5.0 reshape.907
  547.1 5.3 constant_dynamic-slice_fusion.86
  571.7 5.0 reshape.907
  582.9 36.5 %gather_fusion = bf16[10240,32]{1,0:T(8,128)(2,1)} fusion(bf16[32,8192]{0,1:T(8,128)(2,1)S(1)} %bitcast.191, s32[10240]{0:T(1024)S(1)} %copy-done.5), kind=kCustom, calls=%fused_computation | custom fusion | bytes 1351680 | tf_op jit(solution)/shard_map/jit(_take)/gather | solution.py:165
  619.3 6.6 %fusion.9 = f32[10240,3]{0,1:T(4,128)S(1)} fusion(bf16[3,32]{1,0:T(4,128)(2,1)S(1)} %copy-done.13, bf16[10240,32]{1,0:T(8,128)(2,1)} %gather_fusion, pred[10240]{0:T(1024)(128)(4,1)S(1)} %copy-done.8), kind=kOutput, calls=%fused_computation.181 | convolution fusion | flops 2293760 | bytes 788672 | tf_op jit(solution)/shard_map/dot_general | solution.py:166
  (511 shorter events, 364.3 us)
Async XLA Ops:
  0.0 108.8 %copy-start = (bf16[32,16]{0,1:T(8,128)(2,1)S(1)}, bf16[32,16]{0,1:T(8,128)(2,1)}, u32[]{:S(2)}) copy-start(bf16[32,16]{0,1:T(8,128)(2,1)} %param.21) | copy-start | bytes 3076
  0.8 10.2 %collective-permute-start.1 = (s32[3,512]{1,0:T(4,128)S(1)}, s32[3,512]{1,0:T(4,128)S(1)}, u32[]{:S(2)}, u32[]{:S(2)}) collective-permute-start(s32[3,512]{1,0:T(4,128)S(1)} %get-tuple-element.300), channel_id=1, source_target_pairs={{0,4},{4,8},{8,12},{12,0},{1,5},{5,9},{9,13},{13,1},{2,6},{6,10},{... | collective-permute-start | bytes 18440 | tf_op jit(solution)/shard_map/ppermute | solution.py:14
  1.3 9.7 %collective-permute-start = (s32[3,512]{1,0:T(4,128)S(1)}, s32[3,512]{1,0:T(4,128)S(1)}, u32[]{:S(2)}, u32[]{:S(2)}) collective-permute-start(s32[3,512]{1,0:T(4,128)S(1)} %get-tuple-element.299), channel_id=1, source_target_pairs={{0,12},{4,0},{8,4},{12,8},{1,13},{5,1},{9,5},{13,9},{2,14},{6,2},{... | collective-permute-start | bytes 18440 | tf_op jit(solution)/shard_map/ppermute | solution.py:14
  4.3 55.6 %collective-permute-start.4 = (bf16[16,3,512]{2,0,1:T(8,128)(2,1)S(1)}, bf16[16,3,512]{2,0,1:T(8,128)(2,1)S(1)}, u32[]{:S(2)}, u32[]{:S(2)}) collective-permute-start(bf16[16,3,512]{2,0,1:T(8,128)(2,1)S(1)} %get-tuple-element.287), channel_id=1, source_target_pairs={{0,12},{4,0},{8,4},{12,8},{1,13},{5,1},{9,5},{13,9},{2,14},{6,2},{... | collective-permute-start | bytes 147464 | tf_op jit(solution)/shard_map/ppermute | solution.py:14
  5.0 54.9 %collective-permute-start.5 = (bf16[16,3,512]{2,0,1:T(8,128)(2,1)S(1)}, bf16[16,3,512]{2,0,1:T(8,128)(2,1)S(1)}, u32[]{:S(2)}, u32[]{:S(2)}) collective-permute-start(bf16[16,3,512]{2,0,1:T(8,128)(2,1)S(1)} %get-tuple-element.288), channel_id=1, source_target_pairs={{0,4},{4,8},{8,12},{12,0},{1,5},{5,9},{9,13},{13,1},{2,6},{6,10},{... | collective-permute-start | bytes 147464 | tf_op jit(solution)/shard_map/ppermute | solution.py:14
  11.0 5.6 collective-permute-start.2
  15.2 5.5 collective-permute-start.3
  59.9 4.1 collective-permute-start.6
  60.0 5.9 collective-permute-start.7
  66.0 32.3 %copy-start.3 = (bf16[16,10240]{1,0:T(8,128)(2,1)}, bf16[16,10240]{1,0:T(8,128)(2,1)S(1)}, u32[]{:S(2)}) copy-start(bf16[16,10240]{1,0:T(8,128)(2,1)S(1)} %constant_dynamic-update-slice_fusion.10) | copy-start | bytes 983044
  109.2 13.9 %copy-start.2 = (bf16[8,32,8,128]{3,1,2,0:T(8,128)(2,1)}, bf16[8,32,8,128]{3,1,2,0:T(8,128)(2,1)S(1)}, u32[]{:S(2)}) copy-start(bf16[8,32,8,128]{3,1,2,0:T(8,128)(2,1)S(1)} %fusion.27) | copy-start | bytes 1572868
  109.2 3.9 collective-permute-start.8
  109.4 3.7 collective-permute-start.9
  114.0 5.6 collective-permute-start.10
  114.8 5.4 collective-permute-start.11
  118.4 5.7 copy-start.6
  124.1 140.0 %copy-start.11 = (f32[32]{0:T(128)S(1)}, f32[32]{0:T(128)}, u32[]{:S(2)}) copy-start(f32[32]{0:T(128)} %get-tuple-element.314) | copy-start | bytes 388
  264.9 4.4 collective-permute-start.12
  265.5 4.2 collective-permute-start.13
  271.8 6.5 %collective-permute-start.14 = (bf16[8,32,10,1]{1,0,3,2:T(8,128)(2,1)S(1)}, bf16[8,32,10,1]{1,0,3,2:T(8,128)(2,1)S(1)}, u32[]{:S(2)}, u32[]{:S(2)}) collective-permute-start(bf16[8,32,10,1]{1,0,3,2:T(8,128)(2,1)S(1)} %copy.100), channel_id=1, source_target_pairs={{0,1},{1,2},{2,3},{3,0},{4,5},{5,6},{6,7},{7,4},{8,9},{9,10},{10,1... | collective-permute-start | bytes 15368 | tf_op jit(solution)/shard_map/ppermute | solution.py:32
  272.7 6.1 collective-permute-start.15
  282.5 139.8 %copy-start.10 = (f32[32]{0:T(128)S(1)}, f32[32]{0:T(128)}, u32[]{:S(2)}) copy-start(f32[32]{0:T(128)} %get-tuple-element.315) | copy-start | bytes 388
  423.0 4.4 collective-permute-start.16
  424.0 4.1 collective-permute-start.17
  430.1 5.9 collective-permute-start.18
  431.9 4.8 collective-permute-start.19
  440.4 140.0 %copy-start.9 = (f32[32]{0:T(128)S(1)}, f32[32]{0:T(128)}, u32[]{:S(2)}) copy-start(f32[32]{0:T(128)} %get-tuple-element.313) | copy-start | bytes 388
  582.8 36.5 %copy-start.8 = (pred[10240]{0:T(1024)(128)(4,1)S(1)}, pred[10240]{0:T(1024)(128)(4,1)}, u32[]{:S(2)}) copy-start(pred[10240]{0:T(1024)(128)(4,1)} %get-tuple-element.294) | copy-start | bytes 30724
  582.8 36.5 %copy-start.13 = (bf16[3,32]{1,0:T(4,128)(2,1)S(1)}, bf16[3,32]{1,0:T(4,128)(2,1)}, u32[]{:S(2)}) copy-start(bf16[3,32]{1,0:T(4,128)(2,1)} %param.24) | copy-start | bytes 580
  582.8 44.0 %copy-start.1 = (bf16[32,16]{0,1:T(8,128)(2,1)S(1)}, bf16[32,16]{0,1:T(8,128)(2,1)}, u32[]{:S(2)}) copy-start(bf16[32,16]{0,1:T(8,128)(2,1)} %param.21) | copy-start | bytes 3076
  619.3 6.6 %copy-start.4 = (bf16[16,10240]{1,0:T(8,128)(2,1)S(1)}, bf16[16,10240]{1,0:T(8,128)(2,1)}, u32[]{:S(2)}) copy-start(bf16[16,10240]{1,0:T(8,128)(2,1)} %copy-done.3) | copy-start | bytes 983044
  619.3 6.6 %copy-start.12 = (bf16[3,16]{1,0:T(4,128)(2,1)S(1)}, bf16[3,16]{1,0:T(4,128)(2,1)}, u32[]{:S(2)}) copy-start(bf16[3,16]{1,0:T(4,128)(2,1)} %param.25) | copy-start | bytes 292
  (2 other events, 7.8 us)
where the time goes:
time: 639 us; the launch traced here: 627 us
  local copies, waits for them, and re-layouts  504 us (79%)
  matrix products  34.2 us (5%)
  starting transfers between devices  27.3 us (4%)
  loops' own time  22.9 us (4%)
  other arithmetic  20.5 us (3%)
  waiting for transfers between devices  17.5 us (3%)
    while x312, local copies, waits for them, and re-layouts  222 us
    reshape x12, local copies, waits for them, and re-layouts, one_block(): flat_columns = columns.reshape(2, columns.shape[1], width_x * width_y)  60.5 us
    slice x12, local copies, waits for them, and re-layouts, one_block(): window[depth_off:depth_off + 2, :, x_off:x_off + width_x, y_off:y_off + w...  59.1 us
    scatter x1, local copies, waits for them, and re-layouts, local_means(): jnp.zeros((slot_total,), jnp.float32).at[slot_rows].set(1.0, mode='drop')  38 us
    gather x1, local copies, waits for them, and re-layouts, on_device(): picked = jnp.take(flat_out, held_slots % cell_total, axis=1)  36.5 us
    scatter x1, local copies, waits for them, and re-layouts, local_means(): placed = jnp.zeros((feat_dim, slot_total), feature_rows.dtype).at[:, slot...  31 us
    dot_general x12, matrix products, one_block(): jnp.einsum('ok,zkp->zop', weight, flat_columns, preferred_element_type=jn...  27.1 us
    another operation x3, loops' own time, conv_layer(): lax.map(one_block, jnp.arange(layer_count // 2, dtype=jnp.int32) * 2)  22.9 us
  transfers between devices with their start and end apart: 20, of which 11 were waited for; matrix products, arithmetic and copies ran while one was open for 9% of the time, Pallas kernels for 0%

commit v1 on v0

v1 whole, which is shorter than its diff:
```python
import functools

import jax
import jax.numpy as jnp
from jax import lax
from jax.experimental import pallas as pl
from jax.experimental.pallas import tpu as pltpu
from jax.sharding import PartitionSpec as P

Z = 8
CX = 8
CY = 128
CELLS = Z * CX * CY
LO = 2 * CY
HI = CELLS // LO
DEAD = 2 * HI
HALO = 3
SIDE = 8
PITCH = CY + 2 * SIDE
BF = jnp.bfloat16
F32 = jnp.float32
NT = (((1,), (1,)), ((), ()))
NN = (((1,), (0,)), ((), ()))


def cell_codes(slots):
    cell = slots & (CELLS - 1)
    low = cell & (LO - 1)
    zx = cell // LO
    return (zx & (CX // 2 - 1)) * Z + zx // (CX // 2), low


def passed_along(x, axis, by):
    length = lax.axis_size(axis)
    return lax.ppermute(x, axis, [(i, (i + by) % length) for i in range(length)])


def dot(a, b, dims=NN):
    return lax.dot_general(a, b, dims, preferred_element_type=F32)


def vmem():
    return pl.BlockSpec(memory_space=pltpu.VMEM)


def call(kernel, name, outs, scratch, cost, count):
    single = not isinstance(outs, (list, tuple))
    return pl.pallas_call(
        kernel,
        name=name,
        out_shape=outs,
        in_specs=[vmem()] * count,
        out_specs=vmem() if single else [vmem()] * len(outs),
        scratch_shapes=scratch,
        cost_estimate=pl.CostEstimate(flops=cost, bytes_accessed=4 << 20, transcendentals=0),
        compiler_params=pltpu.CompilerParams(vmem_limit_bytes=48 << 20),
    )


def onehot(code, count):
    rows = lax.broadcasted_iota(jnp.int32, (count, code.shape[1]), 0).astype(F32).astype(BF)
    same = rows == jnp.broadcast_to(code, rows.shape)
    return jnp.where(same, jnp.ones_like(rows), jnp.zeros_like(rows))


def scatter_part(feats, high, low):
    spread = jnp.broadcast_to(high, feats.shape)
    zero = jnp.zeros_like(feats)
    parts = [jnp.where(spread == jnp.asarray(h, BF), feats, zero) for h in range(HI)]
    parts.append(onehot(high, HI))
    return dot(jnp.concatenate(parts, 0), onehot(low, LO), NT)


def stay_kernel(feat_ref, slot_ref, sum_ref):
    chunk = 1024
    sum_ref[...] = jnp.zeros_like(sum_ref)

    def body(step, carry):
        at = pl.ds(pl.multiple_of(step * chunk, chunk), chunk)
        high, low = cell_codes(slot_ref[:, at])
        sum_ref[...] += scatter_part(
            feat_ref[:, at], high.astype(F32).astype(BF), low.astype(F32).astype(BF)
        )
        return carry

    lax.fori_loop(0, feat_ref.shape[1] // chunk, body, 0)


def band_kernel(weight_ref, encoder_ref, band_ref, spread_ref, padded):
    layers, chans, width = weight_ref.shape
    taps = 9
    lane = lax.broadcasted_iota(jnp.int32, (chans, 128), 1) // chans
    per = 128 // chans
    padded[:, :, width:] = jnp.zeros((layers, chans, padded.shape[2] - width), F32)
    padded[:, :, :width] = weight_ref[...].astype(F32)

    def one(layer, carry):
        turned = []
        for block in range(padded.shape[2] // 128):
            source = padded[layer, :, block * 128 : (block + 1) * 128]
            turned.append(
                [source if k == 0 else pltpu.roll(source, k * chans, 1) for k in range(per)]
            )
        for out_z in range(Z):
            for tap in range(taps):
                for part in range(Z // per):
                    tile = jnp.zeros((chans, 128), F32)
                    for depth in range(3):
                        in_z = out_z + depth - 1
                        if in_z < 0 or in_z >= Z or in_z // per != part:
                            continue
                        index = depth * taps + tap
                        moved = turned[index // per][(in_z - index) % per]
                        tile = jnp.where(lane == in_z % per, moved, tile)
                    lanes = tap * Z * chans + part * 128
                    band_ref[
                        layer, out_z * chans : (out_z + 1) * chans, lanes : lanes + 128
                    ] = tile.astype(BF)
        return carry

    lax.fori_loop(0, layers, one, 0)
    feat_dim = encoder_ref.shape[1]
    wide = Z * feat_dim
    pick = lax.broadcasted_iota(jnp.int32, (feat_dim, wide), 0)
    column = lax.broadcasted_iota(jnp.int32, (feat_dim, wide), 1) % feat_dim
    tiled = dot(encoder_ref[...], jnp.where(pick == column, 1.0, 0.0).astype(BF))
    group = lax.broadcasted_iota(jnp.int32, (chans, wide), 1) // feat_dim
    for layer in range(Z):
        spread_ref[layer * chans : (layer + 1) * chans, :] = jnp.where(
            group == layer, tiled, 0.0
        ).astype(BF)


def mean_kernel(
    west_ref, east_ref, down_ref, up_ref, part_ref, mean_ref, first_ref, last_ref, held_ref, total
):
    cap = west_ref.shape[1] // 3
    order = [
        (down_ref, 0),
        (west_ref, 1),
        (up_ref, 0),
        (down_ref, 1),
        (up_ref, 1),
        (down_ref, 2),
        (east_ref, 1),
        (up_ref, 2),
    ]
    for place, (ref, which) in enumerate(order):
        held_ref[:, place * cap : (place + 1) * cap] = ref[:, which * cap : (which + 1) * cap]
    total[...] = part_ref[...]
    chunk = 1024
    feat_dim = held_ref.shape[0] - 2

    def body(step, carry):
        at = pl.ds(pl.multiple_of(step * chunk, chunk), chunk)
        rows = held_ref[:, at]
        total[...] += scatter_part(
            rows[:feat_dim], rows[feat_dim : feat_dim + 1], rows[feat_dim + 1 : feat_dim + 2]
        )
        return carry

    lax.fori_loop(0, held_ref.shape[1] // chunk, body, 0)
    inverse = 1.0 / jnp.maximum(total[HI * feat_dim :, :], 1.0)
    for pair in range(CX // 2):
        blocks = []
        for layer in range(Z):
            code = pair * Z + layer
            blocks.append(
                total[code * feat_dim : (code + 1) * feat_dim, :] * inverse[code : code + 1, :]
            )
        block = jnp.concatenate(blocks, 0)
        for odd in range(2):
            x = pair * 2 + odd
            turned = jnp.transpose(block[:, odd * CY : (odd + 1) * CY]).astype(BF)
            mean_ref[x * CY : (x + 1) * CY, :] = turned
            if x < HALO:
                first_ref[x * CY : (x + 1) * CY, :] = turned
            if x >= CX - HALO:
                at = x - (CX - HALO)
                last_ref[at * CY : (at + 1) * CY, :] = turned


def gelu(v):
    inner = 0.7978845608028654 * (v + 0.044715 * (v * v * v))
    return 0.5 * v * (1.0 + jnp.tanh(inner))


def grid_kernel(
    mean_ref,
    before_ref,
    after_ref,
    below_ref,
    above_ref,
    band_ref,
    spread_ref,
    bias_ref,
    decoder_ref,
    grid_ref,
    left,
    right,
    input_one,
    input_two,
    input_three,
    own,
):
    spread = spread_ref[...]
    left[...] = dot(below_ref[...], spread, NT).astype(BF).astype(F32)
    right[...] = dot(above_ref[...], spread, NT).astype(BF).astype(F32)

    def store_shifted(target, x, block, lead, length):
        rows = pl.ds(pl.multiple_of(x * length, length), length)
        for s, by in enumerate((1, 0, block.shape[0] - 1)):
            moved = pltpu.roll(block, by, 0) if by else block
            target[s, rows, :] = moved[lead : lead + length].astype(BF)

    def encode(ref, count, base, keep):
        def body(x, carry):
            rows = pl.ds(pl.multiple_of(x * CY, CY), CY)
            inside = dot(ref[rows, :], spread, NT).astype(BF)
            if keep:
                own[rows, :] = inside
            at = x + base
            side = pl.ds(pl.multiple_of(at * SIDE, SIDE), SIDE)
            block = jnp.concatenate([left[side, :], inside.astype(F32), right[side, :]], 0)
            store_shifted(input_one, at, block, 0, PITCH)
            return carry

        lax.fori_loop(0, count, body, 0)

    encode(before_ref, HALO, 0, False)
    encode(mean_ref, CX, HALO, True)
    encode(after_ref, HALO, HALO + CX, False)

    def conv(source, layer, x, count, length):
        pieces = []
        for q in range(3):
            rows = pl.ds(pl.multiple_of((x + q) * length, length), count * length)
            for s in range(3):
                pieces.append(source[s, rows, :])
        return dot(jnp.concatenate(pieces, 1), band_ref[layer], NT) + bias_ref[layer : layer + 1, :]

    def hidden(source, layer, target, outs, count, lead, length):
        def body(step, carry):
            x = step * count
            value = gelu(conv(source, layer, x, count, PITCH)).astype(BF).astype(F32)
            for k in range(count):
                store_shifted(
                    target, x + k, value[k * PITCH : (k + 1) * PITCH], lead, length
                )
            return carry

        lax.fori_loop(0, outs // count, body, 0)

    hidden(input_one, 0, input_two, CX + 4, 2, 0, PITCH)
    hidden(input_two, 1, input_three, CX + 2, 2, SIDE, CY)

    chans = decoder_ref.shape[1]
    wide = Z * chans
    pick = lax.broadcasted_iota(jnp.int32, (chans, wide), 0)
    column = lax.broadcasted_iota(jnp.int32, (chans, wide), 1) % chans
    tiled = dot(decoder_ref[...], jnp.where(pick == column, 1.0, 0.0).astype(BF))
    group = lax.broadcasted_iota(jnp.int32, (Z, wide), 1) // chans
    level = lax.broadcasted_iota(jnp.int32, (Z, wide), 0)
    decode = jnp.concatenate(
        [jnp.where(group == level, tiled[k : k + 1, :], 0.0) for k in range(3)], 0
    ).astype(BF)

    def last(step, carry):
        rows = pl.ds(pl.multiple_of(step * LO, LO), LO)
        value = conv(input_three, 2, step * 2, 2, CY) + own[rows, :].astype(F32)
        flow = dot(decode, value.astype(BF), NT)
        top = flow.astype(BF)
        grid_ref[0, step] = top
        grid_ref[1, step] = (flow - top.astype(F32)).astype(BF)
        return carry

    lax.fori_loop(0, CX // 2, last, 0)


def pick_rows(table, feats, high, low, self_weight):
    count = feats.shape[1]
    both = dot(table, onehot(low, LO))
    half = both.shape[0] // 2
    values = both[:half] + both[half:]
    level = lax.broadcasted_iota(jnp.int32, (Z, count), 0).astype(F32)
    spread = jnp.broadcast_to(high, (Z, count))
    masks = [spread == (level + float(pair * Z)) for pair in range(CX // 2)]
    live = high < float(DEAD)
    wide = feats.astype(F32)
    rows = []
    for k in range(3):
        total = jnp.zeros((Z, count), F32)
        for pair in range(CX // 2):
            at = (pair * 3 + k) * Z
            total = total + jnp.where(masks[pair], values[at : at + Z], 0.0)
        for part in range(feats.shape[0] // Z):
            part_rows = slice(part * Z, (part + 1) * Z)
            total = total + wide[part_rows] * self_weight[part_rows, k : k + 1]
        rows.append(jnp.where(live, jnp.sum(total, 0, keepdims=True), 0.0))
    return rows


def pick_kernel(grid_ref, feat_ref, slot_ref, held_ref, self_ref, out_ref, table):
    table[...] = grid_ref[...].reshape(table.shape)
    chunk = 1024
    feat_dim, stay = feat_ref.shape
    eye = jnp.where(
        lax.broadcasted_iota(jnp.int32, (feat_dim, feat_dim), 0)
        == lax.broadcasted_iota(jnp.int32, (feat_dim, feat_dim), 1),
        1.0,
        0.0,
    ).astype(BF)
    weight = dot(eye, self_ref[...], NT)

    def staying(step, carry):
        at = pl.ds(pl.multiple_of(step * chunk, chunk), chunk)
        high, low = cell_codes(slot_ref[:, at])
        rows = pick_rows(
            table[...], feat_ref[:, at], high.astype(F32), low.astype(F32).astype(BF), weight
        )
        for k in range(3):
            out_ref[k : k + 1, at] = rows[k]
        return carry

    lax.fori_loop(0, stay // chunk, staying, 0)

    def arrived(step, carry):
        at = pl.ds(pl.multiple_of(step * chunk, chunk), chunk)
        block = held_ref[:, at]
        rows = pick_rows(
            table[...],
            block[:feat_dim],
            block[feat_dim : feat_dim + 1].astype(F32),
            block[feat_dim + 1 : feat_dim + 2],
            weight,
        )
        to = pl.ds(pl.multiple_of(stay + step * chunk, chunk), chunk)
        for k in range(3):
            out_ref[k : k + 1, to] = rows[k]
        return carry

    lax.fori_loop(0, held_ref.shape[1] // chunk, arrived, 0)


def on_device(
    stay_feats,
    stay_slots,
    move_feats,
    move_slots,
    move_counts,
    encoder,
    conv_weights,
    conv_biases,
    decoder,
    self_weight,
):
    feat_dim = stay_feats.shape[0]
    stay = stay_feats.shape[3]
    cap = move_feats.shape[4]
    chans = encoder.shape[0]
    own_feats = stay_feats.reshape(feat_dim, stay)
    own_slots = stay_slots.reshape(1, stay)

    live = jnp.arange(cap, dtype=jnp.int32)[None, :] < move_counts.reshape(8)[:, None]
    high, low = cell_codes(move_slots.reshape(8, cap))
    high = jnp.where(live, high, DEAD)
    codes = jnp.stack([high, low], 0).astype(BF)
    sent = jnp.concatenate([move_feats.reshape(feat_dim, 8, cap), codes], 0)
    sent = sent.reshape(feat_dim + 2, 8 * cap)
    width = feat_dim + 2
    west = passed_along(sent[:, : 3 * cap], "gx", -1)
    east = passed_along(sent[:, 5 * cap :], "gx", 1)
    down = passed_along(
        jnp.concatenate([west[:, :cap], sent[:, 3 * cap : 4 * cap], east[:, :cap]], 1), "gy", -1
    )
    up = passed_along(
        jnp.concatenate(
            [west[:, 2 * cap :], sent[:, 4 * cap : 5 * cap], east[:, 2 * cap :]], 1
        ),
        "gy",
        1,
    )
    sums = jax.ShapeDtypeStruct((HI * (feat_dim + 1), LO), F32)
    part = call(stay_kernel, "stay", sums, [], 5 << 30, 2)(own_feats, own_slots)
    band, spread = call(
        band_kernel,
        "band",
        [
            jax.ShapeDtypeStruct((3, Z * chans, 9 * Z * chans), BF),
            jax.ShapeDtypeStruct((Z * chans, Z * feat_dim), BF),
        ],
        [pltpu.VMEM((3, chans, 7 * 128), F32)],
        2 << 30,
        2,
    )(conv_weights, encoder)
    lanes = Z * feat_dim
    mean, first, last, held = call(
        mean_kernel,
        "mean",
        [
            jax.ShapeDtypeStruct((CX * CY, lanes), BF),
            jax.ShapeDtypeStruct((HALO * CY, lanes), BF),
            jax.ShapeDtypeStruct((HALO * CY, lanes), BF),
            jax.ShapeDtypeStruct((width, 8 * cap), BF),
        ],
        [pltpu.VMEM(sums.shape, F32)],
        3 << 30,
        5,
    )(west, east, down, up, part)
    after = passed_along(first, "gx", -1)
    before = passed_along(last, "gx", 1)

    def edge(start):
        blocks = [
            value.reshape(-1, CY, lanes)[:, start : start + SIDE] for value in (before, mean, after)
        ]
        return jnp.concatenate(blocks, 0).reshape((CX + 2 * HALO) * SIDE, lanes)

    above = passed_along(edge(0), "gy", -1)
    below = passed_along(edge(CY - SIDE), "gy", 1)
    biases = jnp.tile(conv_biases, (1, Z))
    wide = Z * chans
    rows = CX + 2 * HALO
    grid = call(
        grid_kernel,
        "grid",
        jax.ShapeDtypeStruct((2, CX // 2, 3 * Z, LO), BF),
        [
            pltpu.VMEM((rows * SIDE, wide), F32),
            pltpu.VMEM((rows * SIDE, wide), F32),
            pltpu.VMEM((3, rows * PITCH, wide), BF),
            pltpu.VMEM((3, (rows - 2) * PITCH, wide), BF),
            pltpu.VMEM((3, (rows - 4) * CY, wide), BF),
            pltpu.VMEM((CX * CY, wide), BF),
        ],
        8 << 30,
        9,
    )(mean, before, after, below, above, band, spread, biases, decoder)
    out = call(
        pick_kernel,
        "pick",
        jax.ShapeDtypeStruct((3, stay + 8 * cap), F32),
        [pltpu.VMEM((CX * 3 * Z, LO), BF)],
        5 << 30,
        5,
    )(grid, own_feats, own_slots, held, self_weight)
    return out.reshape(3, 1, 1, stay + 8 * cap)


def solution(mesh):
    placed = (
        P(None, "gx", "gy", "groups"),
        P("gx", "gy", "groups"),
        P(None, "gx", "gy", None, "groups"),
        P("gx", "gy", None, "groups"),
        P("gx", "gy", "groups"),
        P(),
        P(),
        P(),
        P(),
        P(),
    )
    return jax.shard_map(
        on_device,
        mesh=mesh,
        in_specs=placed,
        out_specs=P(None, "gx", "gy", "groups"),
        check_vma=False,
    )
```

time: 639 us -> 49.6 us (0.08); the launches traced: 627 us -> 48.7 us
  local copies, waits for them, and re-layouts: 504 us -> 7.5 us
  matrix products: 34.2 us -> 0 us
  loops' own time: 22.9 us -> 0 us
  Pallas kernels: 0 us -> 22.1 us
  other arithmetic: 20.5 us -> 1.01 us
  starting transfers between devices: 27.3 us -> 12.1 us
  waiting for transfers between devices: 17.5 us -> 5.72 us
    while x312 -> x0, local copies, waits for them, and re-layouts: 222 us -> none
    scatter x2 -> x0, local copies, waits for them, and re-layouts: 69 us -> none  [the longest x1 38 us: local_means(): jnp.zeros((slot_total,), jnp.float32).at[slot_rows].set(1.0, mode='drop')]
    slice x34 -> x6, local copies, waits for them, and re-layouts: 65.5 us -> 0.03 us  [the longest x3 0.01 us: edge(): value.reshape(-1, CY, lanes)[:, start:start + SIDE]]
    reshape x15 -> x1, local copies, waits for them, and re-layouts: 62.3 us -> 0.78 us  [on_device(): return out.reshape(3, 1, 1, stay + 8 * cap)]
    gather x1 -> x0, local copies, waits for them, and re-layouts: 36.5 us -> none  [on_device(): picked = jnp.take(flat_out, held_slots % cell_total, axis=1)]
    dot_general x15 -> x0, matrix products: 34.2 us -> none  [the longest x12 27.1 us: one_block(): jnp.einsum('ok,zkp->zop', weight, flat_columns, preferred_element_type=jn...]
    another operation x3 -> x0, loops' own time: 22.9 us -> none  [conv_layer(): lax.map(one_block, jnp.arange(layer_count // 2, dtype=jnp.int32) * 2)]
    pallas_call x0 -> x5, Pallas kernels: none -> 22.1 us  [the longest x1 12.9 us: on_device(): call(grid_kernel, 'grid', jax.ShapeDtypeStruct((2, CX // 2, 3 * Z, LO), B...]
  transfers between devices with their start and end apart: 20 -> 8, of which waited for: 11 -> 4; matrix products, arithmetic and copies ran while one was open for 9% -> 0% of each run, Pallas kernels for 0% -> 8%
where the time goes in v1:
time: 49.6 us; the launch traced here: 48.7 us
  Pallas kernels  22.1 us (45%)
  starting transfers between devices  12.1 us (24%)
  local copies, waits for them, and re-layouts  7.5 us (15%)
  waiting for transfers between devices  5.72 us (12%)
  other arithmetic  1.01 us (2%)
    pallas_call x1, Pallas kernels, on_device(): call(grid_kernel, 'grid', jax.ShapeDtypeStruct((2, CX // 2, 3 * Z, LO), B...  12.9 us
    ppermute x8, starting transfers between devices, passed_along(): lax.ppermute(x, axis, [(i, (i + by) % length) for i in range(length)])  12.1 us
    unnamed x31, local copies, waits for them, and re-layouts  6.61 us
    ppermute x8, waiting for transfers between devices, passed_along(): lax.ppermute(x, axis, [(i, (i + by) % length) for i in range(length)])  5.72 us
    pallas_call x1, Pallas kernels, on_device(): call(pick_kernel, 'pick', jax.ShapeDtypeStruct((3, stay + 8 * cap), F32),...  3.15 us
    pallas_call x1, Pallas kernels, on_device(): part = call(stay_kernel, 'stay', sums, [], 5 << 30, 2)(own_feats, own_slots)  3.06 us
    pallas_call x1, Pallas kernels, on_device(): call(mean_kernel, 'mean', [jax.ShapeDtypeStruct((CX * CY, lanes), BF), ja...  2.2 us
  transfers between devices with their start and end apart: 8, of which 4 were waited for; matrix products, arithmetic and copies ran while one was open for 0% of the time, Pallas kernels for 8%

profile of v1, /device:TPU:0, one launch (start us, length us, event | category | flops | bytes accessed | tf_op | source)
XLA Modules:
  0.0 48.7 jit_solution(12327891848863632694)
XLA Ops:
  0.0 0.7 %and_bitcast_fusion = s32[1,1,8,512]{3,2,1,0:T(8,128)S(1)} fusion(s32[1,1,8,512]{3,2,1,0:T(8,128)} %param.13), kind=kLoop, calls=%fused_computation.26 | loop fusion | flops 4096 | bytes 32768
  0.8 0.1 broadcast_bitcast_fusion
  0.9 0.9 %copy.13 = bf16[2,8,8,512]{3,1,2,0:T(8,128)(2,1)S(1)} copy(bf16[2,8,8,512]{3,2,1,0:T(8,128)(2,1)} %bitcast.37) | data formatting | bytes 262144
  1.8 0.2 fusion.6
  2.1 0.5 %collective-permute-start.1 = (bf16[18,1536]{1,0:T(8,128)(2,1)S(1)}, bf16[18,1536]{1,0:T(8,128)(2,1)S(1)}, u32[]{:S(2)}, u32[]{:S(2)}) collective-permute-start(bf16[18,1536]{1,0:T(8,128)(2,1)S(1)} %get-tuple-element.19), channel_id=1, source_target_pairs={{0,4},{4,8},{8,12},{12,0},{1,5},{5,9},{9,13},{13,1},{2,6},{6,10},{... | collective-permute-start | bytes 165896 | tf_op jit(solution)/shard_map/ppermute | solution.py:35
  2.6 2.0 %collective-permute-start = (bf16[18,1536]{1,0:T(8,128)(2,1)S(1)}, bf16[18,1536]{1,0:T(8,128)(2,1)S(1)}, u32[]{:S(2)}, u32[]{:S(2)}) collective-permute-start(bf16[18,1536]{1,0:T(8,128)(2,1)S(1)} %get-tuple-element.20), channel_id=1, source_target_pairs={{0,12},{4,0},{8,4},{12,8},{1,13},{5,1},{9,5},{13,9},{2,14},{6,2},{... | collective-permute-start | bytes 165896 | tf_op jit(solution)/shard_map/ppermute | solution.py:35
  4.6 2.0 %collective-permute-done.1.east_ref = bf16[18,1536]{1,0:T(8,128)(2,1)S(1)} collective-permute-done((bf16[18,1536]{1,0:T(8,128)(2,1)S(1)}, bf16[18,1536]{1,0:T(8,128)(2,1)S(1)}, u32[]{:S(2)}, u32[]{:S(2)}) %collective-permute-start.1) | collective-permute-done | bytes 55328 | tf_op jit(solution)/shard_map/ppermute | solution.py:35
  6.6 0.6 %collective-permute-done.west_ref = bf16[18,1536]{1,0:T(8,128)(2,1)S(1)} collective-permute-done((bf16[18,1536]{1,0:T(8,128)(2,1)S(1)}, bf16[18,1536]{1,0:T(8,128)(2,1)S(1)}, u32[]{:S(2)}, u32[]{:S(2)}) %collective-permute-start) | collective-permute-done | bytes 55328 | tf_op jit(solution)/shard_map/ppermute | solution.py:35
  7.3 1.8 %collective-permute-start.3 = (bf16[18,1536]{1,0:T(8,128)(2,1)S(1)}, bf16[18,1536]{1,0:T(8,128)(2,1)S(1)}, u32[]{:S(2)}, u32[]{:S(2)}) collective-permute-start(bf16[18,1536]{1,0:T(8,128)(2,1)S(1)} %get-tuple-element.21), channel_id=1, source_target_pairs={{0,1},{1,2},{2,3},{3,0},{4,5},{5,6},{6,7},{7,4},{8,9},{9,10},{10,1... | collective-permute-start | bytes 165896 | tf_op jit(solution)/shard_map/ppermute | solution.py:35
  9.1 2.1 %collective-permute-start.2 = (bf16[18,1536]{1,0:T(8,128)(2,1)S(1)}, bf16[18,1536]{1,0:T(8,128)(2,1)S(1)}, u32[]{:S(2)}, u32[]{:S(2)}) collective-permute-start(bf16[18,1536]{1,0:T(8,128)(2,1)S(1)} %get-tuple-element.22), channel_id=1, source_target_pairs={{0,3},{1,0},{2,1},{3,2},{4,7},{5,4},{6,5},{7,6},{8,11},{9,8},{10,9... | collective-permute-start | bytes 165896 | tf_op jit(solution)/shard_map/ppermute | solution.py:35
  11.2 0.9 %copy-done.1 = bf16[16,1,1,6144]{3,0,2,1:T(8,128)(2,1)S(1)} copy-done((bf16[16,1,1,6144]{3,0,2,1:T(8,128)(2,1)S(1)}, bf16[16,1,1,6144]{3,0,2,1:T(8,128)(2,1)}, u32[]{:S(2)}) %copy-start.1) | copy-done | bytes 196632
  12.1 0.7 %copy-done.4 = s32[1,1,6144]{2,1,0:T(1,128)S(1)} copy-done((s32[1,1,6144]{2,1,0:T(1,128)S(1)}, s32[1,1,6144]{2,1,0:T(1,128)}, u32[]{:S(2)}) %copy-start.4) | copy-done | bytes 24600
  12.8 3.1 %stay.1.part_ref = f32[544,256]{1,0:T(8,128)S(1)} custom-call(bf16[16,6144]{1,0:T(8,128)(2,1)S(1)} %bitcast.31, s32[1,6144]{1,0:T(1,128)S(1)} %bitcast.33), custom_call_target="tpu_custom_call" | custom-call | flops 5368709120 | bytes 4194304 | tf_op jit(solution)/shard_map/stay/pallas_call | solution.py:384
  15.9 0.1 copy.11.encoder_ref
  16.0 0.0 collective-permute-done.3.up_ref
  16.0 2.2 %mean.1 = (bf16[1024,128]{1,0:T(8,128)(2,1)S(1)}, bf16[384,128]{1,0:T(8,128)(2,1)S(1)}, bf16[384,128]{1,0:T(8,128)(2,1)S(1)}, bf16[18,4096]{1,0:T(8,128)(2,1)S(1)}) custom-call(bf16[18,1536]{1,0:T(8,128)(2,1)S(1)} %collective-permute-done.west_ref, bf16[18,1536]{1,0:T(8,128)(2,1)S(1)} %collective-permute-done.1.east_ref, ...), custom_call_target="tpu_custom_call" | custom-call | flops 3221225472 | bytes 4194304 | tf_op jit(solution)/shard_map/mean/pallas_call | solution.py:397
  18.2 1.4 %collective-permute-start.4 = (bf16[384,128]{1,0:T(8,128)(2,1)S(1)}, bf16[384,128]{1,0:T(8,128)(2,1)S(1)}, u32[]{:S(2)}, u32[]{:S(2)}) collective-permute-start(bf16[384,128]{1,0:T(8,128)(2,1)S(1)} %get-tuple-element.12), channel_id=1, source_target_pairs={{0,4},{4,8},{8,12},{12,0},{1,5},{5,9},{9,13},{13,1},{2,6},{6,10},{... | collective-permute-start | bytes 294920 | tf_op jit(solution)/shard_map/ppermute | solution.py:35
  19.6 0.4 collective-permute-start.5
  20.0 2.3 %collective-permute-done.4.before_ref = bf16[384,128]{1,0:T(8,128)(2,1)S(1)} collective-permute-done((bf16[384,128]{1,0:T(8,128)(2,1)S(1)}, bf16[384,128]{1,0:T(8,128)(2,1)S(1)}, u32[]{:S(2)}, u32[]{:S(2)}) %collective-permute-start.4) | collective-permute-done | bytes 98336 | tf_op jit(solution)/shard_map/ppermute | solution.py:35
  22.3 0.8 %collective-permute-done.5.after_ref = bf16[384,128]{1,0:T(8,128)(2,1)S(1)} collective-permute-done((bf16[384,128]{1,0:T(8,128)(2,1)S(1)}, bf16[384,128]{1,0:T(8,128)(2,1)S(1)}, u32[]{:S(2)}, u32[]{:S(2)}) %collective-permute-start.5) | collective-permute-done | bytes 98336 | tf_op jit(solution)/shard_map/ppermute | solution.py:35
  23.2 0.1 collective-permute-start.6
  23.3 0.0 copy-start.11
  23.3 0.0 copy-start.6
  23.3 3.8 %collective-permute-start.7 = (bf16[112,128]{1,0:T(8,128)(2,1)S(1)}, bf16[112,128]{1,0:T(8,128)(2,1)S(1)}, u32[]{:S(2)}, u32[]{:S(2)}) collective-permute-start(bf16[112,128]{1,0:T(8,128)(2,1)S(1)} %maximum_bitcast_fusion.1), channel_id=1, source_target_pairs={{0,3},{1,0},{2,1},{3,2},{4,7},{5,4},{6,5},{7,6},{8,11},{9,8},{10,9... | collective-permute-start | bytes 86024 | tf_op jit(solution)/shard_map/ppermute | solution.py:35
  27.1 0.8 %band.1 = (bf16[3,256,2304]{2,1,0:T(8,128)(2,1)S(1)}, bf16[256,128]{1,0:T(8,128)(2,1)S(1)}) custom-call(bf16[3,32,864]{2,1,0:T(8,128)(2,1)S(1)} %copy-done.3, bf16[32,16]{1,0:T(8,128)(2,1)S(1)} %copy.11.encoder_ref), custom_call_target="tpu_custom_call" | custom-call | flops 2147483648 | bytes 4194304 | tf_op jit(solution)/shard_map/band/pallas_call | solution.py:385
  27.9 1.7 %copy-done.8 = bf16[3,256,2304]{2,1,0:T(8,128)(2,1)} copy-done((bf16[3,256,2304]{2,1,0:T(8,128)(2,1)}, bf16[3,256,2304]{2,1,0:T(8,128)(2,1)S(1)}, u32[]{:S(2)}) %copy-start.8) | copy-done | bytes 3538968
  29.7 0.1 tile.10.bias_ref
  29.8 2.0 %copy-done.9 = bf16[3,256,2304]{2,1,0:T(8,128)(2,1)S(1)} copy-done((bf16[3,256,2304]{2,1,0:T(8,128)(2,1)S(1)}, bf16[3,256,2304]{2,1,0:T(8,128)(2,1)}, u32[]{:S(2)}) %copy-start.9) | copy-done | bytes 3538968
  31.8 12.9 %grid.1.grid_ref = bf16[2,4,24,256]{3,2,1,0:T(8,128)(2,1)S(1)} custom-call(bf16[1024,128]{1,0:T(8,128)(2,1)S(1)} %get-tuple-element.11.mean_ref, bf16[384,128]{1,0:T(8,128)(2,1)S(1)} %collective-permute-done.4.before_ref, bf16[384,128]{1,0:T(8,128)(2,1)S(1)} %collective-permute-done.5.after_ref, bf16[112,128]{1,0:T(8,128)(2,1)S(1)} %collective-permute-done.6.below_ref, ...), custom_call_target="tpu_custom_call" | custom-call | flops 8589934592 | bytes 4194304 | tf_op jit(solution)/shard_map/grid/pallas_call | solution.py:424
  44.7 0.0 copy-done.2
  44.7 3.1 %pick.1 = f32[3,10240]{1,0:T(4,128)S(1)} custom-call(bf16[2,4,24,256]{3,2,1,0:T(8,128)(2,1)S(1)} %grid.1.grid_ref, bf16[16,6144]{1,0:T(8,128)(2,1)S(1)} %bitcast.32, s32[1,6144]{1,0:T(1,128)S(1)} %bitcast.34, bf16[18,4096]{1,0:T(8,128)(2,1)S(1)} %get-tuple-element.16.held_ref, bf16[3,16]{1,0:T(4,128)(2,1)S(1)} %copy-done.7), custom_call_target="tpu_custom_call" | custom-call | flops 5368709120 | bytes 4194304 | tf_op jit(solution)/shard_map/pick/pallas_call | solution.py:439
  47.9 0.8 %copy.12 = f32[3,1,1,10240]{3,2,1,0:T(1,128)} copy(f32[3,1,1,10240]{3,0,2,1:T(4,128)S(1)} %bitcast.27) | data formatting | bytes 245760 | tf_op jit(solution)/shard_map/reshape | solution.py:447
  (35 shorter events, 0.2 us)
Async XLA Ops:
  0.0 0.8 %copy-start = (s32[1,1,8]{2,1,0:T(1,128)S(1)}, s32[1,1,8]{2,1,0:T(1,128)}, u32[]{:S(2)}) copy-start(s32[1,1,8]{2,1,0:T(1,128)} %param.14) | copy-start | bytes 100
  2.1 4.5 %collective-permute-start.1 = (bf16[18,1536]{1,0:T(8,128)(2,1)S(1)}, bf16[18,1536]{1,0:T(8,128)(2,1)S(1)}, u32[]{:S(2)}, u32[]{:S(2)}) collective-permute-start(bf16[18,1536]{1,0:T(8,128)(2,1)S(1)} %get-tuple-element.19), channel_id=1, source_target_pairs={{0,4},{4,8},{8,12},{12,0},{1,5},{5,9},{9,13},{13,1},{2,6},{6,10},{... | collective-permute-start | bytes 165896 | tf_op jit(solution)/shard_map/ppermute | solution.py:35
  2.6 4.6 %collective-permute-start = (bf16[18,1536]{1,0:T(8,128)(2,1)S(1)}, bf16[18,1536]{1,0:T(8,128)(2,1)S(1)}, u32[]{:S(2)}, u32[]{:S(2)}) collective-permute-start(bf16[18,1536]{1,0:T(8,128)(2,1)S(1)} %get-tuple-element.20), channel_id=1, source_target_pairs={{0,12},{4,0},{8,4},{12,8},{1,13},{5,1},{9,5},{13,9},{2,14},{6,2},{... | collective-permute-start | bytes 165896 | tf_op jit(solution)/shard_map/ppermute | solution.py:35
  7.3 8.8 %collective-permute-start.3 = (bf16[18,1536]{1,0:T(8,128)(2,1)S(1)}, bf16[18,1536]{1,0:T(8,128)(2,1)S(1)}, u32[]{:S(2)}, u32[]{:S(2)}) collective-permute-start(bf16[18,1536]{1,0:T(8,128)(2,1)S(1)} %get-tuple-element.21), channel_id=1, source_target_pairs={{0,1},{1,2},{2,3},{3,0},{4,5},{5,6},{6,7},{7,4},{8,9},{9,10},{10,1... | collective-permute-start | bytes 165896 | tf_op jit(solution)/shard_map/ppermute | solution.py:35
  9.1 6.9 %collective-permute-start.2 = (bf16[18,1536]{1,0:T(8,128)(2,1)S(1)}, bf16[18,1536]{1,0:T(8,128)(2,1)S(1)}, u32[]{:S(2)}, u32[]{:S(2)}) collective-permute-start(bf16[18,1536]{1,0:T(8,128)(2,1)S(1)} %get-tuple-element.22), channel_id=1, source_target_pairs={{0,3},{1,0},{2,1},{3,2},{4,7},{5,4},{6,5},{7,6},{8,11},{9,8},{10,9... | collective-permute-start | bytes 165896 | tf_op jit(solution)/shard_map/ppermute | solution.py:35
  11.2 0.9 %copy-start.1 = (bf16[16,1,1,6144]{3,0,2,1:T(8,128)(2,1)S(1)}, bf16[16,1,1,6144]{3,0,2,1:T(8,128)(2,1)}, u32[]{:S(2)}) copy-start(bf16[16,1,1,6144]{3,0,2,1:T(8,128)(2,1)} %param.10) | copy-start | bytes 589828
  12.1 0.7 %copy-start.4 = (s32[1,1,6144]{2,1,0:T(1,128)S(1)}, s32[1,1,6144]{2,1,0:T(1,128)}, u32[]{:S(2)}) copy-start(s32[1,1,6144]{2,1,0:T(1,128)} %param.11) | copy-start | bytes 73732
  12.8 3.1 %copy-start.10 = (bf16[32,16]{0,1:T(8,128)(2,1)S(1)}, bf16[32,16]{0,1:T(8,128)(2,1)}, u32[]{:S(2)}) copy-start(bf16[32,16]{0,1:T(8,128)(2,1)} %param.15) | copy-start | bytes 3076
  16.0 11.1 %copy-start.3 = (bf16[3,32,864]{2,1,0:T(8,128)(2,1)S(1)}, bf16[3,32,864]{2,1,0:T(8,128)(2,1)}, u32[]{:S(2)}) copy-start(bf16[3,32,864]{2,1,0:T(8,128)(2,1)} %weight_ref.1) | copy-start | bytes 497668
  18.2 4.1 %collective-permute-start.4 = (bf16[384,128]{1,0:T(8,128)(2,1)S(1)}, bf16[384,128]{1,0:T(8,128)(2,1)S(1)}, u32[]{:S(2)}, u32[]{:S(2)}) collective-permute-start(bf16[384,128]{1,0:T(8,128)(2,1)S(1)} %get-tuple-element.12), channel_id=1, source_target_pairs={{0,4},{4,8},{8,12},{12,0},{1,5},{5,9},{9,13},{13,1},{2,6},{6,10},{... | collective-permute-start | bytes 294920 | tf_op jit(solution)/shard_map/ppermute | solution.py:35
  19.6 3.6 %collective-permute-start.5 = (bf16[384,128]{1,0:T(8,128)(2,1)S(1)}, bf16[384,128]{1,0:T(8,128)(2,1)S(1)}, u32[]{:S(2)}, u32[]{:S(2)}) collective-permute-start(bf16[384,128]{1,0:T(8,128)(2,1)S(1)} %get-tuple-element.13), channel_id=1, source_target_pairs={{0,12},{4,0},{8,4},{12,8},{1,13},{5,1},{9,5},{13,9},{2,14},{6,2},{... | collective-permute-start | bytes 294920 | tf_op jit(solution)/shard_map/ppermute | solution.py:35
  23.2 6.6 %collective-permute-start.6 = (bf16[112,128]{1,0:T(8,128)(2,1)S(1)}, bf16[112,128]{1,0:T(8,128)(2,1)S(1)}, u32[]{:S(2)}, u32[]{:S(2)}) collective-permute-start(bf16[112,128]{1,0:T(8,128)(2,1)S(1)} %maximum_bitcast_fusion), channel_id=1, source_target_pairs={{0,1},{1,2},{2,3},{3,0},{4,5},{5,6},{6,7},{7,4},{8,9},{9,10},{10,1... | collective-permute-start | bytes 86024 | tf_op jit(solution)/shard_map/ppermute | solution.py:35
  23.3 6.4 %copy-start.11 = (f32[3,32]{1,0:T(4,128)S(1)}, f32[3,32]{1,0:T(4,128)}, u32[]{:S(2)}) copy-start(f32[3,32]{1,0:T(4,128)} %param.17) | copy-start | bytes 1156
  23.3 6.5 %copy-start.6 = (bf16[3,32]{1,0:T(4,128)(2,1)S(1)}, bf16[3,32]{1,0:T(4,128)(2,1)}, u32[]{:S(2)}) copy-start(bf16[3,32]{1,0:T(4,128)(2,1)} %decoder_ref.1) | copy-start | bytes 580
  23.3 6.5 %collective-permute-start.7 = (bf16[112,128]{1,0:T(8,128)(2,1)S(1)}, bf16[112,128]{1,0:T(8,128)(2,1)S(1)}, u32[]{:S(2)}, u32[]{:S(2)}) collective-permute-start(bf16[112,128]{1,0:T(8,128)(2,1)S(1)} %maximum_bitcast_fusion.1), channel_id=1, source_target_pairs={{0,3},{1,0},{2,1},{3,2},{4,7},{5,4},{6,5},{7,6},{8,11},{9,8},{10,9... | collective-permute-start | bytes 86024 | tf_op jit(solution)/shard_map/ppermute | solution.py:35
  27.9 1.7 %copy-start.8 = (bf16[3,256,2304]{2,1,0:T(8,128)(2,1)}, bf16[3,256,2304]{2,1,0:T(8,128)(2,1)S(1)}, u32[]{:S(2)}) copy-start(bf16[3,256,2304]{2,1,0:T(8,128)(2,1)S(1)} %get-tuple-element.14.band_ref) | copy-start | bytes 10616836
  29.8 2.0 %copy-start.9 = (bf16[3,256,2304]{2,1,0:T(8,128)(2,1)S(1)}, bf16[3,256,2304]{2,1,0:T(8,128)(2,1)}, u32[]{:S(2)}) copy-start(bf16[3,256,2304]{2,1,0:T(8,128)(2,1)} %copy-done.8) | copy-start | bytes 10616836
  31.8 12.9 %copy-start.2 = (bf16[16,1,1,6144]{3,0,2,1:T(8,128)(2,1)S(1)}, bf16[16,1,1,6144]{3,0,2,1:T(8,128)(2,1)}, u32[]{:S(2)}) copy-start(bf16[16,1,1,6144]{3,0,2,1:T(8,128)(2,1)} %param.10) | copy-start | bytes 589828
  31.8 12.9 %copy-start.5 = (s32[1,1,6144]{2,1,0:T(1,128)S(1)}, s32[1,1,6144]{2,1,0:T(1,128)}, u32[]{:S(2)}) copy-start(s32[1,1,6144]{2,1,0:T(1,128)} %param.11) | copy-start | bytes 73732
  31.8 12.9 %copy-start.7 = (bf16[3,16]{1,0:T(4,128)(2,1)S(1)}, bf16[3,16]{1,0:T(4,128)(2,1)}, u32[]{:S(2)}) copy-start(bf16[3,16]{1,0:T(4,128)(2,1)} %self_ref.1) | copy-start | bytes 292

commit v2 on v1

v2 whole, which is shorter than its diff:
```python
import functools

import jax
import jax.numpy as jnp
from jax import lax
from jax.experimental import pallas as pl
from jax.experimental.pallas import tpu as pltpu
from jax.sharding import PartitionSpec as P

Z = 8
CX = 8
CY = 128
CELLS = Z * CX * CY
LO = 2 * CY
HI = CELLS // LO
DEAD = 2 * HI
HALO = 3
SIDE = 8
PITCH = CY + 2 * SIDE
BF = jnp.bfloat16
F32 = jnp.float32
NT = (((1,), (1,)), ((), ()))
NN = (((1,), (0,)), ((), ()))


CHUNK = 1024
COUNTS = (4, 5, 4)


def repeat(count, body):
    for step in range(count):
        body(step)


def aligned(start, length):
    return slice(start, start + length)


def cell_codes(slots):
    cell = slots & (CELLS - 1)
    low = cell & (LO - 1)
    zx = cell // LO
    return (zx & (CX // 2 - 1)) * Z + zx // (CX // 2), low


def passed_along(x, axis, by):
    length = lax.axis_size(axis)
    return lax.ppermute(x, axis, [(i, (i + by) % length) for i in range(length)])


def dot(a, b, dims=NN):
    return lax.dot_general(a, b, dims, preferred_element_type=F32)


def vmem():
    return pl.BlockSpec(memory_space=pltpu.VMEM)


def smem():
    return pl.BlockSpec(memory_space=pltpu.SMEM)


def call(kernel, name, ins, outs, scratch, flops, mib):
    return pl.pallas_call(
        kernel,
        name=name,
        out_shape=[jax.ShapeDtypeStruct(*shape) for shape, _ in outs],
        in_specs=ins,
        out_specs=[spec for _, spec in outs],
        scratch_shapes=scratch,
        cost_estimate=pl.CostEstimate(flops=flops, bytes_accessed=1 << 20, transcendentals=0),
        compiler_params=pltpu.CompilerParams(vmem_limit_bytes=mib << 20),
    )


def onehot(code, count):
    rows = lax.broadcasted_iota(jnp.int32, (count, code.shape[1]), 0).astype(F32).astype(BF)
    same = rows == jnp.broadcast_to(code, rows.shape)
    return jnp.where(same, jnp.ones_like(rows), jnp.zeros_like(rows))


def scatter_part(feats, high, low):
    spread = jnp.broadcast_to(high, feats.shape)
    zero = jnp.zeros_like(feats)
    parts = [jnp.where(spread == jnp.asarray(h, BF), feats, zero) for h in range(HI)]
    parts.append(onehot(high, HI))
    return dot(jnp.concatenate(parts, 0), onehot(low, LO), NT)


def pack_kernel(feat_ref, slot_ref, count_ref, west_ref, east_ref, middle_ref):
    feat_dim, buckets, cap = feat_ref.shape
    turned = jnp.swapaxes(feat_ref[...].astype(F32), 0, 1)
    high, low = cell_codes(slot_ref[...])
    lane = lax.broadcasted_iota(jnp.int32, (1, cap), 1)
    high = high.astype(F32)
    low = low.astype(F32)
    for bucket in range(buckets):
        out_ref, place = (
            (west_ref, bucket)
            if bucket < 3
            else (middle_ref, bucket - 3)
            if bucket < 5
            else (east_ref, bucket - 5)
        )
        at = slice(place * cap, (place + 1) * cap)
        code = jnp.where(
            lane < count_ref[bucket], high[bucket : bucket + 1], jnp.full((1, cap), DEAD, F32)
        )
        codes = jnp.concatenate([code, low[bucket : bucket + 1]], 0)
        out_ref[:feat_dim, at] = turned[bucket].astype(BF)
        out_ref[feat_dim:, at] = codes.astype(BF)


def stay_kernel(feat_ref, slot_ref, sum_ref):
    chunk = CHUNK
    sum_ref[...] = jnp.zeros_like(sum_ref)

    def body(step):
        at = aligned(step * chunk, chunk)
        high, low = cell_codes(slot_ref[:, at])
        sum_ref[...] += scatter_part(
            feat_ref[:, at], high.astype(F32).astype(BF), low.astype(F32).astype(BF)
        )

    repeat(feat_ref.shape[1] // chunk, body)


def tiled_rows(small, count):
    width = small.shape[1]
    pick = lax.broadcasted_iota(jnp.int32, (width, count * width), 0)
    column = lax.broadcasted_iota(jnp.int32, (width, count * width), 1) % width
    return dot(small, jnp.where(pick == column, 1.0, 0.0).astype(BF))


def build_spread(encoder):
    chans, feat_dim = encoder.shape
    tiled = tiled_rows(encoder, Z)
    group = lax.broadcasted_iota(jnp.int32, tiled.shape, 1) // feat_dim
    return jnp.concatenate([jnp.where(group == layer, tiled, 0.0) for layer in range(Z)], 0).astype(
        BF
    )


def build_band(weight_ref, layer, band_ref):
    _, chans, width = weight_ref.shape
    taps = 9
    per = 128 // chans
    lane = lax.broadcasted_iota(jnp.int32, (chans, 128), 1) // chans
    weight = weight_ref[layer].astype(F32)
    turned = []
    for start in range(0, width, 128):
        source = weight[:, start : start + 128]
        if source.shape[1] < 128:
            source = jnp.concatenate([source, jnp.zeros((chans, 128 - source.shape[1]), F32)], 1)
        turned.append(
            [(source if k == 0 else pltpu.roll(source, k * chans, 1)).astype(BF) for k in range(per)]
        )
    for out_z in range(Z):
        for tap in range(taps):
            for part in range(Z // per):
                tile = jnp.zeros((chans, 128), BF)
                for depth in range(3):
                    in_z = out_z + depth - 1
                    if in_z < 0 or in_z >= Z or in_z // per != part:
                        continue
                    index = depth * taps + tap
                    moved = turned[index // per][(in_z - index) % per]
                    tile = jnp.where(lane == in_z % per, moved, tile)
                lanes = tap * Z * chans + part * 128
                band_ref[layer, out_z * chans : (out_z + 1) * chans, lanes : lanes + 128] = tile


def mean_kernel(
    west_ref, east_ref, down_ref, up_ref, part_ref, mean_ref, first_ref, last_ref, held_ref, total
):
    cap = west_ref.shape[1] // 3
    order = [
        (down_ref, 0),
        (west_ref, 1),
        (up_ref, 0),
        (down_ref, 1),
        (up_ref, 1),
        (down_ref, 2),
        (east_ref, 1),
        (up_ref, 2),
    ]
    for place, (ref, which) in enumerate(order):
        held_ref[:, place * cap : (place + 1) * cap] = ref[:, which * cap : (which + 1) * cap]
    total[...] = part_ref[...]
    chunk = CHUNK
    feat_dim = held_ref.shape[0] - 2

    def body(step):
        at = aligned(step * chunk, chunk)
        rows = held_ref[:, at]
        total[...] += scatter_part(
            rows[:feat_dim], rows[feat_dim : feat_dim + 1], rows[feat_dim + 1 : feat_dim + 2]
        )

    repeat(held_ref.shape[1] // chunk, body)
    inverse = 1.0 / jnp.maximum(total[HI * feat_dim :, :], 1.0)
    for pair in range(CX // 2):
        blocks = []
        for layer in range(Z):
            code = pair * Z + layer
            blocks.append(
                total[code * feat_dim : (code + 1) * feat_dim, :] * inverse[code : code + 1, :]
            )
        block = jnp.concatenate(blocks, 0)
        for odd in range(2):
            x = pair * 2 + odd
            turned = jnp.transpose(block[:, odd * CY : (odd + 1) * CY]).astype(BF)
            mean_ref[x * CY : (x + 1) * CY, :] = turned
            if x < HALO:
                first_ref[x * CY : (x + 1) * CY, :] = turned
            if x >= CX - HALO:
                at = x - (CX - HALO)
                last_ref[at * CY : (at + 1) * CY, :] = turned


def gelu(v):
    inner = 0.7978845608028654 * (v + 0.044715 * (v * v * v))
    return 0.5 * v * (1.0 + jnp.tanh(inner))


def grid_kernel(
    mean_ref,
    before_ref,
    after_ref,
    below_ref,
    above_ref,
    weight_ref,
    encoder_ref,
    bias_ref,
    decoder_ref,
    grid_ref,
    left,
    right,
    input_one,
    input_two,
    input_three,
    own,
    band_ref,
):
    spread = build_spread(encoder_ref[...])
    left[...] = dot(below_ref[...], spread, NT).astype(BF).astype(F32)
    right[...] = dot(above_ref[...], spread, NT).astype(BF).astype(F32)

    def store_shifted(target, x, block, lead, length):
        rows = aligned(x * length, length)
        for s, by in enumerate((1, 0, block.shape[0] - 1)):
            moved = pltpu.roll(block, by, 0) if by else block
            target[s, rows, :] = moved[lead : lead + length].astype(BF)

    def encode(ref, count, base, keep):
        def body(x):
            rows = aligned(x * CY, CY)
            inside = dot(ref[rows, :], spread, NT).astype(BF)
            if keep:
                own[rows, :] = inside
            at = x + base
            side = aligned(at * SIDE, SIDE)
            block = jnp.concatenate([left[side, :], inside.astype(F32), right[side, :]], 0)
            store_shifted(input_one, at, block, 0, PITCH)

        repeat(count, body)

    encode(before_ref, HALO, 0, False)
    encode(mean_ref, CX, HALO, True)
    encode(after_ref, HALO, HALO + CX, False)

    def conv(source, layer, x, count, length):
        pieces = []
        for q in range(3):
            rows = aligned((x + q) * length, count * length)
            for s in range(3):
                pieces.append(source[s, rows, :])
        return dot(jnp.concatenate(pieces, 1), band_ref[layer], NT) + bias_ref[layer : layer + 1, :]

    def hidden(source, layer, target, outs, count, lead, length):
        def body(step):
            x = step * count
            value = gelu(conv(source, layer, x, count, PITCH)).astype(BF).astype(F32)
            for k in range(count):
                store_shifted(
                    target, x + k, value[k * PITCH : (k + 1) * PITCH], lead, length
                )

        repeat(outs // count, body)

    build_band(weight_ref, 0, band_ref)
    hidden(input_one, 0, input_two, CX + 4, COUNTS[0], 0, PITCH)
    build_band(weight_ref, 1, band_ref)
    hidden(input_two, 1, input_three, CX + 2, COUNTS[1], SIDE, CY)

    chans = decoder_ref.shape[1]
    wide = Z * chans
    tiled = tiled_rows(decoder_ref[...], Z)
    group = lax.broadcasted_iota(jnp.int32, (Z, wide), 1) // chans
    level = lax.broadcasted_iota(jnp.int32, (Z, wide), 0)
    decode = jnp.concatenate(
        [jnp.where(group == level, tiled[k : k + 1, :], 0.0) for k in range(3)], 0
    ).astype(BF)

    def last(step):
        count = COUNTS[2]
        rows = aligned(step * count * CY, count * CY)
        value = conv(input_three, 2, step * count, count, CY) + own[rows, :].astype(F32)
        flow = dot(decode, value.astype(BF), NT)
        top = flow.astype(BF)
        low = (flow - top.astype(F32)).astype(BF)
        for pair in range(count // 2):
            lanes = slice(pair * LO, (pair + 1) * LO)
            grid_ref[0, step * (count // 2) + pair] = top[:, lanes]
            grid_ref[1, step * (count // 2) + pair] = low[:, lanes]

    build_band(weight_ref, 2, band_ref)
    repeat(CX // COUNTS[2], last)


def pick_rows(table, feats, high, low, self_weight):
    count = feats.shape[1]
    both = dot(table, onehot(low, LO))
    half = both.shape[0] // 2
    values = both[:half] + both[half:]
    level = lax.broadcasted_iota(jnp.int32, (Z, count), 0).astype(F32)
    spread = jnp.broadcast_to(high, (Z, count))
    masks = [spread == (level + float(pair * Z)) for pair in range(CX // 2)]
    live = high < float(DEAD)
    wide = feats.astype(F32)
    rows = []
    for k in range(3):
        total = jnp.zeros((Z, count), F32)
        for pair in range(CX // 2):
            at = (pair * 3 + k) * Z
            total = total + jnp.where(masks[pair], values[at : at + Z], 0.0)
        for part in range(feats.shape[0] // Z):
            part_rows = slice(part * Z, (part + 1) * Z)
            total = total + wide[part_rows] * self_weight[part_rows, k : k + 1]
        rows.append(jnp.where(live, jnp.sum(total, 0, keepdims=True), 0.0))
    return rows


def pick_kernel(grid_ref, feat_ref, slot_ref, held_ref, self_ref, out_ref, table):
    table[...] = grid_ref[...].reshape(table.shape)
    chunk = CHUNK
    feat_dim, stay = feat_ref.shape
    eye = jnp.where(
        lax.broadcasted_iota(jnp.int32, (feat_dim, feat_dim), 0)
        == lax.broadcasted_iota(jnp.int32, (feat_dim, feat_dim), 1),
        1.0,
        0.0,
    ).astype(BF)
    weight = dot(eye, self_ref[...], NT)

    def staying(step):
        at = aligned(step * chunk, chunk)
        high, low = cell_codes(slot_ref[:, at])
        rows = pick_rows(
            table[...], feat_ref[:, at], high.astype(F32), low.astype(F32).astype(BF), weight
        )
        for k in range(3):
            out_ref[k, :, at] = rows[k]

    repeat(stay // chunk, staying)

    def arrived(step):
        at = aligned(step * chunk, chunk)
        block = held_ref[:, at]
        rows = pick_rows(
            table[...],
            block[:feat_dim],
            block[feat_dim : feat_dim + 1].astype(F32),
            block[feat_dim + 1 : feat_dim + 2],
            weight,
        )
        to = aligned(stay + step * chunk, chunk)
        for k in range(3):
            out_ref[k, :, to] = rows[k]

    repeat(held_ref.shape[1] // chunk, arrived)


def on_device(
    stay_feats,
    stay_slots,
    move_feats,
    move_slots,
    move_counts,
    encoder,
    conv_weights,
    conv_biases,
    decoder,
    self_weight,
):
    feat_dim = stay_feats.shape[0]
    stay = stay_feats.shape[3]
    cap = move_feats.shape[4]
    chans = encoder.shape[0]
    own_feats = stay_feats.reshape(feat_dim, stay)
    own_slots = stay_slots.reshape(1, stay)

    width = feat_dim + 2
    west, east, middle = call(
        pack_kernel,
        "pack",
        [vmem(), vmem(), smem()],
        [
            (((width, 3 * cap), BF), vmem()),
            (((width, 3 * cap), BF), vmem()),
            (((width, 2 * cap), BF), vmem()),
        ],
        [],
        1 << 20,
        4,
    )(
        move_feats.reshape(feat_dim, 8, cap),
        move_slots.reshape(8, cap),
        move_counts.reshape(8),
    )
    west = passed_along(west, "gx", -1)
    east = passed_along(east, "gx", 1)
    down = passed_along(
        jnp.concatenate([west[:, :cap], middle[:, :cap], east[:, :cap]], 1), "gy", -1
    )
    up = passed_along(
        jnp.concatenate([west[:, 2 * cap :], middle[:, cap:], east[:, 2 * cap :]], 1), "gy", 1
    )
    sums = (HI * (feat_dim + 1), LO)
    (part,) = call(
        stay_kernel, "stay", [vmem(), vmem()], [((sums, F32), vmem())], [], 5 << 30, 8
    )(own_feats, own_slots)
    wide = Z * chans
    lanes = Z * feat_dim
    mean, first, last, held = call(
        mean_kernel,
        "mean",
        [vmem()] * 5,
        [
            (((CX * CY, lanes), BF), vmem()),
            (((HALO * CY, lanes), BF), vmem()),
            (((HALO * CY, lanes), BF), vmem()),
            (((width, 8 * cap), BF), vmem()),
        ],
        [pltpu.VMEM(sums, F32)],
        3 << 30,
        8,
    )(west, east, down, up, part)
    after = passed_along(first, "gx", -1)
    before = passed_along(last, "gx", 1)

    def edge(start):
        blocks = [
            value.reshape(-1, CY, lanes)[:, start : start + SIDE] for value in (before, mean, after)
        ]
        return jnp.concatenate(blocks, 0).reshape((CX + 2 * HALO) * SIDE, lanes)

    above = passed_along(edge(0), "gy", -1)
    below = passed_along(edge(CY - SIDE), "gy", 1)
    biases = jnp.tile(conv_biases, (1, Z))
    rows = CX + 2 * HALO
    (grid,) = call(
        grid_kernel,
        "grid",
        [vmem()] * 9,
        [(((2, CX // 2, 3 * Z, LO), BF), vmem())],
        [
            pltpu.VMEM((rows * SIDE, wide), F32),
            pltpu.VMEM((rows * SIDE, wide), F32),
            pltpu.VMEM((3, rows * PITCH, wide), BF),
            pltpu.VMEM((3, (rows - 2) * PITCH, wide), BF),
            pltpu.VMEM((3, (rows - 4) * CY, wide), BF),
            pltpu.VMEM((CX * CY, wide), BF),
            pltpu.VMEM((3, wide, 9 * wide), BF),
        ],
        8 << 30,
        32,
    )(mean, before, after, below, above, conv_weights, encoder, biases, decoder)
    (out,) = call(
        pick_kernel,
        "pick",
        [vmem()] * 5,
        [(((3, 1, stay + 8 * cap), F32), vmem())],
        [pltpu.VMEM((CX * 3 * Z, LO), BF)],
        5 << 30,
        8,
    )(grid, own_feats, own_slots, held, self_weight)
    return out.reshape(3, 1, 1, stay + 8 * cap)


def solution(mesh):
    placed = (
        P(None, "gx", "gy", "groups"),
        P("gx", "gy", "groups"),
        P(None, "gx", "gy", None, "groups"),
        P("gx", "gy", None, "groups"),
        P("gx", "gy", "groups"),
        P(),
        P(),
        P(),
        P(),
        P(),
    )
    return jax.shard_map(
        on_device,
        mesh=mesh,
        in_specs=placed,
        out_specs=P(None, "gx", "gy", "groups"),
        check_vma=False,
    )
```

time: 49.6 us -> 40.3 us (0.81); the launches traced: 48.7 us -> 40 us
  Pallas kernels: 22.1 us -> 12.6 us
  waiting for transfers between devices: 5.72 us -> 11.7 us
  local copies, waits for them, and re-layouts: 7.5 us -> 4.38 us
  other arithmetic: 1.01 us -> 0.03 us
  starting transfers between devices: 12.1 us -> 11.2 us
    pallas_call x5, Pallas kernels: 22.1 us -> 12.6 us  [the longest x1 6.46 us: on_device(): call(grid_kernel, 'grid', [vmem()] * 9, [(((2, CX // 2, 3 * Z, LO), BF),...]
    ppermute x8, waiting for transfers between devices: 5.72 us -> 11.7 us  [passed_along(): lax.ppermute(x, axis, [(i, (i + by) % length) for i in range(length)])]
    unnamed x31 -> x21, local copies, waits for them, and re-layouts: 6.61 us -> 4.28 us
    ppermute x8, starting transfers between devices: 12.1 us -> 11.2 us  [passed_along(): lax.ppermute(x, axis, [(i, (i + by) % length) for i in range(length)])]
    reshape x1 -> x0, local copies, waits for them, and re-layouts: 0.78 us -> none  [on_device(): return out.reshape(3, 1, 1, stay + 8 * cap)]
    unnamed x1 -> x0, other arithmetic: 0.73 us -> none
  transfers between devices with their start and end apart: 8 -> 8, of which waited for: 4 -> 7; matrix products, arithmetic and copies ran while one was open for 0% -> 1% of each run, Pallas kernels for 8% -> 5%
where the time goes in v2:
time: 40.3 us; the launch traced here: 40 us
  Pallas kernels  12.6 us (31%)
  waiting for transfers between devices  11.7 us (29%)
  starting transfers between devices  11.2 us (28%)
  local copies, waits for them, and re-layouts  4.38 us (11%)
    ppermute x8, waiting for transfers between devices, passed_along(): lax.ppermute(x, axis, [(i, (i + by) % length) for i in range(length)])  11.7 us
    ppermute x8, starting transfers between devices, passed_along(): lax.ppermute(x, axis, [(i, (i + by) % length) for i in range(length)])  11.2 us
    pallas_call x1, Pallas kernels, on_device(): call(grid_kernel, 'grid', [vmem()] * 9, [(((2, CX // 2, 3 * Z, LO), BF),...  6.46 us
    unnamed x21, local copies, waits for them, and re-layouts  4.28 us
    pallas_call x1, Pallas kernels, on_device(): call(pick_kernel, 'pick', [vmem()] * 5, [(((3, 1, stay + 8 * cap), F32),...  2 us
    pallas_call x1, Pallas kernels, on_device(): call(stay_kernel, 'stay', [vmem(), vmem()], [((sums, F32), vmem())], [],...  1.93 us
    pallas_call x1, Pallas kernels, on_device(): call(mean_kernel, 'mean', [vmem()] * 5, [(((CX * CY, lanes), BF), vmem())...  1.51 us
  transfers between devices with their start and end apart: 8, of which 7 were waited for; matrix products, arithmetic and copies ran while one was open for 1% of the time, Pallas kernels for 5%

profile of v2, /device:TPU:0, one launch (start us, length us, event | category | flops | bytes accessed | tf_op | source)
XLA Modules:
  0.0 40.0 jit_solution(2892119972591284929)
XLA Ops:
  0.0 0.7 %copy-done.2 = s32[1,1,8]{2,1,0:T(1,128)S(1)} copy-done((s32[1,1,8]{2,1,0:T(1,128)S(1)}, s32[1,1,8]{2,1,0:T(1,128)}, u32[]{:S(2)}) %copy-start.2) | copy-done | bytes 56
  0.7 0.9 %copy-done = bf16[16,1,1,8,512]{4,3,2,1,0:T(8,128)(2,1)S(1)} copy-done((bf16[16,1,1,8,512]{4,3,2,1,0:T(8,128)(2,1)S(1)}, bf16[16,1,1,8,512]{4,3,2,1,0:T(8,128)(2,1)}, u32[]{:S(2)}) %copy-start) | copy-done | bytes 131096
  1.6 0.7 %copy-done.1 = s32[1,1,8,512]{3,2,1,0:T(8,128)S(1)} copy-done((s32[1,1,8,512]{3,2,1,0:T(8,128)S(1)}, s32[1,1,8,512]{3,2,1,0:T(8,128)}, u32[]{:S(2)}) %copy-start.1) | copy-done | bytes 16408
  2.3 0.7 %pack.1 = (bf16[18,1536]{1,0:T(8,128)(2,1)S(1)}, bf16[18,1536]{1,0:T(8,128)(2,1)S(1)}, bf16[18,1024]{1,0:T(8,128)(2,1)S(1)}) custom-call(bf16[16,8,512]{2,1,0:T(8,128)(2,1)S(1)} %bitcast.15, s32[8,512]{1,0:T(8,128)S(1)} %bitcast.16, s32[8]{0:T(128)S(1)} %bitcast.20), custom_call_target="tpu_custom_call" | custom-call | flops 1048576 | bytes 1048576 | tf_op jit(solution)/shard_map/pack/pallas_call | solution.py:404
  2.9 2.5 %collective-permute-start = (bf16[18,1536]{1,0:T(8,128)(2,1)S(1)}, bf16[18,1536]{1,0:T(8,128)(2,1)S(1)}, u32[]{:S(2)}, u32[]{:S(2)}) collective-permute-start(bf16[18,1536]{1,0:T(8,128)(2,1)S(1)} %get-tuple-element.12), channel_id=1, source_target_pairs={{0,12},{4,0},{8,4},{12,8},{1,13},{5,1},{9,5},{13,9},{2,14},{6,2},{... | collective-permute-start | bytes 165896 | tf_op jit(solution)/shard_map/ppermute | solution.py:48
  5.4 0.0 collective-permute-start.1
  5.4 2.6 %collective-permute-done.west_ref = bf16[18,1536]{1,0:T(8,128)(2,1)S(1)} collective-permute-done((bf16[18,1536]{1,0:T(8,128)(2,1)S(1)}, bf16[18,1536]{1,0:T(8,128)(2,1)S(1)}, u32[]{:S(2)}, u32[]{:S(2)}) %collective-permute-start) | collective-permute-done | bytes 55328 | tf_op jit(solution)/shard_map/ppermute | solution.py:48
  8.0 1.2 %collective-permute-done.1.east_ref = bf16[18,1536]{1,0:T(8,128)(2,1)S(1)} collective-permute-done((bf16[18,1536]{1,0:T(8,128)(2,1)S(1)}, bf16[18,1536]{1,0:T(8,128)(2,1)S(1)}, u32[]{:S(2)}, u32[]{:S(2)}) %collective-permute-start.1) | collective-permute-done | bytes 55328 | tf_op jit(solution)/shard_map/ppermute | solution.py:48
  9.2 1.6 %collective-permute-start.3 = (bf16[18,1536]{1,0:T(8,128)(2,1)S(1)}, bf16[18,1536]{1,0:T(8,128)(2,1)S(1)}, u32[]{:S(2)}, u32[]{:S(2)}) collective-permute-start(bf16[18,1536]{1,0:T(8,128)(2,1)S(1)} %pad_maximum_fusion.1), channel_id=1, source_target_pairs={{0,1},{1,2},{2,3},{3,0},{4,5},{5,6},{6,7},{7,4},{8,9},{9,10},{10,1... | collective-permute-start | bytes 165896 | tf_op jit(solution)/shard_map/ppermute | solution.py:48
  10.8 2.3 %collective-permute-start.2 = (bf16[18,1536]{1,0:T(8,128)(2,1)S(1)}, bf16[18,1536]{1,0:T(8,128)(2,1)S(1)}, u32[]{:S(2)}, u32[]{:S(2)}) collective-permute-start(bf16[18,1536]{1,0:T(8,128)(2,1)S(1)} %pad_maximum_fusion), channel_id=1, source_target_pairs={{0,3},{1,0},{2,1},{3,2},{4,7},{5,4},{6,5},{7,6},{8,11},{9,8},{10,9... | collective-permute-start | bytes 165896 | tf_op jit(solution)/shard_map/ppermute | solution.py:48
  13.1 0.0 copy-done.3
  13.1 1.9 %stay.1.part_ref = f32[544,256]{1,0:T(8,128)S(1)} custom-call(bf16[16,6144]{1,0:T(8,128)(2,1)S(1)} %bitcast.21, s32[1,6144]{1,0:T(1,128)S(1)} %bitcast.23), custom_call_target="tpu_custom_call" | custom-call | flops 5368709120 | bytes 1048576 | tf_op jit(solution)/shard_map/stay/pallas_call | solution.py:430
  15.1 0.9 %collective-permute-done.3.up_ref = bf16[18,1536]{1,0:T(8,128)(2,1)S(1)} collective-permute-done((bf16[18,1536]{1,0:T(8,128)(2,1)S(1)}, bf16[18,1536]{1,0:T(8,128)(2,1)S(1)}, u32[]{:S(2)}, u32[]{:S(2)}) %collective-permute-start.3) | collective-permute-done | bytes 55328 | tf_op jit(solution)/shard_map/ppermute | solution.py:48
  16.0 0.0 collective-permute-done.2.down_ref
  16.0 1.5 %mean.1 = (bf16[1024,128]{1,0:T(8,128)(2,1)S(1)}, bf16[384,128]{1,0:T(8,128)(2,1)S(1)}, bf16[384,128]{1,0:T(8,128)(2,1)S(1)}, bf16[18,4096]{1,0:T(8,128)(2,1)S(1)}) custom-call(bf16[18,1536]{1,0:T(8,128)(2,1)S(1)} %collective-permute-done.west_ref, bf16[18,1536]{1,0:T(8,128)(2,1)S(1)} %collective-permute-done.1.east_ref, ...), custom_call_target="tpu_custom_call" | custom-call | flops 3221225472 | bytes 1048576 | tf_op jit(solution)/shard_map/mean/pallas_call | solution.py:435
  17.6 0.0 copy-start.4
  17.6 0.1 collective-permute-start.4
  17.6 1.7 %collective-permute-start.5 = (bf16[384,128]{1,0:T(8,128)(2,1)S(1)}, bf16[384,128]{1,0:T(8,128)(2,1)S(1)}, u32[]{:S(2)}, u32[]{:S(2)}) collective-permute-start(bf16[384,128]{1,0:T(8,128)(2,1)S(1)} %get-tuple-element.17), channel_id=1, source_target_pairs={{0,12},{4,0},{8,4},{12,8},{1,13},{5,1},{9,5},{13,9},{2,14},{6,2},{... | collective-permute-start | bytes 294920 | tf_op jit(solution)/shard_map/ppermute | solution.py:48
  19.4 2.3 %collective-permute-done.4.before_ref = bf16[384,128]{1,0:T(8,128)(2,1)S(1)} collective-permute-done((bf16[384,128]{1,0:T(8,128)(2,1)S(1)}, bf16[384,128]{1,0:T(8,128)(2,1)S(1)}, u32[]{:S(2)}, u32[]{:S(2)}) %collective-permute-start.4) | collective-permute-done | bytes 98336 | tf_op jit(solution)/shard_map/ppermute | solution.py:48
  21.7 0.4 collective-permute-done.5.after_ref
  22.0 3.0 %collective-permute-start.7 = (bf16[112,128]{1,0:T(8,128)(2,1)S(1)}, bf16[112,128]{1,0:T(8,128)(2,1)S(1)}, u32[]{:S(2)}, u32[]{:S(2)}) collective-permute-start(bf16[112,128]{1,0:T(8,128)(2,1)S(1)} %maximum_bitcast_fusion.1), channel_id=1, source_target_pairs={{0,3},{1,0},{2,1},{3,2},{4,7},{5,4},{6,5},{7,6},{8,11},{9,8},{10,9... | collective-permute-start | bytes 86024 | tf_op jit(solution)/shard_map/ppermute | solution.py:48
  25.0 0.1 collective-permute-start.6
  25.1 0.6 %copy-done.9 = f32[3,32]{1,0:T(4,128)S(1)} copy-done((f32[3,32]{1,0:T(4,128)S(1)}, f32[3,32]{1,0:T(4,128)}, u32[]{:S(2)}) %copy-start.9) | copy-done | bytes 408
  25.7 0.1 tile.10.bias_ref
  25.8 0.6 %copy-done.8 = bf16[32,16]{0,1:T(8,128)(2,1)S(1)} copy-done((bf16[32,16]{0,1:T(8,128)(2,1)S(1)}, bf16[32,16]{0,1:T(8,128)(2,1)}, u32[]{:S(2)}) %copy-start.8) | copy-done | bytes 1048
  26.4 0.1 copy.11.encoder_ref
  26.5 0.1 collective-permute-done.7.above_ref
  26.6 4.3 %collective-permute-done.6.below_ref = bf16[112,128]{1,0:T(8,128)(2,1)S(1)} collective-permute-done((bf16[112,128]{1,0:T(8,128)(2,1)S(1)}, bf16[112,128]{1,0:T(8,128)(2,1)S(1)}, u32[]{:S(2)}, u32[]{:S(2)}) %collective-permute-start.6) | collective-permute-done | bytes 28704 | tf_op jit(solution)/shard_map/ppermute | solution.py:48
  30.8 6.5 %grid.1.grid_ref = bf16[2,4,24,256]{3,2,1,0:T(8,128)(2,1)S(1)} custom-call(bf16[1024,128]{1,0:T(8,128)(2,1)S(1)} %get-tuple-element.15.mean_ref, bf16[384,128]{1,0:T(8,128)(2,1)S(1)} %collective-permute-done.4.before_ref, bf16[384,128]{1,0:T(8,128)(2,1)S(1)} %collective-permute-done.5.after_ref, bf16[112,128]{1,0:T(8,128)(2,1)S(1)} %collective-permute-done.6.below_ref, ...), custom_call_target="tpu_custom_call" | custom-call | flops 8589934592 | bytes 1048576 | tf_op jit(solution)/shard_map/grid/pallas_call | solution.py:462
  37.3 0.0 copy-start.7
  37.3 0.7 %copy-done.7 = bf16[3,16]{1,0:T(4,128)(2,1)S(1)} copy-done((bf16[3,16]{1,0:T(4,128)(2,1)S(1)}, bf16[3,16]{1,0:T(4,128)(2,1)}, u32[]{:S(2)}) %copy-start.7) | copy-done | bytes 120
  38.0 2.0 %pick.1 = f32[3,1,10240]{2,1,0:T(1,128)} custom-call(bf16[2,4,24,256]{3,2,1,0:T(8,128)(2,1)S(1)} %grid.1.grid_ref, bf16[16,6144]{1,0:T(8,128)(2,1)S(1)} %bitcast.22, s32[1,6144]{1,0:T(1,128)S(1)} %bitcast.24, bf16[18,4096]{1,0:T(8,128)(2,1)S(1)} %get-tuple-element.18.held_ref, bf16[3,16]{1,0:T(4,128)(2,1)S(1)} %copy-done.7), custom_call_target="tpu_custom_call" | custom-call | flops 5368709120 | bytes 1048576 | tf_op jit(solution)/shard_map/pick/pallas_call | solution.py:479
  (22 shorter events, 0.1 us)
Async XLA Ops:
  0.0 0.7 %copy-start.2 = (s32[1,1,8]{2,1,0:T(1,128)S(1)}, s32[1,1,8]{2,1,0:T(1,128)}, u32[]{:S(2)}) copy-start(s32[1,1,8]{2,1,0:T(1,128)} %param.14) | copy-start | bytes 100
  0.7 0.9 %copy-start = (bf16[16,1,1,8,512]{4,3,2,1,0:T(8,128)(2,1)S(1)}, bf16[16,1,1,8,512]{4,3,2,1,0:T(8,128)(2,1)}, u32[]{:S(2)}) copy-start(bf16[16,1,1,8,512]{4,3,2,1,0:T(8,128)(2,1)} %param.12) | copy-start | bytes 393220
  1.6 0.7 %copy-start.1 = (s32[1,1,8,512]{3,2,1,0:T(8,128)S(1)}, s32[1,1,8,512]{3,2,1,0:T(8,128)}, u32[]{:S(2)}) copy-start(s32[1,1,8,512]{3,2,1,0:T(8,128)} %param.13) | copy-start | bytes 49156
  2.9 5.1 %collective-permute-start = (bf16[18,1536]{1,0:T(8,128)(2,1)S(1)}, bf16[18,1536]{1,0:T(8,128)(2,1)S(1)}, u32[]{:S(2)}, u32[]{:S(2)}) collective-permute-start(bf16[18,1536]{1,0:T(8,128)(2,1)S(1)} %get-tuple-element.12), channel_id=1, source_target_pairs={{0,12},{4,0},{8,4},{12,8},{1,13},{5,1},{9,5},{13,9},{2,14},{6,2},{... | collective-permute-start | bytes 165896 | tf_op jit(solution)/shard_map/ppermute | solution.py:48
  5.4 3.8 %collective-permute-start.1 = (bf16[18,1536]{1,0:T(8,128)(2,1)S(1)}, bf16[18,1536]{1,0:T(8,128)(2,1)S(1)}, u32[]{:S(2)}, u32[]{:S(2)}) collective-permute-start(bf16[18,1536]{1,0:T(8,128)(2,1)S(1)} %get-tuple-element.13), channel_id=1, source_target_pairs={{0,4},{4,8},{8,12},{12,0},{1,5},{5,9},{9,13},{13,1},{2,6},{6,10},{... | collective-permute-start | bytes 165896 | tf_op jit(solution)/shard_map/ppermute | solution.py:48
  8.0 5.1 %copy-start.3 = (bf16[16,1,1,6144]{3,0,2,1:T(8,128)(2,1)S(1)}, bf16[16,1,1,6144]{3,0,2,1:T(8,128)(2,1)}, u32[]{:S(2)}) copy-start(bf16[16,1,1,6144]{3,0,2,1:T(8,128)(2,1)} %param.10) | copy-start | bytes 589828
  9.2 6.8 %collective-permute-start.3 = (bf16[18,1536]{1,0:T(8,128)(2,1)S(1)}, bf16[18,1536]{1,0:T(8,128)(2,1)S(1)}, u32[]{:S(2)}, u32[]{:S(2)}) collective-permute-start(bf16[18,1536]{1,0:T(8,128)(2,1)S(1)} %pad_maximum_fusion.1), channel_id=1, source_target_pairs={{0,1},{1,2},{2,3},{3,0},{4,5},{5,6},{6,7},{7,4},{8,9},{9,10},{10,1... | collective-permute-start | bytes 165896 | tf_op jit(solution)/shard_map/ppermute | solution.py:48
  10.8 2.3 %copy-start.5 = (s32[1,1,6144]{2,1,0:T(1,128)S(1)}, s32[1,1,6144]{2,1,0:T(1,128)}, u32[]{:S(2)}) copy-start(s32[1,1,6144]{2,1,0:T(1,128)} %param.11) | copy-start | bytes 73732
  10.8 5.2 %collective-permute-start.2 = (bf16[18,1536]{1,0:T(8,128)(2,1)S(1)}, bf16[18,1536]{1,0:T(8,128)(2,1)S(1)}, u32[]{:S(2)}, u32[]{:S(2)}) collective-permute-start(bf16[18,1536]{1,0:T(8,128)(2,1)S(1)} %pad_maximum_fusion), channel_id=1, source_target_pairs={{0,3},{1,0},{2,1},{3,2},{4,7},{5,4},{6,5},{7,6},{8,11},{9,8},{10,9... | collective-permute-start | bytes 165896 | tf_op jit(solution)/shard_map/ppermute | solution.py:48
  17.6 13.3 %copy-start.4 = (bf16[3,32,864]{2,1,0:T(8,128)(2,1)S(1)}, bf16[3,32,864]{2,1,0:T(8,128)(2,1)}, u32[]{:S(2)}) copy-start(bf16[3,32,864]{2,1,0:T(8,128)(2,1)} %weight_ref.1) | copy-start | bytes 497668
  17.6 4.1 %collective-permute-start.4 = (bf16[384,128]{1,0:T(8,128)(2,1)S(1)}, bf16[384,128]{1,0:T(8,128)(2,1)S(1)}, u32[]{:S(2)}, u32[]{:S(2)}) collective-permute-start(bf16[384,128]{1,0:T(8,128)(2,1)S(1)} %get-tuple-element.16), channel_id=1, source_target_pairs={{0,4},{4,8},{8,12},{12,0},{1,5},{5,9},{9,13},{13,1},{2,6},{6,10},{... | collective-permute-start | bytes 294920 | tf_op jit(solution)/shard_map/ppermute | solution.py:48
  17.6 4.4 %collective-permute-start.5 = (bf16[384,128]{1,0:T(8,128)(2,1)S(1)}, bf16[384,128]{1,0:T(8,128)(2,1)S(1)}, u32[]{:S(2)}, u32[]{:S(2)}) collective-permute-start(bf16[384,128]{1,0:T(8,128)(2,1)S(1)} %get-tuple-element.17), channel_id=1, source_target_pairs={{0,12},{4,0},{8,4},{12,8},{1,13},{5,1},{9,5},{13,9},{2,14},{6,2},{... | collective-permute-start | bytes 294920 | tf_op jit(solution)/shard_map/ppermute | solution.py:48
  22.0 4.5 %collective-permute-start.7 = (bf16[112,128]{1,0:T(8,128)(2,1)S(1)}, bf16[112,128]{1,0:T(8,128)(2,1)S(1)}, u32[]{:S(2)}, u32[]{:S(2)}) collective-permute-start(bf16[112,128]{1,0:T(8,128)(2,1)S(1)} %maximum_bitcast_fusion.1), channel_id=1, source_target_pairs={{0,3},{1,0},{2,1},{3,2},{4,7},{5,4},{6,5},{7,6},{8,11},{9,8},{10,9... | collective-permute-start | bytes 86024 | tf_op jit(solution)/shard_map/ppermute | solution.py:48
  25.0 0.7 %copy-start.9 = (f32[3,32]{1,0:T(4,128)S(1)}, f32[3,32]{1,0:T(4,128)}, u32[]{:S(2)}) copy-start(f32[3,32]{1,0:T(4,128)} %param.17) | copy-start | bytes 1156
  25.0 5.8 %collective-permute-start.6 = (bf16[112,128]{1,0:T(8,128)(2,1)S(1)}, bf16[112,128]{1,0:T(8,128)(2,1)S(1)}, u32[]{:S(2)}, u32[]{:S(2)}) collective-permute-start(bf16[112,128]{1,0:T(8,128)(2,1)S(1)} %maximum_bitcast_fusion), channel_id=1, source_target_pairs={{0,1},{1,2},{2,3},{3,0},{4,5},{5,6},{6,7},{7,4},{8,9},{9,10},{10,1... | collective-permute-start | bytes 86024 | tf_op jit(solution)/shard_map/ppermute | solution.py:48
  25.7 0.7 %copy-start.8 = (bf16[32,16]{0,1:T(8,128)(2,1)S(1)}, bf16[32,16]{0,1:T(8,128)(2,1)}, u32[]{:S(2)}) copy-start(bf16[32,16]{0,1:T(8,128)(2,1)} %param.15) | copy-start | bytes 3076
  26.4 4.5 %copy-start.6 = (bf16[3,32]{1,0:T(4,128)(2,1)S(1)}, bf16[3,32]{1,0:T(4,128)(2,1)}, u32[]{:S(2)}) copy-start(bf16[3,32]{1,0:T(4,128)(2,1)} %decoder_ref.1) | copy-start | bytes 580
  37.3 0.7 %copy-start.7 = (bf16[3,16]{1,0:T(4,128)(2,1)S(1)}, bf16[3,16]{1,0:T(4,128)(2,1)}, u32[]{:S(2)}) copy-start(bf16[3,16]{1,0:T(4,128)(2,1)} %self_ref.1) | copy-start | bytes 292

commit v3 on v2

--- a/solution.py
+++ b/solution.py
@@ -16,7 +16,8 @@
 DEAD = 2 * HI
 HALO = 3
 SIDE = 8
-PITCH = CY + 2 * SIDE
+KEPT = SIDE // 2
+STRIP = 4 * SIDE
 BF = jnp.bfloat16
 F32 = jnp.float32
 NT = (((1,), (1,)), ((), ()))
@@ -56,8 +57,8 @@
     return pl.BlockSpec(memory_space=pltpu.VMEM)
 
 
-def smem():
-    return pl.BlockSpec(memory_space=pltpu.SMEM)
+def hbm():
+    return pl.BlockSpec(memory_space=pl.ANY)
 
 
 def call(kernel, name, ins, outs, scratch, flops, mib):
@@ -87,7 +88,15 @@
     return dot(jnp.concatenate(parts, 0), onehot(low, LO), NT)
 
 
-def pack_kernel(feat_ref, slot_ref, count_ref, west_ref, east_ref, middle_ref):
+def pack_kernel(
+    feat_in, slot_in, count_in, west_ref, east_ref, middle_ref, feat_ref, slot_ref, count_ref, sems
+):
+    pairs = ((count_in, count_ref), (slot_in, slot_ref), (feat_in, feat_ref))
+    copies = [pltpu.make_async_copy(a, b, sems.at[k]) for k, (a, b) in enumerate(pairs)]
+    for copy in copies:
+        copy.start()
+    for copy in copies:
+        copy.wait()
     feat_dim, buckets, cap = feat_ref.shape
     turned = jnp.swapaxes(feat_ref[...].astype(F32), 0, 1)
     high, low = cell_codes(slot_ref[...])
@@ -223,99 +232,75 @@
     return 0.5 * v * (1.0 + jnp.tanh(inner))
 
 
-def grid_kernel(
+def store_shifted(target, start, block):
+    rows = block.shape[0]
+    for s, by in enumerate((1, 0, rows - 1)):
+        moved = pltpu.roll(block, by, 0) if by else block
+        target[s, start : start + rows, :] = moved.astype(BF)
+
+
+def conv(source, band_ref, bias_ref, layer, x, count, pitch):
+    pieces = [
+        source[s, (x + q) * pitch : (x + q + count) * pitch, :] for q in range(3) for s in range(3)
+    ]
+    return dot(jnp.concatenate(pieces, 1), band_ref[layer], NT) + bias_ref[layer : layer + 1, :]
+
+
+def hidden(source, band_ref, bias_ref, layer, target, outs, count, pitch):
+    for x in range(0, outs, count):
+        value = gelu(conv(source, band_ref, bias_ref, layer, x, count, pitch))
+        store_shifted(target, x * pitch, value.astype(BF).astype(F32))
+
+
+def build_decode(decoder):
+    chans = decoder.shape[1]
+    tiled = tiled_rows(decoder, Z)
+    group = lax.broadcasted_iota(jnp.int32, (Z, Z * chans), 1) // chans
+    level = lax.broadcasted_iota(jnp.int32, (Z, Z * chans), 0)
+    return jnp.concatenate(
+        [jnp.where(group == level, tiled[k : k + 1, :], 0.0) for k in range(3)], 0
+    ).astype(BF)
+
+
+def inner_kernel(
     mean_ref,
     before_ref,
     after_ref,
-    below_ref,
-    above_ref,
     weight_ref,
     encoder_ref,
     bias_ref,
     decoder_ref,
-    grid_ref,
-    left,
-    right,
+    flow_ref,
+    band_ref,
     input_one,
     input_two,
     input_three,
     own,
-    band_ref,
 ):
     spread = build_spread(encoder_ref[...])
-    left[...] = dot(below_ref[...], spread, NT).astype(BF).astype(F32)
-    right[...] = dot(above_ref[...], spread, NT).astype(BF).astype(F32)
-
-    def store_shifted(target, x, block, lead, length):
-        rows = aligned(x * length, length)
-        for s, by in enumerate((1, 0, block.shape[0] - 1)):
-            moved = pltpu.roll(block, by, 0) if by else block
-            target[s, rows, :] = moved[lead : lead + length].astype(BF)
-
-    def encode(ref, count, base, keep):
-        def body(x):
-            rows = aligned(x * CY, CY)
-            inside = dot(ref[rows, :], spread, NT).astype(BF)
-            if keep:
-                own[rows, :] = inside
-            at = x + base
-            side = aligned(at * SIDE, SIDE)
-            block = jnp.concatenate([left[side, :], inside.astype(F32), right[side, :]], 0)
-            store_shifted(input_one, at, block, 0, PITCH)
-
-        repeat(count, body)
-
-    encode(before_ref, HALO, 0, False)
-    encode(mean_ref, CX, HALO, True)
-    encode(after_ref, HALO, HALO + CX, False)
-
-    def conv(source, layer, x, count, length):
-        pieces = []
-        for q in range(3):
-            rows = aligned((x + q) * length, count * length)
-            for s in range(3):
-                pieces.append(source[s, rows, :])
-        return dot(jnp.concatenate(pieces, 1), band_ref[layer], NT) + bias_ref[layer : layer + 1, :]
-
-    def hidden(source, layer, target, outs, count, lead, length):
-        def body(step):
-            x = step * count
-            value = gelu(conv(source, layer, x, count, PITCH)).astype(BF).astype(F32)
-            for k in range(count):
-                store_shifted(
-                    target, x + k, value[k * PITCH : (k + 1) * PITCH], lead, length
-                )
-
-        repeat(outs // count, body)
-
+
+    def encode(ref, base, keep):
+        inside = dot(ref[...], spread, NT).astype(BF)
+        if keep:
+            own[...] = inside
+        store_shifted(input_one, base * CY, inside.astype(F32))
+
+    encode(before_ref, 0, False)
+    encode(mean_ref, HALO, True)
+    encode(after_ref, HALO + CX, False)
     build_band(weight_ref, 0, band_ref)
-    hidden(input_one, 0, input_two, CX + 4, COUNTS[0], 0, PITCH)
+    hidden(input_one, band_ref, bias_ref, 0, input_two, CX + 4, COUNTS[0], CY)
     build_band(weight_ref, 1, band_ref)
-    hidden(input_two, 1, input_three, CX + 2, COUNTS[1], SIDE, CY)
-
-    chans = decoder_ref.shape[1]
-    wide = Z * chans
-    tiled = tiled_rows(decoder_ref[...], Z)
-    group = lax.broadcasted_iota(jnp.int32, (Z, wide), 1) // chans
-    level = lax.broadcasted_iota(jnp.int32, (Z, wide), 0)
-    decode = jnp.concatenate(
-        [jnp.where(group == level, tiled[k : k + 1, :], 0.0) for k in range(3)], 0
-    ).astype(BF)
-
-    def last(step):
-        count = COUNTS[2]
-        rows = aligned(step * count * CY, count * CY)
-        value = conv(input_three, 2, step * count, count, CY) + own[rows, :].astype(F32)
+    hidden(input_two, band_ref, bias_ref, 1, input_three, CX + 2, COUNTS[1], CY)
+    build_band(weight_ref, 2, band_ref)
+    decode = build_decode(decoder_ref[...])
+    count = COUNTS[2]
+    for x in range(0, CX, count):
+        rows = slice(x * CY, (x + count) * CY)
+        value = conv(input_three, band_ref, bias_ref, 2, x, count, CY) + own[rows, :].astype(F32)
         flow = dot(decode, value.astype(BF), NT)
-        top = flow.astype(BF)
-        low = (flow - top.astype(F32)).astype(BF)
         for pair in range(count // 2):
-            lanes = slice(pair * LO, (pair + 1) * LO)
-            grid_ref[0, step * (count // 2) + pair] = top[:, lanes]
-            grid_ref[1, step * (count // 2) + pair] = low[:, lanes]
-
-    build_band(weight_ref, 2, band_ref)
-    repeat(CX // COUNTS[2], last)
+            flow_ref[x // 2 + pair] = flow[:, pair * LO : (pair + 1) * LO]
 
 
 def pick_rows(table, feats, high, low, self_weight):
@@ -341,8 +326,61 @@
     return rows
 
 
-def pick_kernel(grid_ref, feat_ref, slot_ref, held_ref, self_ref, out_ref, table):
-    table[...] = grid_ref[...].reshape(table.shape)
+def pick_kernel(
+    flow_ref,
+    below_ref,
+    low_ref,
+    high_ref,
+    above_ref,
+    band_ref,
+    encoder_ref,
+    bias_ref,
+    decoder_ref,
+    feat_ref,
+    slot_ref,
+    held_ref,
+    self_ref,
+    out_ref,
+    input_one,
+    input_two,
+    input_three,
+    table,
+):
+    spread = build_spread(encoder_ref[...])
+    sides = [
+        dot(ref[...], spread, NT).astype(BF).astype(F32)
+        for ref in (below_ref, low_ref, high_ref, above_ref)
+    ]
+    rows = CX + 2 * HALO
+    strips = jnp.concatenate(
+        [side[x * SIDE : (x + 1) * SIDE] for x in range(rows) for side in sides], 0
+    )
+    store_shifted(input_one, 0, strips)
+    hidden(input_one, band_ref, bias_ref, 0, input_two, rows - 2, rows - 2, STRIP)
+    hidden(input_two, band_ref, bias_ref, 1, input_three, rows - 4, rows - 4, STRIP)
+    value = conv(input_three, band_ref, bias_ref, 2, 0, CX, STRIP)
+    value = value + strips[HALO * STRIP : (HALO + CX) * STRIP]
+    ends = dot(build_decode(decoder_ref[...]), value.astype(BF), NT)
+    lane = lax.broadcasted_iota(jnp.int32, (ends.shape[0], CY), 1)
+    for pair in range(CX // 2):
+        halves = []
+        for x in (2 * pair, 2 * pair + 1):
+            place = x * STRIP
+            source = ends[:, place // 128 * 128 : (place // 128 + 1) * 128]
+            inside = place % 128
+            start = pltpu.roll(source, (128 - inside - SIDE) % 128, 1)
+            end = pltpu.roll(source, (CY - 3 * SIDE - inside) % 128, 1)
+            middle = flow_ref[pair, :, (x % 2) * CY : (x % 2 + 1) * CY]
+            halves.append(
+                jnp.where(lane < KEPT, start, jnp.where(lane >= CY - KEPT, end, middle))
+            )
+        flow = jnp.concatenate(halves, 1)
+        top = flow.astype(BF)
+        size = flow.shape[0]
+        table[pair * size : (pair + 1) * size, :] = top
+        table[(CX // 2 + pair) * size : (CX // 2 + pair + 1) * size, :] = (
+            flow - top.astype(F32)
+        ).astype(BF)
     chunk = CHUNK
     feat_dim, stay = feat_ref.shape
     eye = jnp.where(
@@ -404,15 +442,20 @@
     west, east, middle = call(
         pack_kernel,
         "pack",
-        [vmem(), vmem(), smem()],
+        [hbm()] * 3,
         [
             (((width, 3 * cap), BF), vmem()),
             (((width, 3 * cap), BF), vmem()),
             (((width, 2 * cap), BF), vmem()),
         ],
-        [],
+        [
+            pltpu.VMEM((feat_dim, 8, cap), BF),
+            pltpu.VMEM((8, cap), jnp.int32),
+            pltpu.SMEM((8,), jnp.int32),
+            pltpu.SemaphoreType.DMA((3,)),
+        ],
         1 << 20,
-        4,
+        61,
     )(
         move_feats.reshape(feat_dim, 8, cap),
         move_slots.reshape(8, cap),
@@ -455,36 +498,56 @@
         ]
         return jnp.concatenate(blocks, 0).reshape((CX + 2 * HALO) * SIDE, lanes)
 
-    above = passed_along(edge(0), "gy", -1)
-    below = passed_along(edge(CY - SIDE), "gy", 1)
+    low, high = edge(0), edge(CY - SIDE)
+    above = passed_along(low, "gy", -1)
+    below = passed_along(high, "gy", 1)
     biases = jnp.tile(conv_biases, (1, Z))
     rows = CX + 2 * HALO
-    (grid,) = call(
-        grid_kernel,
-        "grid",
-        [vmem()] * 9,
-        [(((2, CX // 2, 3 * Z, LO), BF), vmem())],
+    flow, band = call(
+        inner_kernel,
+        "inner",
+        [vmem()] * 7,
         [
-            pltpu.VMEM((rows * SIDE, wide), F32),
-            pltpu.VMEM((rows * SIDE, wide), F32),
-            pltpu.VMEM((3, rows * PITCH, wide), BF),
-            pltpu.VMEM((3, (rows - 2) * PITCH, wide), BF),
+            (((CX // 2, 3 * Z, LO), F32), vmem()),
+            (((3, wide, 9 * wide), BF), vmem()),
+        ],
+        [
+            pltpu.VMEM((3, rows * CY, wide), BF),
+            pltpu.VMEM((3, (rows - 2) * CY, wide), BF),
             pltpu.VMEM((3, (rows - 4) * CY, wide), BF),
             pltpu.VMEM((CX * CY, wide), BF),
-            pltpu.VMEM((3, wide, 9 * wide), BF),
         ],
         8 << 30,
-        32,
-    )(mean, before, after, below, above, conv_weights, encoder, biases, decoder)
+        24,
+    )(mean, before, after, conv_weights, encoder, biases, decoder)
     (out,) = call(
         pick_kernel,
         "pick",
-        [vmem()] * 5,
+        [vmem()] * 13,
         [(((3, 1, stay + 8 * cap), F32), vmem())],
-        [pltpu.VMEM((CX * 3 * Z, LO), BF)],
+        [
+            pltpu.VMEM((3, rows * STRIP, wide), BF),
+            pltpu.VMEM((3, (rows - 2) * STRIP, wide), BF),
+            pltpu.VMEM((3, (rows - 4) * STRIP, wide), BF),
+            pltpu.VMEM((2 * CX // 2 * 3 * Z, LO), BF),
+        ],
         5 << 30,
-        8,
-    )(grid, own_feats, own_slots, held, self_weight)
+        16,
+    )(
+        flow,
+        below,
+        low,
+        high,
+        above,
+        band,
+        encoder,
+        biases,
+        decoder,
+        own_feats,
+        own_slots,
+        held,
+        self_weight,
+    )
     return out.reshape(3, 1, 1, stay + 8 * cap)
 
 

time: 40.3 us -> 41.1 us (1.020); the launches traced: 40 us -> 40.3 us
  Pallas kernels: 12.6 us -> 17.7 us
  waiting for transfers between devices: 11.7 us -> 7.85 us
  local copies, waits for them, and re-layouts: 4.38 us -> 2.65 us
  starting transfers between devices: 11.2 us -> 11.9 us
    pallas_call x3, Pallas kernels: 9.11 us -> 14.3 us  [the longest x1 7.32 us: on_device(): call(inner_kernel, 'inner', [vmem()] * 7, [(((CX // 2, 3 * Z, LO), F32),...]
    ppermute x8, waiting for transfers between devices: 11.7 us -> 7.85 us  [passed_along(): lax.ppermute(x, axis, [(i, (i + by) % length) for i in range(length)])]
    unnamed x21 -> x19, local copies, waits for them, and re-layouts: 4.28 us -> 1.78 us
    slice x1, local copies, waits for them, and re-layouts: 0.01 us -> 0.76 us  [on_device(): middle[:, cap:]]
    ppermute x8, starting transfers between devices: 11.2 us -> 11.9 us  [passed_along(): lax.ppermute(x, axis, [(i, (i + by) % length) for i in range(length)])]
  transfers between devices with their start and end apart: 8 -> 8, of which waited for: 7 -> 4; matrix products, arithmetic and copies ran while one was open for 1% -> 2% of each run, Pallas kernels for 5% -> 23%
where the time goes in v3:
time: 41.1 us; the launch traced here: 40.3 us
  Pallas kernels  17.7 us (43%)
  starting transfers between devices  11.9 us (29%)
  waiting for transfers between devices  7.85 us (19%)
  local copies, waits for them, and re-layouts  2.65 us (6%)
    ppermute x8, starting transfers between devices, passed_along(): lax.ppermute(x, axis, [(i, (i + by) % length) for i in range(length)])  11.9 us
    ppermute x8, waiting for transfers between devices, passed_along(): lax.ppermute(x, axis, [(i, (i + by) % length) for i in range(length)])  7.85 us
    pallas_call x1, Pallas kernels, on_device(): call(inner_kernel, 'inner', [vmem()] * 7, [(((CX // 2, 3 * Z, LO), F32),...  7.32 us
    pallas_call x1, Pallas kernels, on_device(): call(pick_kernel, 'pick', [vmem()] * 13, [(((3, 1, stay + 8 * cap), F32),...  5.3 us
    pallas_call x1, Pallas kernels, on_device(): call(stay_kernel, 'stay', [vmem(), vmem()], [((sums, F32), vmem())], [],...  1.94 us
    unnamed x19, local copies, waits for them, and re-layouts  1.78 us
    pallas_call x1, Pallas kernels, on_device(): call(pack_kernel, 'pack', [hbm()] * 3, [(((width, 3 * cap), BF), vmem()),...  1.68 us
    pallas_call x1, Pallas kernels, on_device(): call(mean_kernel, 'mean', [vmem()] * 5, [(((CX * CY, lanes), BF), vmem())...  1.51 us
  transfers between devices with their start and end apart: 8, of which 4 were waited for; matrix products, arithmetic and copies ran while one was open for 2% of the time, Pallas kernels for 23%

profile of v3, /device:TPU:0, one launch (start us, length us, event | category | flops | bytes accessed | tf_op | source)
XLA Modules:
  0.0 40.3 jit_solution(7325203377220914159)
XLA Ops:
  0.0 1.7 %pack.1 = (bf16[18,1536]{1,0:T(8,128)(2,1)}, bf16[18,1536]{1,0:T(8,128)(2,1)}, bf16[18,1024]{1,0:T(8,128)(2,1)}) custom-call(bf16[16,8,512]{2,1,0:T(8,128)(2,1)} %bitcast.22, s32[8,512]{1,0:T(8,128)} %bitcast.23, s32[8]{0:T(128)} %bitcast.24), custom_call_target="tpu_custom_call" | custom-call | flops 1048576 | bytes 1048576 | tf_op jit(solution)/shard_map/pack/pallas_call | solution.py:442
  1.7 2.5 %collective-permute-start = (bf16[18,1536]{1,0:T(8,128)(2,1)}, bf16[18,1536]{1,0:T(8,128)(2,1)S(1)}, u32[]{:S(2)}, u32[]{:S(2)}) collective-permute-start(bf16[18,1536]{1,0:T(8,128)(2,1)} %get-tuple-element.14), channel_id=1, source_target_pairs={{0,12},{4,0},{8,4},{12,8},{1,13},{5,1},{9,5},{13,9},{2,14},{6,2},{... | collective-permute-start | bytes 165896 | tf_op jit(solution)/shard_map/ppermute | solution.py:49
  4.1 0.0 collective-permute-start.1
  4.2 0.8 %fusion.5 = (bf16[18,512]{1,0:T(8,128)(2,1)S(1)}, bf16[18,512]{1,0:T(8,128)(2,1)S(1)}) fusion(bf16[18,1024]{1,0:T(8,128)(2,1)} %get-tuple-element.16), kind=kLoop, calls=%fused_computation.9 | loop fusion | bytes 73728 | tf_op jit(solution)/shard_map/slice | solution.py:470
  4.9 3.2 %collective-permute-done.1.east_ref = bf16[18,1536]{1,0:T(8,128)(2,1)S(1)} collective-permute-done((bf16[18,1536]{1,0:T(8,128)(2,1)}, bf16[18,1536]{1,0:T(8,128)(2,1)S(1)}, u32[]{:S(2)}, u32[]{:S(2)}) %collective-permute-start.1) | collective-permute-done | bytes 55328 | tf_op jit(solution)/shard_map/ppermute | solution.py:49
  8.1 0.0 collective-permute-done.west_ref
  8.2 3.7 %collective-permute-start.2 = (bf16[18,1536]{1,0:T(8,128)(2,1)S(1)}, bf16[18,1536]{1,0:T(8,128)(2,1)S(1)}, u32[]{:S(2)}, u32[]{:S(2)}) collective-permute-start(bf16[18,1536]{1,0:T(8,128)(2,1)S(1)} %pad_maximum_fusion), channel_id=1, source_target_pairs={{0,3},{1,0},{2,1},{3,2},{4,7},{5,4},{6,5},{7,6},{8,11},{9,8},{10,9... | collective-permute-start | bytes 165896 | tf_op jit(solution)/shard_map/ppermute | solution.py:49
  11.8 0.1 collective-permute-start.3
  11.9 0.0 copy-start
  11.9 0.9 %copy-done = bf16[16,1,1,6144]{3,0,2,1:T(8,128)(2,1)S(1)} copy-done((bf16[16,1,1,6144]{3,0,2,1:T(8,128)(2,1)S(1)}, bf16[16,1,1,6144]{3,0,2,1:T(8,128)(2,1)}, u32[]{:S(2)}) %copy-start) | copy-done | bytes 196632
  12.8 0.7 %copy-done.3 = s32[1,1,6144]{2,1,0:T(1,128)S(1)} copy-done((s32[1,1,6144]{2,1,0:T(1,128)S(1)}, s32[1,1,6144]{2,1,0:T(1,128)}, u32[]{:S(2)}) %copy-start.3) | copy-done | bytes 24600
  13.6 1.9 %stay.1.part_ref = f32[544,256]{1,0:T(8,128)S(1)} custom-call(bf16[16,6144]{1,0:T(8,128)(2,1)S(1)} %bitcast.18, s32[1,6144]{1,0:T(1,128)S(1)} %bitcast.20), custom_call_target="tpu_custom_call" | custom-call | flops 5368709120 | bytes 1048576 | tf_op jit(solution)/shard_map/stay/pallas_call | solution.py:473
  15.5 0.0 copy-done.7
  15.5 0.1 copy.11.encoder_ref
  15.6 0.1 tile.10.bias_ref
  15.7 0.0 collective-permute-done.2.down_ref
  15.7 2.3 %collective-permute-done.3.up_ref = bf16[18,1536]{1,0:T(8,128)(2,1)S(1)} collective-permute-done((bf16[18,1536]{1,0:T(8,128)(2,1)S(1)}, bf16[18,1536]{1,0:T(8,128)(2,1)S(1)}, u32[]{:S(2)}, u32[]{:S(2)}) %collective-permute-start.3) | collective-permute-done | bytes 55328 | tf_op jit(solution)/shard_map/ppermute | solution.py:49
  18.0 1.5 %mean.1 = (bf16[1024,128]{1,0:T(8,128)(2,1)S(1)}, bf16[384,128]{1,0:T(8,128)(2,1)S(1)}, bf16[384,128]{1,0:T(8,128)(2,1)S(1)}, bf16[18,4096]{1,0:T(8,128)(2,1)S(1)}) custom-call(bf16[18,1536]{1,0:T(8,128)(2,1)S(1)} %collective-permute-done.west_ref, bf16[18,1536]{1,0:T(8,128)(2,1)S(1)} %collective-permute-done.1.east_ref, ...), custom_call_target="tpu_custom_call" | custom-call | flops 3221225472 | bytes 1048576 | tf_op jit(solution)/shard_map/mean/pallas_call | solution.py:478
  19.6 0.1 collective-permute-start.4
  19.6 1.7 %collective-permute-start.5 = (bf16[384,128]{1,0:T(8,128)(2,1)S(1)}, bf16[384,128]{1,0:T(8,128)(2,1)S(1)}, u32[]{:S(2)}, u32[]{:S(2)}) collective-permute-start(bf16[384,128]{1,0:T(8,128)(2,1)S(1)} %get-tuple-element.19), channel_id=1, source_target_pairs={{0,12},{4,0},{8,4},{12,8},{1,13},{5,1},{9,5},{13,9},{2,14},{6,2},{... | collective-permute-start | bytes 294920 | tf_op jit(solution)/shard_map/ppermute | solution.py:49
  21.4 2.2 %collective-permute-done.5.after_ref = bf16[384,128]{1,0:T(8,128)(2,1)S(1)} collective-permute-done((bf16[384,128]{1,0:T(8,128)(2,1)S(1)}, bf16[384,128]{1,0:T(8,128)(2,1)S(1)}, u32[]{:S(2)}, u32[]{:S(2)}) %collective-permute-start.5) | collective-permute-done | bytes 98336 | tf_op jit(solution)/shard_map/ppermute | solution.py:49
  23.6 0.1 collective-permute-done.4.before_ref
  23.7 0.1 collective-permute-start.6
  23.8 0.0 copy-start.1
  23.8 0.0 copy-start.4
  23.8 0.0 copy-start.6
  23.8 3.8 %collective-permute-start.7 = (bf16[112,128]{1,0:T(8,128)(2,1)S(1)}, bf16[112,128]{1,0:T(8,128)(2,1)S(1)}, u32[]{:S(2)}, u32[]{:S(2)}) collective-permute-start(bf16[112,128]{1,0:T(8,128)(2,1)S(1)} %maximum_bitcast_fusion.1.low_ref), channel_id=1, source_target_pairs={{0,3},{1,0},{2,1},{3,2},{4,7},{5,4},{6,5},{7,6},{8,11},{9,8},{10,9... | collective-permute-start | bytes 86024 | tf_op jit(solution)/shard_map/ppermute | solution.py:49
  27.6 0.0 copy-done.2
  27.6 7.3 %inner.1 = (f32[4,24,256]{2,1,0:T(8,128)S(1)}, bf16[3,256,2304]{2,1,0:T(8,128)(2,1)S(1)}) custom-call(bf16[1024,128]{1,0:T(8,128)(2,1)S(1)} %get-tuple-element.17.mean_ref, bf16[384,128]{1,0:T(8,128)(2,1)S(1)} %collective-permute-done.4.before_ref, bf16[384,128]{1,0:T(8,128)(2,1)S(1)} %collective-permute-done.5.after_ref, bf16[3,32,864]{2,1,0:T(8,128)(2,1)S(1)} %copy-done.2, ...), custom_call_target="tpu_custom_call" | custom-call | flops 8589934592 | bytes 1048576 | tf_op jit(solution)/shard_map/inner/pallas_call | solution.py:506
  35.0 0.0 collective-permute-done.6.below_ref
  35.0 0.0 collective-permute-done.7.above_ref
  35.0 5.3 %pick.1 = f32[3,1,10240]{2,1,0:T(1,128)} custom-call(f32[4,24,256]{2,1,0:T(8,128)S(1)} %get-tuple-element.20.flow_ref, bf16[112,128]{1,0:T(8,128)(2,1)S(1)} %collective-permute-done.6.below_ref, bf16[112,128]{1,0:T(8,128)(2,1)S(1)} %maximum_bitcast_fusion.1.low_ref, bf16[112,128]{1,0:T(8,128)(2,1)S(1)} %maximum_bitcast_fusion.high_ref, ...), custom_call_target="tpu_custom_call" | custom-call | flops 5368709120 | bytes 1048576 | tf_op jit(solution)/shard_map/pick/pallas_call | solution.py:523
  (20 shorter events, 0.1 us)
Async XLA Ops:
  1.7 6.5 %collective-permute-start = (bf16[18,1536]{1,0:T(8,128)(2,1)}, bf16[18,1536]{1,0:T(8,128)(2,1)S(1)}, u32[]{:S(2)}, u32[]{:S(2)}) collective-permute-start(bf16[18,1536]{1,0:T(8,128)(2,1)} %get-tuple-element.14), channel_id=1, source_target_pairs={{0,12},{4,0},{8,4},{12,8},{1,13},{5,1},{9,5},{13,9},{2,14},{6,2},{... | collective-permute-start | bytes 165896 | tf_op jit(solution)/shard_map/ppermute | solution.py:49
  4.1 4.0 %collective-permute-start.1 = (bf16[18,1536]{1,0:T(8,128)(2,1)}, bf16[18,1536]{1,0:T(8,128)(2,1)S(1)}, u32[]{:S(2)}, u32[]{:S(2)}) collective-permute-start(bf16[18,1536]{1,0:T(8,128)(2,1)} %get-tuple-element.15), channel_id=1, source_target_pairs={{0,4},{4,8},{8,12},{12,0},{1,5},{5,9},{9,13},{13,1},{2,6},{6,10},{... | collective-permute-start | bytes 165896 | tf_op jit(solution)/shard_map/ppermute | solution.py:49
  8.2 7.5 %collective-permute-start.2 = (bf16[18,1536]{1,0:T(8,128)(2,1)S(1)}, bf16[18,1536]{1,0:T(8,128)(2,1)S(1)}, u32[]{:S(2)}, u32[]{:S(2)}) collective-permute-start(bf16[18,1536]{1,0:T(8,128)(2,1)S(1)} %pad_maximum_fusion), channel_id=1, source_target_pairs={{0,3},{1,0},{2,1},{3,2},{4,7},{5,4},{6,5},{7,6},{8,11},{9,8},{10,9... | collective-permute-start | bytes 165896 | tf_op jit(solution)/shard_map/ppermute | solution.py:49
  11.8 6.2 %collective-permute-start.3 = (bf16[18,1536]{1,0:T(8,128)(2,1)S(1)}, bf16[18,1536]{1,0:T(8,128)(2,1)S(1)}, u32[]{:S(2)}, u32[]{:S(2)}) collective-permute-start(bf16[18,1536]{1,0:T(8,128)(2,1)S(1)} %pad_maximum_fusion.1), channel_id=1, source_target_pairs={{0,1},{1,2},{2,3},{3,0},{4,5},{5,6},{6,7},{7,4},{8,9},{9,10},{10,1... | collective-permute-start | bytes 165896 | tf_op jit(solution)/shard_map/ppermute | solution.py:49
  11.9 0.9 %copy-start = (bf16[16,1,1,6144]{3,0,2,1:T(8,128)(2,1)S(1)}, bf16[16,1,1,6144]{3,0,2,1:T(8,128)(2,1)}, u32[]{:S(2)}) copy-start(bf16[16,1,1,6144]{3,0,2,1:T(8,128)(2,1)} %param.10) | copy-start | bytes 589828
  12.8 0.7 %copy-start.3 = (s32[1,1,6144]{2,1,0:T(1,128)S(1)}, s32[1,1,6144]{2,1,0:T(1,128)}, u32[]{:S(2)}) copy-start(s32[1,1,6144]{2,1,0:T(1,128)} %param.11) | copy-start | bytes 73732
  13.6 1.9 %copy-start.7 = (bf16[32,16]{0,1:T(8,128)(2,1)S(1)}, bf16[32,16]{0,1:T(8,128)(2,1)}, u32[]{:S(2)}) copy-start(bf16[32,16]{0,1:T(8,128)(2,1)} %param.15) | copy-start | bytes 3076
  13.6 2.0 %copy-start.8 = (f32[3,32]{1,0:T(4,128)S(1)}, f32[3,32]{1,0:T(4,128)}, u32[]{:S(2)}) copy-start(f32[3,32]{1,0:T(4,128)} %param.17) | copy-start | bytes 1156
  15.7 11.9 %copy-start.2 = (bf16[3,32,864]{2,1,0:T(8,128)(2,1)S(1)}, bf16[3,32,864]{2,1,0:T(8,128)(2,1)}, u32[]{:S(2)}) copy-start(bf16[3,32,864]{2,1,0:T(8,128)(2,1)} %weight_ref.1) | copy-start | bytes 497668
  15.7 11.9 %copy-start.5 = (bf16[3,32]{1,0:T(4,128)(2,1)S(1)}, bf16[3,32]{1,0:T(4,128)(2,1)}, u32[]{:S(2)}) copy-start(bf16[3,32]{1,0:T(4,128)(2,1)} %decoder_ref.3) | copy-start | bytes 580
  19.6 4.1 %collective-permute-start.4 = (bf16[384,128]{1,0:T(8,128)(2,1)S(1)}, bf16[384,128]{1,0:T(8,128)(2,1)S(1)}, u32[]{:S(2)}, u32[]{:S(2)}) collective-permute-start(bf16[384,128]{1,0:T(8,128)(2,1)S(1)} %get-tuple-element.18), channel_id=1, source_target_pairs={{0,4},{4,8},{8,12},{12,0},{1,5},{5,9},{9,13},{13,1},{2,6},{6,10},{... | collective-permute-start | bytes 294920 | tf_op jit(solution)/shard_map/ppermute | solution.py:49
  19.6 4.0 %collective-permute-start.5 = (bf16[384,128]{1,0:T(8,128)(2,1)S(1)}, bf16[384,128]{1,0:T(8,128)(2,1)S(1)}, u32[]{:S(2)}, u32[]{:S(2)}) collective-permute-start(bf16[384,128]{1,0:T(8,128)(2,1)S(1)} %get-tuple-element.19), channel_id=1, source_target_pairs={{0,12},{4,0},{8,4},{12,8},{1,13},{5,1},{9,5},{13,9},{2,14},{6,2},{... | collective-permute-start | bytes 294920 | tf_op jit(solution)/shard_map/ppermute | solution.py:49
  23.7 11.3 %collective-permute-start.6 = (bf16[112,128]{1,0:T(8,128)(2,1)S(1)}, bf16[112,128]{1,0:T(8,128)(2,1)S(1)}, u32[]{:S(2)}, u32[]{:S(2)}) collective-permute-start(bf16[112,128]{1,0:T(8,128)(2,1)S(1)} %maximum_bitcast_fusion.high_ref), channel_id=1, source_target_pairs={{0,1},{1,2},{2,3},{3,0},{4,5},{5,6},{6,7},{7,4},{8,9},{9,10},{10,1... | collective-permute-start | bytes 86024 | tf_op jit(solution)/shard_map/ppermute | solution.py:49
  23.8 11.2 %copy-start.1 = (bf16[16,1,1,6144]{3,0,2,1:T(8,128)(2,1)S(1)}, bf16[16,1,1,6144]{3,0,2,1:T(8,128)(2,1)}, u32[]{:S(2)}) copy-start(bf16[16,1,1,6144]{3,0,2,1:T(8,128)(2,1)} %param.10) | copy-start | bytes 589828
  23.8 11.2 %copy-start.4 = (s32[1,1,6144]{2,1,0:T(1,128)S(1)}, s32[1,1,6144]{2,1,0:T(1,128)}, u32[]{:S(2)}) copy-start(s32[1,1,6144]{2,1,0:T(1,128)} %param.11) | copy-start | bytes 73732
  23.8 11.2 %copy-start.6 = (bf16[3,16]{1,0:T(4,128)(2,1)S(1)}, bf16[3,16]{1,0:T(4,128)(2,1)}, u32[]{:S(2)}) copy-start(bf16[3,16]{1,0:T(4,128)(2,1)} %self_ref.1) | copy-start | bytes 292
  23.8 11.2 %collective-permute-start.7 = (bf16[112,128]{1,0:T(8,128)(2,1)S(1)}, bf16[112,128]{1,0:T(8,128)(2,1)S(1)}, u32[]{:S(2)}, u32[]{:S(2)}) collective-permute-start(bf16[112,128]{1,0:T(8,128)(2,1)S(1)} %maximum_bitcast_fusion.1.low_ref), channel_id=1, source_target_pairs={{0,3},{1,0},{2,1},{3,2},{4,7},{5,4},{6,5},{7,6},{8,11},{9,8},{10,9... | collective-permute-start | bytes 86024 | tf_op jit(solution)/shard_map/ppermute | solution.py:49

commit v4 on v3

--- a/solution.py
+++ b/solution.py
@@ -25,7 +25,10 @@
 
 
 CHUNK = 1024
-COUNTS = (4, 5, 4)
+GRANT = 24
+CORE_PARTS = ((0, 3), (3, 3))
+INNER_PARTS = ((0, 5), (5, 5))
+LAST_PARTS = ((0, 4), (4, 4))
 
 
 def repeat(count, body):
@@ -239,17 +242,19 @@
         target[s, start : start + rows, :] = moved.astype(BF)
 
 
-def conv(source, band_ref, bias_ref, layer, x, count, pitch):
-    pieces = [
-        source[s, (x + q) * pitch : (x + q + count) * pitch, :] for q in range(3) for s in range(3)
-    ]
+def rows_of(source, pitch):
+    return lambda s, x, count: source[s, x * pitch : (x + count) * pitch, :]
+
+
+def conv(pick, band_ref, bias_ref, layer, x, count):
+    pieces = [pick(s, x + q, count) for q in range(3) for s in range(3)]
     return dot(jnp.concatenate(pieces, 1), band_ref[layer], NT) + bias_ref[layer : layer + 1, :]
 
 
-def hidden(source, band_ref, bias_ref, layer, target, outs, count, pitch):
-    for x in range(0, outs, count):
-        value = gelu(conv(source, band_ref, bias_ref, layer, x, count, pitch))
-        store_shifted(target, x * pitch, value.astype(BF).astype(F32))
+def hidden(pick, band_ref, bias_ref, layer, target, parts, pitch, base=0):
+    for x, count in parts:
+        value = gelu(conv(pick, band_ref, bias_ref, layer, x, count))
+        store_shifted(target, (x - base) * pitch, value.astype(BF).astype(F32))
 
 
 def build_decode(decoder):
@@ -262,16 +267,29 @@
     ).astype(BF)
 
 
+def core_kernel(
+    mean_ref, weight_ref, encoder_ref, bias_ref, middle_ref, band_ref, input_one
+):
+    inside = dot(mean_ref[...], build_spread(encoder_ref[...]), NT).astype(BF)
+    store_shifted(input_one, 0, inside.astype(F32))
+    build_band(weight_ref, 0, band_ref)
+    hidden(
+        rows_of(input_one, CY), band_ref, bias_ref, 0, middle_ref, CORE_PARTS, CY
+    )
+    build_band(weight_ref, 1, band_ref)
+    build_band(weight_ref, 2, band_ref)
+
+
 def inner_kernel(
     mean_ref,
     before_ref,
     after_ref,
-    weight_ref,
+    middle_ref,
+    band_ref,
     encoder_ref,
     bias_ref,
     decoder_ref,
     flow_ref,
-    band_ref,
     input_one,
     input_two,
     input_three,
@@ -288,16 +306,34 @@
     encode(before_ref, 0, False)
     encode(mean_ref, HALO, True)
     encode(after_ref, HALO + CX, False)
-    build_band(weight_ref, 0, band_ref)
-    hidden(input_one, band_ref, bias_ref, 0, input_two, CX + 4, COUNTS[0], CY)
-    build_band(weight_ref, 1, band_ref)
-    hidden(input_two, band_ref, bias_ref, 1, input_three, CX + 2, COUNTS[1], CY)
-    build_band(weight_ref, 2, band_ref)
+    hidden(
+        rows_of(input_one, CY),
+        band_ref,
+        bias_ref,
+        0,
+        input_two,
+        ((0, HALO), (HALO + CX - 2, HALO)),
+        CY,
+    )
+
+    def mixed(s, x, count):
+        blocks = []
+        for ref, low, high, base in (
+            (input_two, 0, HALO, 0),
+            (middle_ref, HALO, HALO + CX - 2, HALO),
+            (input_two, HALO + CX - 2, 2 * HALO + CX - 2, 0),
+        ):
+            start, end = max(low, x), min(high, x + count)
+            if start < end:
+                blocks.append(ref[s, (start - base) * CY : (end - base) * CY, :])
+        return jnp.concatenate(blocks, 0)
+
+    hidden(mixed, band_ref, bias_ref, 1, input_three, INNER_PARTS, CY)
     decode = build_decode(decoder_ref[...])
-    count = COUNTS[2]
-    for x in range(0, CX, count):
+    source = rows_of(input_three, CY)
+    for x, count in LAST_PARTS:
         rows = slice(x * CY, (x + count) * CY)
-        value = conv(input_three, band_ref, bias_ref, 2, x, count, CY) + own[rows, :].astype(F32)
+        value = conv(source, band_ref, bias_ref, 2, x, count) + own[rows, :].astype(F32)
         flow = dot(decode, value.astype(BF), NT)
         for pair in range(count // 2):
             flow_ref[x // 2 + pair] = flow[:, pair * LO : (pair + 1) * LO]
@@ -356,9 +392,10 @@
         [side[x * SIDE : (x + 1) * SIDE] for x in range(rows) for side in sides], 0
     )
     store_shifted(input_one, 0, strips)
-    hidden(input_one, band_ref, bias_ref, 0, input_two, rows - 2, rows - 2, STRIP)
-    hidden(input_two, band_ref, bias_ref, 1, input_three, rows - 4, rows - 4, STRIP)
-    value = conv(input_three, band_ref, bias_ref, 2, 0, CX, STRIP)
+    first, second, third = (rows_of(ref, STRIP) for ref in (input_one, input_two, input_three))
+    hidden(first, band_ref, bias_ref, 0, input_two, ((0, rows - 2),), STRIP)
+    hidden(second, band_ref, bias_ref, 1, input_three, ((0, rows - 4),), STRIP)
+    value = conv(third, band_ref, bias_ref, 2, 0, CX)
     value = value + strips[HALO * STRIP : (HALO + CX) * STRIP]
     ends = dot(build_decode(decoder_ref[...]), value.astype(BF), NT)
     lane = lax.broadcasted_iota(jnp.int32, (ends.shape[0], CY), 1)
@@ -503,14 +540,20 @@
     below = passed_along(high, "gy", 1)
     biases = jnp.tile(conv_biases, (1, Z))
     rows = CX + 2 * HALO
-    flow, band = call(
+    middle, band = call(
+        core_kernel,
+        "core",
+        [vmem()] * 4,
+        [(((3, (CX - 2) * CY, wide), BF), vmem()), (((3, wide, 9 * wide), BF), vmem())],
+        [pltpu.VMEM((3, CX * CY, wide), BF)],
+        2 << 30,
+        GRANT,
+    )(mean, conv_weights, encoder, biases)
+    (flow,) = call(
         inner_kernel,
         "inner",
-        [vmem()] * 7,
-        [
-            (((CX // 2, 3 * Z, LO), F32), vmem()),
-            (((3, wide, 9 * wide), BF), vmem()),
-        ],
+        [vmem()] * 8,
+        [(((CX // 2, 3 * Z, LO), F32), vmem())],
         [
             pltpu.VMEM((3, rows * CY, wide), BF),
             pltpu.VMEM((3, (rows - 2) * CY, wide), BF),
@@ -518,8 +561,8 @@
             pltpu.VMEM((CX * CY, wide), BF),
         ],
         8 << 30,
-        24,
-    )(mean, before, after, conv_weights, encoder, biases, decoder)
+        GRANT,
+    )(mean, before, after, middle, band, encoder, biases, decoder)
     (out,) = call(
         pick_kernel,
         "pick",
@@ -532,7 +575,7 @@
             pltpu.VMEM((2 * CX // 2 * 3 * Z, LO), BF),
         ],
         5 << 30,
-        16,
+        GRANT,
     )(
         flow,
         below,

time: 41.1 us -> 39.9 us (0.971)
  waiting for transfers between devices: 7.85 us -> 5.77 us
  Pallas kernels: 17.7 us -> 18.7 us
    ppermute x8, waiting for transfers between devices: 7.85 us -> 5.77 us  [passed_along(): lax.ppermute(x, axis, [(i, (i + by) % length) for i in range(length)])]
    pallas_call x1 -> x2, Pallas kernels: 7.32 us -> 8.3 us  [the longest x1 6.22 us: on_device(): call(inner_kernel, 'inner', [vmem()] * 8, [(((CX // 2, 3 * Z, LO), F32),...]
  transfers between devices with their start and end apart: 8 -> 8, of which waited for: 4 -> 4; matrix products, arithmetic and copies ran while one was open for 2% -> 2% of each run, Pallas kernels for 23% -> 26%
where the time goes in v4:
time: 39.9 us; the launch traced here: 39.1 us
  Pallas kernels  18.7 us (47%)
  starting transfers between devices  11.8 us (30%)
  waiting for transfers between devices  5.77 us (14%)
  local copies, waits for them, and re-layouts  2.64 us (7%)
    ppermute x8, starting transfers between devices, passed_along(): lax.ppermute(x, axis, [(i, (i + by) % length) for i in range(length)])  11.8 us
    pallas_call x1, Pallas kernels, on_device(): call(inner_kernel, 'inner', [vmem()] * 8, [(((CX // 2, 3 * Z, LO), F32),...  6.22 us
    ppermute x8, waiting for transfers between devices, passed_along(): lax.ppermute(x, axis, [(i, (i + by) % length) for i in range(length)])  5.77 us
    pallas_call x1, Pallas kernels, on_device(): call(pick_kernel, 'pick', [vmem()] * 13, [(((3, 1, stay + 8 * cap), F32),...  5.29 us
    pallas_call x1, Pallas kernels, on_device(): call(core_kernel, 'core', [vmem()] * 4, [(((3, (CX - 2) * CY, wide), BF),...  2.08 us
    pallas_call x1, Pallas kernels, on_device(): call(stay_kernel, 'stay', [vmem(), vmem()], [((sums, F32), vmem())], [],...  1.92 us
    unnamed x19, local copies, waits for them, and re-layouts  1.78 us
    pallas_call x1, Pallas kernels, on_device(): call(pack_kernel, 'pack', [hbm()] * 3, [(((width, 3 * cap), BF), vmem()),...  1.68 us
  transfers between devices with their start and end apart: 8, of which 4 were waited for; matrix products, arithmetic and copies ran while one was open for 2% of the time, Pallas kernels for 26%

profile of v4, /device:TPU:0, one launch (start us, length us, event | category | flops | bytes accessed | tf_op | source)
XLA Modules:
  0.0 39.1 jit_solution(17470959486744189223)
XLA Ops:
  0.0 1.7 %pack.1 = (bf16[18,1536]{1,0:T(8,128)(2,1)}, bf16[18,1536]{1,0:T(8,128)(2,1)}, bf16[18,1024]{1,0:T(8,128)(2,1)}) custom-call(bf16[16,8,512]{2,1,0:T(8,128)(2,1)} %bitcast.22, s32[8,512]{1,0:T(8,128)} %bitcast.23, s32[8]{0:T(128)} %bitcast.24), custom_call_target="tpu_custom_call" | custom-call | flops 1048576 | bytes 1048576 | tf_op jit(solution)/shard_map/pack/pallas_call | solution.py:479
  1.7 2.5 %collective-permute-start = (bf16[18,1536]{1,0:T(8,128)(2,1)}, bf16[18,1536]{1,0:T(8,128)(2,1)S(1)}, u32[]{:S(2)}, u32[]{:S(2)}) collective-permute-start(bf16[18,1536]{1,0:T(8,128)(2,1)} %get-tuple-element.14), channel_id=1, source_target_pairs={{0,12},{4,0},{8,4},{12,8},{1,13},{5,1},{9,5},{13,9},{2,14},{6,2},{... | collective-permute-start | bytes 165896 | tf_op jit(solution)/shard_map/ppermute | solution.py:52
  4.1 0.0 collective-permute-start.1
  4.2 0.8 %fusion.5 = (bf16[18,512]{1,0:T(8,128)(2,1)S(1)}, bf16[18,512]{1,0:T(8,128)(2,1)S(1)}) fusion(bf16[18,1024]{1,0:T(8,128)(2,1)} %get-tuple-element.16), kind=kLoop, calls=%fused_computation.9 | loop fusion | bytes 73728 | tf_op jit(solution)/shard_map/slice | solution.py:507
  4.9 3.2 %collective-permute-done.1.east_ref = bf16[18,1536]{1,0:T(8,128)(2,1)S(1)} collective-permute-done((bf16[18,1536]{1,0:T(8,128)(2,1)}, bf16[18,1536]{1,0:T(8,128)(2,1)S(1)}, u32[]{:S(2)}, u32[]{:S(2)}) %collective-permute-start.1) | collective-permute-done | bytes 55328 | tf_op jit(solution)/shard_map/ppermute | solution.py:52
  8.1 0.0 collective-permute-done.west_ref
  8.2 3.7 %collective-permute-start.2 = (bf16[18,1536]{1,0:T(8,128)(2,1)S(1)}, bf16[18,1536]{1,0:T(8,128)(2,1)S(1)}, u32[]{:S(2)}, u32[]{:S(2)}) collective-permute-start(bf16[18,1536]{1,0:T(8,128)(2,1)S(1)} %pad_maximum_fusion), channel_id=1, source_target_pairs={{0,3},{1,0},{2,1},{3,2},{4,7},{5,4},{6,5},{7,6},{8,11},{9,8},{10,9... | collective-permute-start | bytes 165896 | tf_op jit(solution)/shard_map/ppermute | solution.py:52
  11.8 0.1 collective-permute-start.3
  11.9 0.0 copy-start
  11.9 0.9 %copy-done = bf16[16,1,1,6144]{3,0,2,1:T(8,128)(2,1)S(1)} copy-done((bf16[16,1,1,6144]{3,0,2,1:T(8,128)(2,1)S(1)}, bf16[16,1,1,6144]{3,0,2,1:T(8,128)(2,1)}, u32[]{:S(2)}) %copy-start) | copy-done | bytes 196632
  12.8 0.7 %copy-done.3 = s32[1,1,6144]{2,1,0:T(1,128)S(1)} copy-done((s32[1,1,6144]{2,1,0:T(1,128)S(1)}, s32[1,1,6144]{2,1,0:T(1,128)}, u32[]{:S(2)}) %copy-start.3) | copy-done | bytes 24600
  13.6 1.9 %stay.1.part_ref = f32[544,256]{1,0:T(8,128)S(1)} custom-call(bf16[16,6144]{1,0:T(8,128)(2,1)S(1)} %bitcast.18, s32[1,6144]{1,0:T(1,128)S(1)} %bitcast.20), custom_call_target="tpu_custom_call" | custom-call | flops 5368709120 | bytes 1048576 | tf_op jit(solution)/shard_map/stay/pallas_call | solution.py:510
  15.5 0.0 copy-done.7
  15.5 0.1 copy.11.encoder_ref
  15.6 0.0 copy-done.8
  15.6 0.1 tile.10.bias_ref
  15.7 0.0 collective-permute-done.2.down_ref
  15.7 2.3 %collective-permute-done.3.up_ref = bf16[18,1536]{1,0:T(8,128)(2,1)S(1)} collective-permute-done((bf16[18,1536]{1,0:T(8,128)(2,1)S(1)}, bf16[18,1536]{1,0:T(8,128)(2,1)S(1)}, u32[]{:S(2)}, u32[]{:S(2)}) %collective-permute-start.3) | collective-permute-done | bytes 55328 | tf_op jit(solution)/shard_map/ppermute | solution.py:52
  18.0 1.5 %mean.1 = (bf16[1024,128]{1,0:T(8,128)(2,1)S(1)}, bf16[384,128]{1,0:T(8,128)(2,1)S(1)}, bf16[384,128]{1,0:T(8,128)(2,1)S(1)}, bf16[18,4096]{1,0:T(8,128)(2,1)S(1)}) custom-call(bf16[18,1536]{1,0:T(8,128)(2,1)S(1)} %collective-permute-done.west_ref, bf16[18,1536]{1,0:T(8,128)(2,1)S(1)} %collective-permute-done.1.east_ref, ...), custom_call_target="tpu_custom_call" | custom-call | flops 3221225472 | bytes 1048576 | tf_op jit(solution)/shard_map/mean/pallas_call | solution.py:515
  19.6 0.1 collective-permute-start.4
  19.6 1.7 %collective-permute-start.5 = (bf16[384,128]{1,0:T(8,128)(2,1)S(1)}, bf16[384,128]{1,0:T(8,128)(2,1)S(1)}, u32[]{:S(2)}, u32[]{:S(2)}) collective-permute-start(bf16[384,128]{1,0:T(8,128)(2,1)S(1)} %get-tuple-element.19), channel_id=1, source_target_pairs={{0,12},{4,0},{8,4},{12,8},{1,13},{5,1},{9,5},{13,9},{2,14},{6,2},{... | collective-permute-start | bytes 294920 | tf_op jit(solution)/shard_map/ppermute | solution.py:52
  21.4 0.0 copy-start.5
  21.4 2.1 %core.1 = (bf16[3,768,256]{2,1,0:T(8,128)(2,1)S(1)}, bf16[3,256,2304]{2,1,0:T(8,128)(2,1)S(1)}) custom-call(bf16[1024,128]{1,0:T(8,128)(2,1)S(1)} %get-tuple-element.17.mean_ref, bf16[3,32,864]{2,1,0:T(8,128)(2,1)S(1)} %copy-done.2, bf16[32,16]{1,0:T(8,128)(2,1)S(1)} %copy.11.encoder_ref, f32[3,256]{1,0:T(4,128)S(1)} %tile.10.bias_ref), custom_call_target="tpu_custom_call" | custom-call | flops 2147483648 | bytes 1048576 | tf_op jit(solution)/shard_map/core/pallas_call | solution.py:543
  23.5 0.1 collective-permute-done.5.after_ref
  23.6 0.1 collective-permute-done.4.before_ref
  23.7 0.1 collective-permute-start.6
  23.8 3.8 %collective-permute-start.7 = (bf16[112,128]{1,0:T(8,128)(2,1)S(1)}, bf16[112,128]{1,0:T(8,128)(2,1)S(1)}, u32[]{:S(2)}, u32[]{:S(2)}) collective-permute-start(bf16[112,128]{1,0:T(8,128)(2,1)S(1)} %maximum_bitcast_fusion.1.low_ref), channel_id=1, source_target_pairs={{0,3},{1,0},{2,1},{3,2},{4,7},{5,4},{6,5},{7,6},{8,11},{9,8},{10,9... | collective-permute-start | bytes 86024 | tf_op jit(solution)/shard_map/ppermute | solution.py:52
  27.6 0.0 copy-done.5
  27.6 6.2 %inner.1.flow_ref = f32[4,24,256]{2,1,0:T(8,128)S(1)} custom-call(bf16[1024,128]{1,0:T(8,128)(2,1)S(1)} %get-tuple-element.17.mean_ref, bf16[384,128]{1,0:T(8,128)(2,1)S(1)} %collective-permute-done.4.before_ref, bf16[384,128]{1,0:T(8,128)(2,1)S(1)} %collective-permute-done.5.after_ref, bf16[3,768,256]{2,1,0:T(8,128)(2,1)S(1)} %get-tuple-element.20.middle_ref, ...), custom_call_target="tpu_custom_call" | custom-call | flops 8589934592 | bytes 1048576 | tf_op jit(solution)/shard_map/inner/pallas_call | solution.py:552
  33.8 0.0 collective-permute-done.6.below_ref
  33.8 0.0 collective-permute-done.7.above_ref
  33.8 5.3 %pick.1 = f32[3,1,10240]{2,1,0:T(1,128)} custom-call(f32[4,24,256]{2,1,0:T(8,128)S(1)} %inner.1.flow_ref, bf16[112,128]{1,0:T(8,128)(2,1)S(1)} %collective-permute-done.6.below_ref, bf16[112,128]{1,0:T(8,128)(2,1)S(1)} %maximum_bitcast_fusion.1.low_ref, bf16[112,128]{1,0:T(8,128)(2,1)S(1)} %maximum_bitcast_fusion.high_ref, ...), custom_call_target="tpu_custom_call" | custom-call | flops 5368709120 | bytes 1048576 | tf_op jit(solution)/shard_map/pick/pallas_call | solution.py:566
  (21 shorter events, 0.1 us)
Async XLA Ops:
  1.7 6.5 %collective-permute-start = (bf16[18,1536]{1,0:T(8,128)(2,1)}, bf16[18,1536]{1,0:T(8,128)(2,1)S(1)}, u32[]{:S(2)}, u32[]{:S(2)}) collective-permute-start(bf16[18,1536]{1,0:T(8,128)(2,1)} %get-tuple-element.14), channel_id=1, source_target_pairs={{0,12},{4,0},{8,4},{12,8},{1,13},{5,1},{9,5},{13,9},{2,14},{6,2},{... | collective-permute-start | bytes 165896 | tf_op jit(solution)/shard_map/ppermute | solution.py:52
  4.1 4.0 %collective-permute-start.1 = (bf16[18,1536]{1,0:T(8,128)(2,1)}, bf16[18,1536]{1,0:T(8,128)(2,1)S(1)}, u32[]{:S(2)}, u32[]{:S(2)}) collective-permute-start(bf16[18,1536]{1,0:T(8,128)(2,1)} %get-tuple-element.15), channel_id=1, source_target_pairs={{0,4},{4,8},{8,12},{12,0},{1,5},{5,9},{9,13},{13,1},{2,6},{6,10},{... | collective-permute-start | bytes 165896 | tf_op jit(solution)/shard_map/ppermute | solution.py:52
  8.2 7.5 %collective-permute-start.2 = (bf16[18,1536]{1,0:T(8,128)(2,1)S(1)}, bf16[18,1536]{1,0:T(8,128)(2,1)S(1)}, u32[]{:S(2)}, u32[]{:S(2)}) collective-permute-start(bf16[18,1536]{1,0:T(8,128)(2,1)S(1)} %pad_maximum_fusion), channel_id=1, source_target_pairs={{0,3},{1,0},{2,1},{3,2},{4,7},{5,4},{6,5},{7,6},{8,11},{9,8},{10,9... | collective-permute-start | bytes 165896 | tf_op jit(solution)/shard_map/ppermute | solution.py:52
  11.8 6.2 %collective-permute-start.3 = (bf16[18,1536]{1,0:T(8,128)(2,1)S(1)}, bf16[18,1536]{1,0:T(8,128)(2,1)S(1)}, u32[]{:S(2)}, u32[]{:S(2)}) collective-permute-start(bf16[18,1536]{1,0:T(8,128)(2,1)S(1)} %pad_maximum_fusion.1), channel_id=1, source_target_pairs={{0,1},{1,2},{2,3},{3,0},{4,5},{5,6},{6,7},{7,4},{8,9},{9,10},{10,1... | collective-permute-start | bytes 165896 | tf_op jit(solution)/shard_map/ppermute | solution.py:52
  11.9 0.9 %copy-start = (bf16[16,1,1,6144]{3,0,2,1:T(8,128)(2,1)S(1)}, bf16[16,1,1,6144]{3,0,2,1:T(8,128)(2,1)}, u32[]{:S(2)}) copy-start(bf16[16,1,1,6144]{3,0,2,1:T(8,128)(2,1)} %param.10) | copy-start | bytes 589828
  12.8 0.7 %copy-start.3 = (s32[1,1,6144]{2,1,0:T(1,128)S(1)}, s32[1,1,6144]{2,1,0:T(1,128)}, u32[]{:S(2)}) copy-start(s32[1,1,6144]{2,1,0:T(1,128)} %param.11) | copy-start | bytes 73732
  13.6 1.9 %copy-start.7 = (bf16[32,16]{0,1:T(8,128)(2,1)S(1)}, bf16[32,16]{0,1:T(8,128)(2,1)}, u32[]{:S(2)}) copy-start(bf16[32,16]{0,1:T(8,128)(2,1)} %param.15) | copy-start | bytes 3076
  13.6 2.0 %copy-start.8 = (f32[3,32]{1,0:T(4,128)S(1)}, f32[3,32]{1,0:T(4,128)}, u32[]{:S(2)}) copy-start(f32[3,32]{1,0:T(4,128)} %param.17) | copy-start | bytes 1156
  15.7 5.7 %copy-start.2 = (bf16[3,32,864]{2,1,0:T(8,128)(2,1)S(1)}, bf16[3,32,864]{2,1,0:T(8,128)(2,1)}, u32[]{:S(2)}) copy-start(bf16[3,32,864]{2,1,0:T(8,128)(2,1)} %weight_ref.1) | copy-start | bytes 497668
  19.6 4.1 %collective-permute-start.4 = (bf16[384,128]{1,0:T(8,128)(2,1)S(1)}, bf16[384,128]{1,0:T(8,128)(2,1)S(1)}, u32[]{:S(2)}, u32[]{:S(2)}) collective-permute-start(bf16[384,128]{1,0:T(8,128)(2,1)S(1)} %get-tuple-element.18), channel_id=1, source_target_pairs={{0,4},{4,8},{8,12},{12,0},{1,5},{5,9},{9,13},{13,1},{2,6},{6,10},{... | collective-permute-start | bytes 294920 | tf_op jit(solution)/shard_map/ppermute | solution.py:52
  19.6 4.0 %collective-permute-start.5 = (bf16[384,128]{1,0:T(8,128)(2,1)S(1)}, bf16[384,128]{1,0:T(8,128)(2,1)S(1)}, u32[]{:S(2)}, u32[]{:S(2)}) collective-permute-start(bf16[384,128]{1,0:T(8,128)(2,1)S(1)} %get-tuple-element.19), channel_id=1, source_target_pairs={{0,12},{4,0},{8,4},{12,8},{1,13},{5,1},{9,5},{13,9},{2,14},{6,2},{... | collective-permute-start | bytes 294920 | tf_op jit(solution)/shard_map/ppermute | solution.py:52
  21.4 6.2 %copy-start.5 = (bf16[3,32]{1,0:T(4,128)(2,1)S(1)}, bf16[3,32]{1,0:T(4,128)(2,1)}, u32[]{:S(2)}) copy-start(bf16[3,32]{1,0:T(4,128)(2,1)} %decoder_ref.3) | copy-start | bytes 580
  23.7 10.1 %collective-permute-start.6 = (bf16[112,128]{1,0:T(8,128)(2,1)S(1)}, bf16[112,128]{1,0:T(8,128)(2,1)S(1)}, u32[]{:S(2)}, u32[]{:S(2)}) collective-permute-start(bf16[112,128]{1,0:T(8,128)(2,1)S(1)} %maximum_bitcast_fusion.high_ref), channel_id=1, source_target_pairs={{0,1},{1,2},{2,3},{3,0},{4,5},{5,6},{6,7},{7,4},{8,9},{9,10},{10,1... | collective-permute-start | bytes 86024 | tf_op jit(solution)/shard_map/ppermute | solution.py:52
  23.8 10.1 %collective-permute-start.7 = (bf16[112,128]{1,0:T(8,128)(2,1)S(1)}, bf16[112,128]{1,0:T(8,128)(2,1)S(1)}, u32[]{:S(2)}, u32[]{:S(2)}) collective-permute-start(bf16[112,128]{1,0:T(8,128)(2,1)S(1)} %maximum_bitcast_fusion.1.low_ref), channel_id=1, source_target_pairs={{0,3},{1,0},{2,1},{3,2},{4,7},{5,4},{6,5},{7,6},{8,11},{9,8},{10,9... | collective-permute-start | bytes 86024 | tf_op jit(solution)/shard_map/ppermute | solution.py:52
  27.6 6.3 %copy-start.1 = (bf16[16,1,1,6144]{3,0,2,1:T(8,128)(2,1)S(1)}, bf16[16,1,1,6144]{3,0,2,1:T(8,128)(2,1)}, u32[]{:S(2)}) copy-start(bf16[16,1,1,6144]{3,0,2,1:T(8,128)(2,1)} %param.10) | copy-start | bytes 589828
  27.6 6.3 %copy-start.4 = (s32[1,1,6144]{2,1,0:T(1,128)S(1)}, s32[1,1,6144]{2,1,0:T(1,128)}, u32[]{:S(2)}) copy-start(s32[1,1,6144]{2,1,0:T(1,128)} %param.11) | copy-start | bytes 73732
  27.6 6.3 %copy-start.6 = (bf16[3,16]{1,0:T(4,128)(2,1)S(1)}, bf16[3,16]{1,0:T(4,128)(2,1)}, u32[]{:S(2)}) copy-start(bf16[3,16]{1,0:T(4,128)(2,1)} %self_ref.1) | copy-start | bytes 292

commit v5 on v4

--- a/solution.py
+++ b/solution.py
@@ -16,6 +16,7 @@
 DEAD = 2 * HI
 HALO = 3
 SIDE = 8
+PITCH = CY + 2 * SIDE
 KEPT = SIDE // 2
 STRIP = 4 * SIDE
 BF = jnp.bfloat16
@@ -61,7 +62,11 @@
 
 
 def hbm():
-    return pl.BlockSpec(memory_space=pl.ANY)
+    return pl.BlockSpec(memory_space=pltpu.HBM)
+
+
+def in_hbm(x):
+    return pltpu.with_memory_space_constraint(x, pltpu.HBM)
 
 
 def call(kernel, name, ins, outs, scratch, flops, mib):
@@ -123,18 +128,23 @@
         out_ref[feat_dim:, at] = codes.astype(BF)
 
 
-def stay_kernel(feat_ref, slot_ref, sum_ref):
+def stay_kernel(feat_in, slot_in, sum_ref, feat_ref, slot_ref, sems):
+    copies = [
+        pltpu.make_async_copy(slot_in, slot_ref, sems.at[0]),
+        pltpu.make_async_copy(feat_in, feat_ref, sems.at[1]),
+    ]
+    for copy in copies:
+        copy.start()
+    for copy in copies:
+        copy.wait()
     chunk = CHUNK
-    sum_ref[...] = jnp.zeros_like(sum_ref)
-
-    def body(step):
+    for step in range(feat_ref.shape[1] // chunk):
         at = aligned(step * chunk, chunk)
         high, low = cell_codes(slot_ref[:, at])
-        sum_ref[...] += scatter_part(
+        part = scatter_part(
             feat_ref[:, at], high.astype(F32).astype(BF), low.astype(F32).astype(BF)
         )
-
-    repeat(feat_ref.shape[1] // chunk, body)
+        sum_ref[...] = sum_ref[...] + part if step else part
 
 
 def tiled_rows(small, count):
@@ -267,76 +277,44 @@
     ).astype(BF)
 
 
+def store_padded(target, x, value):
+    side = jnp.zeros((SIDE, value.shape[1]), F32)
+    for k in range(value.shape[0] // CY):
+        block = jnp.concatenate([side, value[k * CY : (k + 1) * CY], side], 0)
+        store_shifted(target, (x + k) * PITCH, block)
+
+
 def core_kernel(
-    mean_ref, weight_ref, encoder_ref, bias_ref, middle_ref, band_ref, input_one
+    mean_ref, weight_ref, encoder_ref, bias_ref, middle_ref, own_ref, band_ref, input_one
 ):
     inside = dot(mean_ref[...], build_spread(encoder_ref[...]), NT).astype(BF)
+    own_ref[...] = inside
     store_shifted(input_one, 0, inside.astype(F32))
     build_band(weight_ref, 0, band_ref)
-    hidden(
-        rows_of(input_one, CY), band_ref, bias_ref, 0, middle_ref, CORE_PARTS, CY
-    )
+    source = rows_of(input_one, CY)
+    for x, count in CORE_PARTS:
+        value = gelu(conv(source, band_ref, bias_ref, 0, x, count))
+        store_padded(middle_ref, x, value.astype(BF).astype(F32))
     build_band(weight_ref, 1, band_ref)
     build_band(weight_ref, 2, band_ref)
 
 
-def inner_kernel(
-    mean_ref,
-    before_ref,
-    after_ref,
-    middle_ref,
-    band_ref,
-    encoder_ref,
-    bias_ref,
-    decoder_ref,
-    flow_ref,
-    input_one,
-    input_two,
-    input_three,
-    own,
+def outer_kernel(
+    own_ref, before_ref, after_ref, band_ref, encoder_ref, bias_ref, outer_ref, input_one
 ):
     spread = build_spread(encoder_ref[...])
-
-    def encode(ref, base, keep):
-        inside = dot(ref[...], spread, NT).astype(BF)
-        if keep:
-            own[...] = inside
-        store_shifted(input_one, base * CY, inside.astype(F32))
-
-    encode(before_ref, 0, False)
-    encode(mean_ref, HALO, True)
-    encode(after_ref, HALO + CX, False)
-    hidden(
-        rows_of(input_one, CY),
-        band_ref,
-        bias_ref,
-        0,
-        input_two,
-        ((0, HALO), (HALO + CX - 2, HALO)),
-        CY,
-    )
-
-    def mixed(s, x, count):
-        blocks = []
-        for ref, low, high, base in (
-            (input_two, 0, HALO, 0),
-            (middle_ref, HALO, HALO + CX - 2, HALO),
-            (input_two, HALO + CX - 2, 2 * HALO + CX - 2, 0),
-        ):
-            start, end = max(low, x), min(high, x + count)
-            if start < end:
-                blocks.append(ref[s, (start - base) * CY : (end - base) * CY, :])
-        return jnp.concatenate(blocks, 0)
-
-    hidden(mixed, band_ref, bias_ref, 1, input_three, INNER_PARTS, CY)
-    decode = build_decode(decoder_ref[...])
-    source = rows_of(input_three, CY)
-    for x, count in LAST_PARTS:
-        rows = slice(x * CY, (x + count) * CY)
-        value = conv(source, band_ref, bias_ref, 2, x, count) + own[rows, :].astype(F32)
-        flow = dot(decode, value.astype(BF), NT)
-        for pair in range(count // 2):
-            flow_ref[x // 2 + pair] = flow[:, pair * LO : (pair + 1) * LO]
+    near = (HALO - 1) * CY
+    first = dot(before_ref[...], spread, NT).astype(BF).astype(F32)
+    last = dot(after_ref[...], spread, NT).astype(BF).astype(F32)
+    low = jnp.concatenate([first, own_ref[:near].astype(F32)], 0)
+    high = jnp.concatenate([own_ref[CX * CY - near :].astype(F32), last], 0)
+    store_shifted(input_one, 0, low)
+    store_shifted(input_one, low.shape[0], high)
+    source = rows_of(input_one, CY)
+    for side in range(2):
+        x = side * (2 * HALO - 1)
+        value = gelu(conv(source, band_ref, bias_ref, 0, x, HALO))
+        store_padded(outer_ref, side * HALO, value.astype(BF).astype(F32))
 
 
 def pick_rows(table, feats, high, low, self_weight):
@@ -363,7 +341,9 @@
 
 
 def pick_kernel(
-    flow_ref,
+    middle_ref,
+    outer_ref,
+    own_ref,
     below_ref,
     low_ref,
     high_ref,
@@ -372,16 +352,25 @@
     encoder_ref,
     bias_ref,
     decoder_ref,
-    feat_ref,
-    slot_ref,
+    feat_in,
+    slot_in,
     held_ref,
     self_ref,
     out_ref,
-    input_one,
-    input_two,
+    strip_ref,
+    ends_ref,
     input_three,
     table,
+    feat_ref,
+    slot_ref,
+    sems,
 ):
+    copies = [
+        pltpu.make_async_copy(slot_in, slot_ref, sems.at[0]),
+        pltpu.make_async_copy(feat_in, feat_ref, sems.at[1]),
+    ]
+    for copy in copies:
+        copy.start()
     spread = build_spread(encoder_ref[...])
     sides = [
         dot(ref[...], spread, NT).astype(BF).astype(F32)
@@ -391,33 +380,57 @@
     strips = jnp.concatenate(
         [side[x * SIDE : (x + 1) * SIDE] for x in range(rows) for side in sides], 0
     )
-    store_shifted(input_one, 0, strips)
-    first, second, third = (rows_of(ref, STRIP) for ref in (input_one, input_two, input_three))
-    hidden(first, band_ref, bias_ref, 0, input_two, ((0, rows - 2),), STRIP)
-    hidden(second, band_ref, bias_ref, 1, input_three, ((0, rows - 4),), STRIP)
-    value = conv(third, band_ref, bias_ref, 2, 0, CX)
-    value = value + strips[HALO * STRIP : (HALO + CX) * STRIP]
-    ends = dot(build_decode(decoder_ref[...]), value.astype(BF), NT)
-    lane = lax.broadcasted_iota(jnp.int32, (ends.shape[0], CY), 1)
-    for pair in range(CX // 2):
-        halves = []
-        for x in (2 * pair, 2 * pair + 1):
-            place = x * STRIP
-            source = ends[:, place // 128 * 128 : (place // 128 + 1) * 128]
-            inside = place % 128
-            start = pltpu.roll(source, (128 - inside - SIDE) % 128, 1)
-            end = pltpu.roll(source, (CY - 3 * SIDE - inside) % 128, 1)
-            middle = flow_ref[pair, :, (x % 2) * CY : (x % 2 + 1) * CY]
-            halves.append(
-                jnp.where(lane < KEPT, start, jnp.where(lane >= CY - KEPT, end, middle))
+    store_shifted(strip_ref, 0, strips)
+    value = gelu(conv(rows_of(strip_ref, STRIP), band_ref, bias_ref, 0, 0, rows - 2))
+    store_shifted(ends_ref, 0, value.astype(BF).astype(F32))
+    wide = own_ref.shape[1]
+    half = STRIP // 2
+    row = lax.broadcasted_iota(jnp.int32, (half, wide), 0)
+
+    def mixed(s, x, count):
+        blocks = []
+        for at in range(x, x + count):
+            if at < HALO:
+                ref, base = outer_ref, at
+            elif at < HALO + CX - 2:
+                ref, base = middle_ref, at - HALO
+            else:
+                ref, base = outer_ref, at - (CX - 2)
+            base = base * PITCH
+            low = ends_ref[s, at * STRIP : at * STRIP + half, :]
+            high = ends_ref[s, at * STRIP + half : (at + 1) * STRIP, :]
+            blocks.append(jnp.where(row < half - KEPT, low, ref[s, base : base + half, :]))
+            blocks.append(ref[s, base + half : base + PITCH - half, :])
+            blocks.append(
+                jnp.where(row >= KEPT, high, ref[s, base + PITCH - half : base + PITCH, :])
             )
-        flow = jnp.concatenate(halves, 1)
+        return jnp.concatenate(blocks, 0)
+
+    for x, count in INNER_PARTS:
+        value = gelu(conv(mixed, band_ref, bias_ref, 1, x, count)).astype(BF).astype(F32)
+        for k in range(count):
+            block = value[k * PITCH : (k + 1) * PITCH]
+            for s, by in enumerate((1, 0, PITCH - 1)):
+                moved = pltpu.roll(block, by, 0) if by else block
+                input_three[s, (x + k) * CY : (x + k + 1) * CY, :] = moved[
+                    SIDE : SIDE + CY
+                ].astype(BF)
+    decode = build_decode(decoder_ref[...])
+    source = rows_of(input_three, CY)
+    size = decode.shape[0]
+    for x, count in LAST_PARTS:
+        own = own_ref[x * CY : (x + count) * CY, :].astype(F32)
+        value = conv(source, band_ref, bias_ref, 2, x, count) + own
+        flow = dot(decode, value.astype(BF), NT)
         top = flow.astype(BF)
-        size = flow.shape[0]
-        table[pair * size : (pair + 1) * size, :] = top
-        table[(CX // 2 + pair) * size : (CX // 2 + pair + 1) * size, :] = (
-            flow - top.astype(F32)
-        ).astype(BF)
+        rest = (flow - top.astype(F32)).astype(BF)
+        for k in range(count // 2):
+            pair = x // 2 + k
+            lanes = slice(k * LO, (k + 1) * LO)
+            table[pair * size : (pair + 1) * size, :] = top[:, lanes]
+            table[(CX // 2 + pair) * size : (CX // 2 + pair + 1) * size, :] = rest[:, lanes]
+    for copy in copies:
+        copy.wait()
     chunk = CHUNK
     feat_dim, stay = feat_ref.shape
     eye = jnp.where(
@@ -492,24 +505,35 @@
             pltpu.SemaphoreType.DMA((3,)),
         ],
         1 << 20,
-        61,
+        4,
     )(
-        move_feats.reshape(feat_dim, 8, cap),
-        move_slots.reshape(8, cap),
-        move_counts.reshape(8),
+        in_hbm(move_feats.reshape(feat_dim, 8, cap)),
+        in_hbm(move_slots.reshape(8, cap)),
+        in_hbm(move_counts.reshape(8)),
     )
     west = passed_along(west, "gx", -1)
     east = passed_along(east, "gx", 1)
+    sums = (HI * (feat_dim + 1), LO)
+    (part,) = call(
+        stay_kernel,
+        "stay",
+        [hbm()] * 2,
+        [((sums, F32), vmem())],
+        [
+            pltpu.VMEM((feat_dim, stay), BF),
+            pltpu.VMEM((1, stay), jnp.int32),
+            pltpu.SemaphoreType.DMA((2,)),
+        ],
+        5 << 30,
+        8,
+    )(in_hbm(own_feats), in_hbm(own_slots))
+    west, east, part = lax.optimization_barrier((west, east, part))
     down = passed_along(
         jnp.concatenate([west[:, :cap], middle[:, :cap], east[:, :cap]], 1), "gy", -1
     )
     up = passed_along(
         jnp.concatenate([west[:, 2 * cap :], middle[:, cap:], east[:, 2 * cap :]], 1), "gy", 1
     )
-    sums = (HI * (feat_dim + 1), LO)
-    (part,) = call(
-        stay_kernel, "stay", [vmem(), vmem()], [((sums, F32), vmem())], [], 5 << 30, 8
-    )(own_feats, own_slots)
     wide = Z * chans
     lanes = Z * feat_dim
     mean, first, last, held = call(
@@ -540,44 +564,48 @@
     below = passed_along(high, "gy", 1)
     biases = jnp.tile(conv_biases, (1, Z))
     rows = CX + 2 * HALO
-    middle, band = call(
+    taken, own, band = call(
         core_kernel,
         "core",
         [vmem()] * 4,
-        [(((3, (CX - 2) * CY, wide), BF), vmem()), (((3, wide, 9 * wide), BF), vmem())],
+        [
+            (((3, (CX - 2) * PITCH, wide), BF), vmem()),
+            (((CX * CY, wide), BF), vmem()),
+            (((3, wide, 9 * wide), BF), vmem()),
+        ],
         [pltpu.VMEM((3, CX * CY, wide), BF)],
         2 << 30,
         GRANT,
     )(mean, conv_weights, encoder, biases)
-    (flow,) = call(
-        inner_kernel,
-        "inner",
-        [vmem()] * 8,
-        [(((CX // 2, 3 * Z, LO), F32), vmem())],
-        [
-            pltpu.VMEM((3, rows * CY, wide), BF),
-            pltpu.VMEM((3, (rows - 2) * CY, wide), BF),
-            pltpu.VMEM((3, (rows - 4) * CY, wide), BF),
-            pltpu.VMEM((CX * CY, wide), BF),
-        ],
-        8 << 30,
+    (outer,) = call(
+        outer_kernel,
+        "outer",
+        [vmem()] * 6,
+        [(((3, 2 * HALO * PITCH, wide), BF), vmem())],
+        [pltpu.VMEM((3, (4 * HALO - 2) * CY, wide), BF)],
+        2 << 30,
         GRANT,
-    )(mean, before, after, middle, band, encoder, biases, decoder)
+    )(own, before, after, band, encoder, biases)
     (out,) = call(
         pick_kernel,
         "pick",
-        [vmem()] * 13,
+        [vmem()] * 11 + [hbm()] * 2 + [vmem()] * 2,
         [(((3, 1, stay + 8 * cap), F32), vmem())],
         [
             pltpu.VMEM((3, rows * STRIP, wide), BF),
             pltpu.VMEM((3, (rows - 2) * STRIP, wide), BF),
-            pltpu.VMEM((3, (rows - 4) * STRIP, wide), BF),
+            pltpu.VMEM((3, (rows - 4) * CY, wide), BF),
             pltpu.VMEM((2 * CX // 2 * 3 * Z, LO), BF),
+            pltpu.VMEM((feat_dim, stay), BF),
+            pltpu.VMEM((1, stay), jnp.int32),
+            pltpu.SemaphoreType.DMA((2,)),
         ],
-        5 << 30,
+        8 << 30,
         GRANT,
     )(
-        flow,
+        taken,
+        outer,
+        own,
         below,
         low,
         high,
@@ -586,8 +614,8 @@
         encoder,
         biases,
         decoder,
-        own_feats,
-        own_slots,
+        in_hbm(own_feats),
+        in_hbm(own_slots),
         held,
         self_weight,
     )

time: 39.9 us -> 38.8 us (0.972)
  local copies, waits for them, and re-layouts: 2.64 us -> 0.22 us
  waiting for transfers between devices: 5.77 us -> 7.06 us
    unnamed x19 -> x11, local copies, waits for them, and re-layouts: 1.78 us -> 0.11 us
    ppermute x8, waiting for transfers between devices: 5.77 us -> 7.06 us  [passed_along(): lax.ppermute(x, axis, [(i, (i + by) % length) for i in range(length)])]
    pallas_call x4, Pallas kernels: 15.5 us -> 16.3 us  [the longest x1 9.55 us: on_device(): call(pick_kernel, 'pick', [vmem()] * 11 + [hbm()] * 2 + [vmem()] * 2, [((...]
    slice x1, local copies, waits for them, and re-layouts: 0.76 us -> 0.01 us  [on_device(): middle[:, cap:]]
    pallas_call x1, Pallas kernels: 1.68 us -> 1.06 us  [on_device(): call(pack_kernel, 'pack', [hbm()] * 3, [(((width, 3 * cap), BF), vmem()),...]
  transfers between devices with their start and end apart: 8 -> 8, of which waited for: 4 -> 5; matrix products, arithmetic and copies ran while one was open for 2% -> 1% of each run, Pallas kernels for 26% -> 18%
where the time goes in v5:
time: 38.8 us; the launch traced here: 38.3 us
  Pallas kernels  18.9 us (49%)
  starting transfers between devices  11.8 us (30%)
  waiting for transfers between devices  7.06 us (18%)
    ppermute x8, starting transfers between devices, passed_along(): lax.ppermute(x, axis, [(i, (i + by) % length) for i in range(length)])  11.8 us
    pallas_call x1, Pallas kernels, on_device(): call(pick_kernel, 'pick', [vmem()] * 11 + [hbm()] * 2 + [vmem()] * 2, [((...  9.55 us
    ppermute x8, waiting for transfers between devices, passed_along(): lax.ppermute(x, axis, [(i, (i + by) % length) for i in range(length)])  7.06 us
    pallas_call x1, Pallas kernels, on_device(): call(stay_kernel, 'stay', [hbm()] * 2, [((sums, F32), vmem())], [pltpu.VM...  2.92 us
    pallas_call x1, Pallas kernels, on_device(): call(core_kernel, 'core', [vmem()] * 4, [(((3, (CX - 2) * PITCH, wide), B...  2.11 us
    pallas_call x1, Pallas kernels, on_device(): call(outer_kernel, 'outer', [vmem()] * 6, [(((3, 2 * HALO * PITCH, wide),...  1.71 us
    pallas_call x1, Pallas kernels, on_device(): call(mean_kernel, 'mean', [vmem()] * 5, [(((CX * CY, lanes), BF), vmem())...  1.51 us
    pallas_call x1, Pallas kernels, on_device(): call(pack_kernel, 'pack', [hbm()] * 3, [(((width, 3 * cap), BF), vmem()),...  1.06 us
  transfers between devices with their start and end apart: 8, of which 5 were waited for; matrix products, arithmetic and copies ran while one was open for 1% of the time, Pallas kernels for 18%

profile of v5, /device:TPU:0, one launch (start us, length us, event | category | flops | bytes accessed | tf_op | source)
XLA Modules:
  0.0 38.3 jit_solution(8134297722348408597)
XLA Ops:
  0.0 1.1 %pack.1 = (bf16[18,1536]{1,0:T(8,128)(2,1)S(1)}, bf16[18,1536]{1,0:T(8,128)(2,1)S(1)}, bf16[18,1024]{1,0:T(8,128)(2,1)S(1)}) custom-call(bf16[16,8,512]{2,1,0:T(8,128)(2,1)} %bitcast.18, s32[8,512]{1,0:T(8,128)} %bitcast.19, s32[8]{0:T(128)} %bitcast.20), custom_call_target="tpu_custom_call" | custom-call | flops 1048576 | bytes 1048576 | tf_op jit(solution)/shard_map/pack/pallas_call | solution.py:492
  1.1 2.5 %collective-permute-start = (bf16[18,1536]{1,0:T(8,128)(2,1)S(1)}, bf16[18,1536]{1,0:T(8,128)(2,1)S(1)}, u32[]{:S(2)}, u32[]{:S(2)}) collective-permute-start(bf16[18,1536]{1,0:T(8,128)(2,1)S(1)} %get-tuple-element.18), channel_id=1, source_target_pairs={{0,12},{4,0},{8,4},{12,8},{1,13},{5,1},{9,5},{13,9},{2,14},{6,2},{... | collective-permute-start | bytes 165896 | tf_op jit(solution)/shard_map/ppermute | solution.py:53
  3.5 0.0 collective-permute-start.1
  3.5 0.0 copy-start.3
  3.5 0.0 copy-start.4
  3.5 2.9 %stay.1.part_ref = f32[544,256]{1,0:T(8,128)S(1)} custom-call(bf16[16,6144]{1,0:T(8,128)(2,1)} %bitcast.21, s32[1,6144]{1,0:T(1,128)} %bitcast.23), custom_call_target="tpu_custom_call" | custom-call | flops 5368709120 | bytes 1048576 | tf_op jit(solution)/shard_map/stay/pallas_call | solution.py:517
  6.5 0.0 collective-permute-done.west_ref
  6.5 0.8 %collective-permute-done.1.east_ref = bf16[18,1536]{1,0:T(8,128)(2,1)S(1)} collective-permute-done((bf16[18,1536]{1,0:T(8,128)(2,1)S(1)}, bf16[18,1536]{1,0:T(8,128)(2,1)S(1)}, u32[]{:S(2)}, u32[]{:S(2)}) %collective-permute-start.1) | collective-permute-done | bytes 55328 | tf_op jit(solution)/shard_map/ppermute | solution.py:53
  7.3 3.7 %collective-permute-start.2 = (bf16[18,1536]{1,0:T(8,128)(2,1)S(1)}, bf16[18,1536]{1,0:T(8,128)(2,1)S(1)}, u32[]{:S(2)}, u32[]{:S(2)}) collective-permute-start(bf16[18,1536]{1,0:T(8,128)(2,1)S(1)} %pad_maximum_fusion), channel_id=1, source_target_pairs={{0,3},{1,0},{2,1},{3,2},{4,7},{5,4},{6,5},{7,6},{8,11},{9,8},{10,9... | collective-permute-start | bytes 165896 | tf_op jit(solution)/shard_map/ppermute | solution.py:53
  11.0 0.1 collective-permute-start.3
  11.1 0.0 copy-done.3
  11.1 0.1 copy.11.encoder_ref
  11.2 0.0 copy-done.4
  11.2 0.1 tile.10.bias_ref
  11.2 0.0 copy-start
  11.3 2.2 %collective-permute-done.2.down_ref = bf16[18,1536]{1,0:T(8,128)(2,1)S(1)} collective-permute-done((bf16[18,1536]{1,0:T(8,128)(2,1)S(1)}, bf16[18,1536]{1,0:T(8,128)(2,1)S(1)}, u32[]{:S(2)}, u32[]{:S(2)}) %collective-permute-start.2) | collective-permute-done | bytes 55328 | tf_op jit(solution)/shard_map/ppermute | solution.py:53
  13.4 3.8 %collective-permute-done.3.up_ref = bf16[18,1536]{1,0:T(8,128)(2,1)S(1)} collective-permute-done((bf16[18,1536]{1,0:T(8,128)(2,1)S(1)}, bf16[18,1536]{1,0:T(8,128)(2,1)S(1)}, u32[]{:S(2)}, u32[]{:S(2)}) %collective-permute-start.3) | collective-permute-done | bytes 55328 | tf_op jit(solution)/shard_map/ppermute | solution.py:53
  17.2 1.5 %mean.1 = (bf16[1024,128]{1,0:T(8,128)(2,1)S(1)}, bf16[384,128]{1,0:T(8,128)(2,1)S(1)}, bf16[384,128]{1,0:T(8,128)(2,1)S(1)}, bf16[18,4096]{1,0:T(8,128)(2,1)S(1)}) custom-call(bf16[18,1536]{1,0:T(8,128)(2,1)S(1)} %collective-permute-done.west_ref, bf16[18,1536]{1,0:T(8,128)(2,1)S(1)} %collective-permute-done.1.east_ref, ...), custom_call_target="tpu_custom_call" | custom-call | flops 3221225472 | bytes 1048576 | tf_op jit(solution)/shard_map/mean/pallas_call | solution.py:539
  18.7 0.1 collective-permute-start.4
  18.8 1.7 %collective-permute-start.5 = (bf16[384,128]{1,0:T(8,128)(2,1)S(1)}, bf16[384,128]{1,0:T(8,128)(2,1)S(1)}, u32[]{:S(2)}, u32[]{:S(2)}) collective-permute-start(bf16[384,128]{1,0:T(8,128)(2,1)S(1)} %get-tuple-element.28), channel_id=1, source_target_pairs={{0,12},{4,0},{8,4},{12,8},{1,13},{5,1},{9,5},{13,9},{2,14},{6,2},{... | collective-permute-start | bytes 294920 | tf_op jit(solution)/shard_map/ppermute | solution.py:53
  20.5 0.0 copy-done
  20.5 2.1 %core.1 = (bf16[3,864,256]{2,1,0:T(8,128)(2,1)S(1)}, bf16[1024,256]{1,0:T(8,128)(2,1)S(1)}, bf16[3,256,2304]{2,1,0:T(8,128)(2,1)S(1)}) custom-call(bf16[1024,128]{1,0:T(8,128)(2,1)S(1)} %get-tuple-element.24.mean_ref, bf16[3,32,864]{2,1,0:T(8,128)(2,1)S(1)} %copy-done, bf16[32,16]{1,0:T(8,128)(2,1)S(1)} %copy.11.encoder_ref, f32[3,256]{1,0:T(4,128)S(1)} %tile.10.bias_ref), custom_call_target="tpu_custom_call" | custom-call | flops 2147483648 | bytes 1048576 | tf_op jit(solution)/shard_map/core/pallas_call | solution.py:567
  22.6 0.2 collective-permute-done.4.before_ref
  22.8 0.0 collective-permute-done.5.after_ref
  22.9 0.1 collective-permute-start.6
  22.9 3.8 %collective-permute-start.7 = (bf16[112,128]{1,0:T(8,128)(2,1)S(1)}, bf16[112,128]{1,0:T(8,128)(2,1)S(1)}, u32[]{:S(2)}, u32[]{:S(2)}) collective-permute-start(bf16[112,128]{1,0:T(8,128)(2,1)S(1)} %maximum_bitcast_fusion.1.low_ref), channel_id=1, source_target_pairs={{0,3},{1,0},{2,1},{3,2},{4,7},{5,4},{6,5},{7,6},{8,11},{9,8},{10,9... | collective-permute-start | bytes 86024 | tf_op jit(solution)/shard_map/ppermute | solution.py:53
  26.7 1.7 %outer.1.outer_ref = bf16[3,864,256]{2,1,0:T(8,128)(2,1)S(1)} custom-call(bf16[1024,256]{1,0:T(8,128)(2,1)S(1)} %get-tuple-element.26.own_ref, bf16[384,128]{1,0:T(8,128)(2,1)S(1)} %collective-permute-done.4.before_ref, bf16[384,128]{1,0:T(8,128)(2,1)S(1)} %collective-permute-done.5.after_ref, bf16[3,256,2304]{2,1,0:T(8,128)(2,1)S(1)} %get-tuple-element.29.band_ref, ...), custom_call_target="tpu_custom_call" | custom-call | flops 2147483648 | bytes 1048576 | tf_op jit(solution)/shard_map/outer/pallas_call | solution.py:580
  28.5 0.1 collective-permute-done.6.below_ref
  28.6 0.0 collective-permute-done.7.above_ref
  28.6 0.0 copy-done.1
  28.6 0.0 copy-done.2
  28.6 9.5 %pick.1 = f32[3,1,10240]{2,1,0:T(1,128)} custom-call(bf16[3,864,256]{2,1,0:T(8,128)(2,1)S(1)} %get-tuple-element.25.middle_ref, bf16[3,864,256]{2,1,0:T(8,128)(2,1)S(1)} %outer.1.outer_ref, bf16[1024,256]{1,0:T(8,128)(2,1)S(1)} %get-tuple-element.26.own_ref, bf16[112,128]{1,0:T(8,128)(2,1)S(1)} %collective-permute-done.6.below_ref, ...), custom_call_target="tpu_custom_call" | custom-call | flops 8589934592 | bytes 1048576 | tf_op jit(solution)/shard_map/pick/pallas_call | solution.py:589
  (12 shorter events, 0.1 us)
Async XLA Ops:
  1.1 5.4 %collective-permute-start = (bf16[18,1536]{1,0:T(8,128)(2,1)S(1)}, bf16[18,1536]{1,0:T(8,128)(2,1)S(1)}, u32[]{:S(2)}, u32[]{:S(2)}) collective-permute-start(bf16[18,1536]{1,0:T(8,128)(2,1)S(1)} %get-tuple-element.18), channel_id=1, source_target_pairs={{0,12},{4,0},{8,4},{12,8},{1,13},{5,1},{9,5},{13,9},{2,14},{6,2},{... | collective-permute-start | bytes 165896 | tf_op jit(solution)/shard_map/ppermute | solution.py:53
  3.5 3.8 %collective-permute-start.1 = (bf16[18,1536]{1,0:T(8,128)(2,1)S(1)}, bf16[18,1536]{1,0:T(8,128)(2,1)S(1)}, u32[]{:S(2)}, u32[]{:S(2)}) collective-permute-start(bf16[18,1536]{1,0:T(8,128)(2,1)S(1)} %get-tuple-element.19), channel_id=1, source_target_pairs={{0,4},{4,8},{8,12},{12,0},{1,5},{5,9},{9,13},{13,1},{2,6},{6,10},{... | collective-permute-start | bytes 165896 | tf_op jit(solution)/shard_map/ppermute | solution.py:53
  3.5 7.5 %copy-start.3 = (bf16[32,16]{0,1:T(8,128)(2,1)S(1)}, bf16[32,16]{0,1:T(8,128)(2,1)}, u32[]{:S(2)}) copy-start(bf16[32,16]{0,1:T(8,128)(2,1)} %param.15) | copy-start | bytes 3076
  3.5 7.6 %copy-start.4 = (f32[3,32]{1,0:T(4,128)S(1)}, f32[3,32]{1,0:T(4,128)}, u32[]{:S(2)}) copy-start(f32[3,32]{1,0:T(4,128)} %param.17) | copy-start | bytes 1156
  7.3 6.1 %collective-permute-start.2 = (bf16[18,1536]{1,0:T(8,128)(2,1)S(1)}, bf16[18,1536]{1,0:T(8,128)(2,1)S(1)}, u32[]{:S(2)}, u32[]{:S(2)}) collective-permute-start(bf16[18,1536]{1,0:T(8,128)(2,1)S(1)} %pad_maximum_fusion), channel_id=1, source_target_pairs={{0,3},{1,0},{2,1},{3,2},{4,7},{5,4},{6,5},{7,6},{8,11},{9,8},{10,9... | collective-permute-start | bytes 165896 | tf_op jit(solution)/shard_map/ppermute | solution.py:53
  11.0 6.2 %collective-permute-start.3 = (bf16[18,1536]{1,0:T(8,128)(2,1)S(1)}, bf16[18,1536]{1,0:T(8,128)(2,1)S(1)}, u32[]{:S(2)}, u32[]{:S(2)}) collective-permute-start(bf16[18,1536]{1,0:T(8,128)(2,1)S(1)} %pad_maximum_fusion.1), channel_id=1, source_target_pairs={{0,1},{1,2},{2,3},{3,0},{4,5},{5,6},{6,7},{7,4},{8,9},{9,10},{10,1... | collective-permute-start | bytes 165896 | tf_op jit(solution)/shard_map/ppermute | solution.py:53
  11.2 9.3 %copy-start = (bf16[3,32,864]{2,1,0:T(8,128)(2,1)S(1)}, bf16[3,32,864]{2,1,0:T(8,128)(2,1)}, u32[]{:S(2)}) copy-start(bf16[3,32,864]{2,1,0:T(8,128)(2,1)} %weight_ref.1) | copy-start | bytes 497668
  18.7 4.1 %collective-permute-start.4 = (bf16[384,128]{1,0:T(8,128)(2,1)S(1)}, bf16[384,128]{1,0:T(8,128)(2,1)S(1)}, u32[]{:S(2)}, u32[]{:S(2)}) collective-permute-start(bf16[384,128]{1,0:T(8,128)(2,1)S(1)} %get-tuple-element.27), channel_id=1, source_target_pairs={{0,4},{4,8},{8,12},{12,0},{1,5},{5,9},{9,13},{13,1},{2,6},{6,10},{... | collective-permute-start | bytes 294920 | tf_op jit(solution)/shard_map/ppermute | solution.py:53
  18.8 4.0 %collective-permute-start.5 = (bf16[384,128]{1,0:T(8,128)(2,1)S(1)}, bf16[384,128]{1,0:T(8,128)(2,1)S(1)}, u32[]{:S(2)}, u32[]{:S(2)}) collective-permute-start(bf16[384,128]{1,0:T(8,128)(2,1)S(1)} %get-tuple-element.28), channel_id=1, source_target_pairs={{0,12},{4,0},{8,4},{12,8},{1,13},{5,1},{9,5},{13,9},{2,14},{6,2},{... | collective-permute-start | bytes 294920 | tf_op jit(solution)/shard_map/ppermute | solution.py:53
  22.9 5.7 %collective-permute-start.6 = (bf16[112,128]{1,0:T(8,128)(2,1)S(1)}, bf16[112,128]{1,0:T(8,128)(2,1)S(1)}, u32[]{:S(2)}, u32[]{:S(2)}) collective-permute-start(bf16[112,128]{1,0:T(8,128)(2,1)S(1)} %maximum_bitcast_fusion.high_ref), channel_id=1, source_target_pairs={{0,1},{1,2},{2,3},{3,0},{4,5},{5,6},{6,7},{7,4},{8,9},{9,10},{10,1... | collective-permute-start | bytes 86024 | tf_op jit(solution)/shard_map/ppermute | solution.py:53
  22.9 5.6 %collective-permute-start.7 = (bf16[112,128]{1,0:T(8,128)(2,1)S(1)}, bf16[112,128]{1,0:T(8,128)(2,1)S(1)}, u32[]{:S(2)}, u32[]{:S(2)}) collective-permute-start(bf16[112,128]{1,0:T(8,128)(2,1)S(1)} %maximum_bitcast_fusion.1.low_ref), channel_id=1, source_target_pairs={{0,3},{1,0},{2,1},{3,2},{4,7},{5,4},{6,5},{7,6},{8,11},{9,8},{10,9... | collective-permute-start | bytes 86024 | tf_op jit(solution)/shard_map/ppermute | solution.py:53
  26.7 1.8 %copy-start.1 = (bf16[3,32]{1,0:T(4,128)(2,1)S(1)}, bf16[3,32]{1,0:T(4,128)(2,1)}, u32[]{:S(2)}) copy-start(bf16[3,32]{1,0:T(4,128)(2,1)} %decoder_ref.1) | copy-start | bytes 580
  26.7 1.8 %copy-start.2 = (bf16[3,16]{1,0:T(4,128)(2,1)S(1)}, bf16[3,16]{1,0:T(4,128)(2,1)}, u32[]{:S(2)}) copy-start(bf16[3,16]{1,0:T(4,128)(2,1)} %self_ref.1) | copy-start | bytes 292

commit v6 on v5

--- a/solution.py
+++ b/solution.py
@@ -28,8 +28,19 @@
 CHUNK = 1024
 GRANT = 24
 CORE_PARTS = ((0, 3), (3, 3))
-INNER_PARTS = ((0, 5), (5, 5))
-LAST_PARTS = ((0, 4), (4, 4))
+ORDER = (
+    (0, 0, 4),
+    (0, 4, 4),
+    (1, 0, 3),
+    (0, 8, 4),
+    (1, 3, 3),
+    (2, 0, 2),
+    (1, 6, 2),
+    (2, 2, 2),
+    (1, 8, 2),
+    (2, 4, 2),
+    (2, 6, 2),
+)
 
 
 def repeat(count, body):
@@ -285,9 +296,22 @@
 
 
 def core_kernel(
-    mean_ref, weight_ref, encoder_ref, bias_ref, middle_ref, own_ref, band_ref, input_one
+    mean_ref,
+    weight_ref,
+    encoder_ref,
+    bias_ref,
+    decoder_ref,
+    middle_ref,
+    own_ref,
+    band_ref,
+    spread_ref,
+    decode_ref,
+    input_one,
 ):
-    inside = dot(mean_ref[...], build_spread(encoder_ref[...]), NT).astype(BF)
+    spread = build_spread(encoder_ref[...])
+    spread_ref[...] = spread
+    decode_ref[...] = build_decode(decoder_ref[...])
+    inside = dot(mean_ref[...], spread, NT).astype(BF)
     own_ref[...] = inside
     store_shifted(input_one, 0, inside.astype(F32))
     build_band(weight_ref, 0, band_ref)
@@ -300,9 +324,9 @@
 
 
 def outer_kernel(
-    own_ref, before_ref, after_ref, band_ref, encoder_ref, bias_ref, outer_ref, input_one
+    own_ref, before_ref, after_ref, band_ref, spread_ref, bias_ref, outer_ref, input_one
 ):
-    spread = build_spread(encoder_ref[...])
+    spread = spread_ref[...]
     near = (HALO - 1) * CY
     first = dot(before_ref[...], spread, NT).astype(BF).astype(F32)
     last = dot(after_ref[...], spread, NT).astype(BF).astype(F32)
@@ -349,9 +373,9 @@
     high_ref,
     above_ref,
     band_ref,
-    encoder_ref,
+    spread_ref,
     bias_ref,
-    decoder_ref,
+    decode_ref,
     feat_in,
     slot_in,
     held_ref,
@@ -371,7 +395,7 @@
     ]
     for copy in copies:
         copy.start()
-    spread = build_spread(encoder_ref[...])
+    spread = spread_ref[...]
     sides = [
         dot(ref[...], spread, NT).astype(BF).astype(F32)
         for ref in (below_ref, low_ref, high_ref, above_ref)
@@ -381,8 +405,11 @@
         [side[x * SIDE : (x + 1) * SIDE] for x in range(rows) for side in sides], 0
     )
     store_shifted(strip_ref, 0, strips)
-    value = gelu(conv(rows_of(strip_ref, STRIP), band_ref, bias_ref, 0, 0, rows - 2))
-    store_shifted(ends_ref, 0, value.astype(BF).astype(F32))
+
+    def end_rows(x, count):
+        value = gelu(conv(rows_of(strip_ref, STRIP), band_ref, bias_ref, 0, x, count))
+        store_shifted(ends_ref, x * STRIP, value.astype(BF).astype(F32))
+
     wide = own_ref.shape[1]
     half = STRIP // 2
     row = lax.broadcasted_iota(jnp.int32, (half, wide), 0)
@@ -406,7 +433,7 @@
             )
         return jnp.concatenate(blocks, 0)
 
-    for x, count in INNER_PARTS:
+    def inner_rows(x, count):
         value = gelu(conv(mixed, band_ref, bias_ref, 1, x, count)).astype(BF).astype(F32)
         for k in range(count):
             block = value[k * PITCH : (k + 1) * PITCH]
@@ -415,10 +442,11 @@
                 input_three[s, (x + k) * CY : (x + k + 1) * CY, :] = moved[
                     SIDE : SIDE + CY
                 ].astype(BF)
-    decode = build_decode(decoder_ref[...])
+    decode = decode_ref[...]
     source = rows_of(input_three, CY)
     size = decode.shape[0]
-    for x, count in LAST_PARTS:
+
+    def last_rows(x, count):
         own = own_ref[x * CY : (x + count) * CY, :].astype(F32)
         value = conv(source, band_ref, bias_ref, 2, x, count) + own
         flow = dot(decode, value.astype(BF), NT)
@@ -429,6 +457,10 @@
             lanes = slice(k * LO, (k + 1) * LO)
             table[pair * size : (pair + 1) * size, :] = top[:, lanes]
             table[(CX // 2 + pair) * size : (CX // 2 + pair + 1) * size, :] = rest[:, lanes]
+
+    steps = (end_rows, inner_rows, last_rows)
+    for step, x, count in ORDER:
+        steps[step](x, count)
     for copy in copies:
         copy.wait()
     chunk = CHUNK
@@ -564,19 +596,21 @@
     below = passed_along(high, "gy", 1)
     biases = jnp.tile(conv_biases, (1, Z))
     rows = CX + 2 * HALO
-    taken, own, band = call(
+    taken, own, band, spread, decode = call(
         core_kernel,
         "core",
-        [vmem()] * 4,
+        [vmem()] * 5,
         [
             (((3, (CX - 2) * PITCH, wide), BF), vmem()),
             (((CX * CY, wide), BF), vmem()),
             (((3, wide, 9 * wide), BF), vmem()),
+            (((wide, lanes), BF), vmem()),
+            (((3 * Z, wide), BF), vmem()),
         ],
         [pltpu.VMEM((3, CX * CY, wide), BF)],
         2 << 30,
         GRANT,
-    )(mean, conv_weights, encoder, biases)
+    )(mean, conv_weights, encoder, biases, decoder)
     (outer,) = call(
         outer_kernel,
         "outer",
@@ -585,7 +619,7 @@
         [pltpu.VMEM((3, (4 * HALO - 2) * CY, wide), BF)],
         2 << 30,
         GRANT,
-    )(own, before, after, band, encoder, biases)
+    )(own, before, after, band, spread, biases)
     (out,) = call(
         pick_kernel,
         "pick",
@@ -611,9 +645,9 @@
         high,
         above,
         band,
-        encoder,
+        spread,
         biases,
-        decoder,
+        decode,
         in_hbm(own_feats),
         in_hbm(own_slots),
         held,

time: 38.8 us -> 37 us (0.954)
  Pallas kernels: 18.9 us -> 17 us
    pallas_call x1, Pallas kernels: 9.55 us -> 7.84 us  [on_device(): call(pick_kernel, 'pick', [vmem()] * 11 + [hbm()] * 2 + [vmem()] * 2, [((...]
where the time goes in v6:
time: 37 us; the launch traced here: 36.6 us
  Pallas kernels  17 us (46%)
  starting transfers between devices  11.8 us (32%)
  waiting for transfers between devices  7.17 us (19%)
    ppermute x8, starting transfers between devices, passed_along(): lax.ppermute(x, axis, [(i, (i + by) % length) for i in range(length)])  11.8 us
    pallas_call x1, Pallas kernels, on_device(): call(pick_kernel, 'pick', [vmem()] * 11 + [hbm()] * 2 + [vmem()] * 2, [((...  7.84 us
    ppermute x8, waiting for transfers between devices, passed_along(): lax.ppermute(x, axis, [(i, (i + by) % length) for i in range(length)])  7.17 us
    pallas_call x1, Pallas kernels, on_device(): call(stay_kernel, 'stay', [hbm()] * 2, [((sums, F32), vmem())], [pltpu.VM...  2.92 us
    pallas_call x1, Pallas kernels, on_device(): call(core_kernel, 'core', [vmem()] * 5, [(((3, (CX - 2) * PITCH, wide), B...  2.11 us
    pallas_call x1, Pallas kernels, on_device(): call(outer_kernel, 'outer', [vmem()] * 6, [(((3, 2 * HALO * PITCH, wide),...  1.6 us
    pallas_call x1, Pallas kernels, on_device(): call(mean_kernel, 'mean', [vmem()] * 5, [(((CX * CY, lanes), BF), vmem())...  1.51 us
    pallas_call x1, Pallas kernels, on_device(): call(pack_kernel, 'pack', [hbm()] * 3, [(((width, 3 * cap), BF), vmem()),...  1.06 us
  transfers between devices with their start and end apart: 8, of which 5 were waited for; matrix products, arithmetic and copies ran while one was open for 1% of the time, Pallas kernels for 18%

profile of v6, /device:TPU:0, one launch (start us, length us, event | category | flops | bytes accessed | tf_op | source)
XLA Modules:
  0.0 36.6 jit_solution(15611619445485014435)
XLA Ops:
  0.0 1.1 %pack.1 = (bf16[18,1536]{1,0:T(8,128)(2,1)S(1)}, bf16[18,1536]{1,0:T(8,128)(2,1)S(1)}, bf16[18,1024]{1,0:T(8,128)(2,1)S(1)}) custom-call(bf16[16,8,512]{2,1,0:T(8,128)(2,1)} %bitcast.18, s32[8,512]{1,0:T(8,128)} %bitcast.19, s32[8]{0:T(128)} %bitcast.20), custom_call_target="tpu_custom_call" | custom-call | flops 1048576 | bytes 1048576 | tf_op jit(solution)/shard_map/pack/pallas_call | solution.py:524
  1.1 2.5 %collective-permute-start = (bf16[18,1536]{1,0:T(8,128)(2,1)S(1)}, bf16[18,1536]{1,0:T(8,128)(2,1)S(1)}, u32[]{:S(2)}, u32[]{:S(2)}) collective-permute-start(bf16[18,1536]{1,0:T(8,128)(2,1)S(1)} %get-tuple-element.20), channel_id=1, source_target_pairs={{0,12},{4,0},{8,4},{12,8},{1,13},{5,1},{9,5},{13,9},{2,14},{6,2},{... | collective-permute-start | bytes 165896 | tf_op jit(solution)/shard_map/ppermute | solution.py:64
  3.5 0.0 collective-permute-start.1
  3.5 0.0 copy-start.3
  3.5 0.0 copy-start.4
  3.5 2.9 %stay.1.part_ref = f32[544,256]{1,0:T(8,128)S(1)} custom-call(bf16[16,6144]{1,0:T(8,128)(2,1)} %bitcast.21, s32[1,6144]{1,0:T(1,128)} %bitcast.23), custom_call_target="tpu_custom_call" | custom-call | flops 5368709120 | bytes 1048576 | tf_op jit(solution)/shard_map/stay/pallas_call | solution.py:549
  6.5 0.0 collective-permute-done.west_ref
  6.5 0.8 %collective-permute-done.1.east_ref = bf16[18,1536]{1,0:T(8,128)(2,1)S(1)} collective-permute-done((bf16[18,1536]{1,0:T(8,128)(2,1)S(1)}, bf16[18,1536]{1,0:T(8,128)(2,1)S(1)}, u32[]{:S(2)}, u32[]{:S(2)}) %collective-permute-start.1) | collective-permute-done | bytes 55328 | tf_op jit(solution)/shard_map/ppermute | solution.py:64
  7.3 3.7 %collective-permute-start.2 = (bf16[18,1536]{1,0:T(8,128)(2,1)S(1)}, bf16[18,1536]{1,0:T(8,128)(2,1)S(1)}, u32[]{:S(2)}, u32[]{:S(2)}) collective-permute-start(bf16[18,1536]{1,0:T(8,128)(2,1)S(1)} %pad_maximum_fusion), channel_id=1, source_target_pairs={{0,3},{1,0},{2,1},{3,2},{4,7},{5,4},{6,5},{7,6},{8,11},{9,8},{10,9... | collective-permute-start | bytes 165896 | tf_op jit(solution)/shard_map/ppermute | solution.py:64
  11.0 0.1 collective-permute-start.3
  11.1 0.0 copy-done.3
  11.1 0.1 copy.11.encoder_ref
  11.2 0.0 copy-done.4
  11.2 0.1 tile.10.bias_ref
  11.2 0.0 copy-start
  11.3 2.2 %collective-permute-done.2.down_ref = bf16[18,1536]{1,0:T(8,128)(2,1)S(1)} collective-permute-done((bf16[18,1536]{1,0:T(8,128)(2,1)S(1)}, bf16[18,1536]{1,0:T(8,128)(2,1)S(1)}, u32[]{:S(2)}, u32[]{:S(2)}) %collective-permute-start.2) | collective-permute-done | bytes 55328 | tf_op jit(solution)/shard_map/ppermute | solution.py:64
  13.4 3.8 %collective-permute-done.3.up_ref = bf16[18,1536]{1,0:T(8,128)(2,1)S(1)} collective-permute-done((bf16[18,1536]{1,0:T(8,128)(2,1)S(1)}, bf16[18,1536]{1,0:T(8,128)(2,1)S(1)}, u32[]{:S(2)}, u32[]{:S(2)}) %collective-permute-start.3) | collective-permute-done | bytes 55328 | tf_op jit(solution)/shard_map/ppermute | solution.py:64
  17.2 1.5 %mean.1 = (bf16[1024,128]{1,0:T(8,128)(2,1)S(1)}, bf16[384,128]{1,0:T(8,128)(2,1)S(1)}, bf16[384,128]{1,0:T(8,128)(2,1)S(1)}, bf16[18,4096]{1,0:T(8,128)(2,1)S(1)}) custom-call(bf16[18,1536]{1,0:T(8,128)(2,1)S(1)} %collective-permute-done.west_ref, bf16[18,1536]{1,0:T(8,128)(2,1)S(1)} %collective-permute-done.1.east_ref, ...), custom_call_target="tpu_custom_call" | custom-call | flops 3221225472 | bytes 1048576 | tf_op jit(solution)/shard_map/mean/pallas_call | solution.py:571
  18.7 0.1 collective-permute-start.4
  18.8 1.7 %collective-permute-start.5 = (bf16[384,128]{1,0:T(8,128)(2,1)S(1)}, bf16[384,128]{1,0:T(8,128)(2,1)S(1)}, u32[]{:S(2)}, u32[]{:S(2)}) collective-permute-start(bf16[384,128]{1,0:T(8,128)(2,1)S(1)} %get-tuple-element.30), channel_id=1, source_target_pairs={{0,12},{4,0},{8,4},{12,8},{1,13},{5,1},{9,5},{13,9},{2,14},{6,2},{... | collective-permute-start | bytes 294920 | tf_op jit(solution)/shard_map/ppermute | solution.py:64
  20.5 0.0 copy-done
  20.5 0.0 copy-done.1
  20.5 2.1 %core.1 = (bf16[3,864,256]{2,1,0:T(8,128)(2,1)S(1)}, bf16[1024,256]{1,0:T(8,128)(2,1)S(1)}, bf16[3,256,2304]{2,1,0:T(8,128)(2,1)S(1)}, bf16[256,128]{1,0:T(8,128)(2,1)S(1)}, bf16[24,256]{1,0:T(8,128)(2,1)S(1)}) custom-call(bf16[1024,128]{1,0:T(8,128)(2,1)S(1)} %get-tuple-element.26.mean_ref, bf16[3,32,864]{2,1,0:T(8,128)(2,1)S(1)} %copy-done, ...), custom_call_target="tpu_custom_call" | custom-call | flops 2147483648 | bytes 1048576 | tf_op jit(solution)/shard_map/core/pallas_call | solution.py:599
  22.7 0.2 collective-permute-done.4.before_ref
  22.8 0.0 collective-permute-done.5.after_ref
  22.9 0.1 collective-permute-start.6
  22.9 3.8 %collective-permute-start.7 = (bf16[112,128]{1,0:T(8,128)(2,1)S(1)}, bf16[112,128]{1,0:T(8,128)(2,1)S(1)}, u32[]{:S(2)}, u32[]{:S(2)}) collective-permute-start(bf16[112,128]{1,0:T(8,128)(2,1)S(1)} %maximum_bitcast_fusion.1.low_ref), channel_id=1, source_target_pairs={{0,3},{1,0},{2,1},{3,2},{4,7},{5,4},{6,5},{7,6},{8,11},{9,8},{10,9... | collective-permute-start | bytes 86024 | tf_op jit(solution)/shard_map/ppermute | solution.py:64
  26.7 1.6 %outer.1.outer_ref = bf16[3,864,256]{2,1,0:T(8,128)(2,1)S(1)} custom-call(bf16[1024,256]{1,0:T(8,128)(2,1)S(1)} %get-tuple-element.28.own_ref, bf16[384,128]{1,0:T(8,128)(2,1)S(1)} %collective-permute-done.4.before_ref, bf16[384,128]{1,0:T(8,128)(2,1)S(1)} %collective-permute-done.5.after_ref, bf16[3,256,2304]{2,1,0:T(8,128)(2,1)S(1)} %get-tuple-element.31.band_ref, ...), custom_call_target="tpu_custom_call" | custom-call | flops 2147483648 | bytes 1048576 | tf_op jit(solution)/shard_map/outer/pallas_call | solution.py:614
  28.4 0.2 collective-permute-done.6.below_ref
  28.6 0.0 collective-permute-done.7.above_ref
  28.6 0.0 copy-done.2
  28.6 7.8 %pick.1 = f32[3,1,10240]{2,1,0:T(1,128)} custom-call(bf16[3,864,256]{2,1,0:T(8,128)(2,1)S(1)} %get-tuple-element.27.middle_ref, bf16[3,864,256]{2,1,0:T(8,128)(2,1)S(1)} %outer.1.outer_ref, bf16[1024,256]{1,0:T(8,128)(2,1)S(1)} %get-tuple-element.28.own_ref, bf16[112,128]{1,0:T(8,128)(2,1)S(1)} %collective-permute-done.6.below_ref, ...), custom_call_target="tpu_custom_call" | custom-call | flops 8589934592 | bytes 1048576 | tf_op jit(solution)/shard_map/pick/pallas_call | solution.py:623
  (12 shorter events, 0.1 us)
Async XLA Ops:
  1.1 5.4 %collective-permute-start = (bf16[18,1536]{1,0:T(8,128)(2,1)S(1)}, bf16[18,1536]{1,0:T(8,128)(2,1)S(1)}, u32[]{:S(2)}, u32[]{:S(2)}) collective-permute-start(bf16[18,1536]{1,0:T(8,128)(2,1)S(1)} %get-tuple-element.20), channel_id=1, source_target_pairs={{0,12},{4,0},{8,4},{12,8},{1,13},{5,1},{9,5},{13,9},{2,14},{6,2},{... | collective-permute-start | bytes 165896 | tf_op jit(solution)/shard_map/ppermute | solution.py:64
  3.5 3.8 %collective-permute-start.1 = (bf16[18,1536]{1,0:T(8,128)(2,1)S(1)}, bf16[18,1536]{1,0:T(8,128)(2,1)S(1)}, u32[]{:S(2)}, u32[]{:S(2)}) collective-permute-start(bf16[18,1536]{1,0:T(8,128)(2,1)S(1)} %get-tuple-element.21), channel_id=1, source_target_pairs={{0,4},{4,8},{8,12},{12,0},{1,5},{5,9},{9,13},{13,1},{2,6},{6,10},{... | collective-permute-start | bytes 165896 | tf_op jit(solution)/shard_map/ppermute | solution.py:64
  3.5 7.5 %copy-start.3 = (bf16[32,16]{0,1:T(8,128)(2,1)S(1)}, bf16[32,16]{0,1:T(8,128)(2,1)}, u32[]{:S(2)}) copy-start(bf16[32,16]{0,1:T(8,128)(2,1)} %param.15) | copy-start | bytes 3076
  3.5 7.6 %copy-start.4 = (f32[3,32]{1,0:T(4,128)S(1)}, f32[3,32]{1,0:T(4,128)}, u32[]{:S(2)}) copy-start(f32[3,32]{1,0:T(4,128)} %param.17) | copy-start | bytes 1156
  7.3 6.1 %collective-permute-start.2 = (bf16[18,1536]{1,0:T(8,128)(2,1)S(1)}, bf16[18,1536]{1,0:T(8,128)(2,1)S(1)}, u32[]{:S(2)}, u32[]{:S(2)}) collective-permute-start(bf16[18,1536]{1,0:T(8,128)(2,1)S(1)} %pad_maximum_fusion), channel_id=1, source_target_pairs={{0,3},{1,0},{2,1},{3,2},{4,7},{5,4},{6,5},{7,6},{8,11},{9,8},{10,9... | collective-permute-start | bytes 165896 | tf_op jit(solution)/shard_map/ppermute | solution.py:64
  11.0 6.2 %collective-permute-start.3 = (bf16[18,1536]{1,0:T(8,128)(2,1)S(1)}, bf16[18,1536]{1,0:T(8,128)(2,1)S(1)}, u32[]{:S(2)}, u32[]{:S(2)}) collective-permute-start(bf16[18,1536]{1,0:T(8,128)(2,1)S(1)} %pad_maximum_fusion.1), channel_id=1, source_target_pairs={{0,1},{1,2},{2,3},{3,0},{4,5},{5,6},{6,7},{7,4},{8,9},{9,10},{10,1... | collective-permute-start | bytes 165896 | tf_op jit(solution)/shard_map/ppermute | solution.py:64
  11.2 9.3 %copy-start = (bf16[3,32,864]{2,1,0:T(8,128)(2,1)S(1)}, bf16[3,32,864]{2,1,0:T(8,128)(2,1)}, u32[]{:S(2)}) copy-start(bf16[3,32,864]{2,1,0:T(8,128)(2,1)} %weight_ref.1) | copy-start | bytes 497668
  11.3 9.3 %copy-start.1 = (bf16[3,32]{1,0:T(4,128)(2,1)S(1)}, bf16[3,32]{1,0:T(4,128)(2,1)}, u32[]{:S(2)}) copy-start(bf16[3,32]{1,0:T(4,128)(2,1)} %decoder_ref.1) | copy-start | bytes 580
  18.7 4.1 %collective-permute-start.4 = (bf16[384,128]{1,0:T(8,128)(2,1)S(1)}, bf16[384,128]{1,0:T(8,128)(2,1)S(1)}, u32[]{:S(2)}, u32[]{:S(2)}) collective-permute-start(bf16[384,128]{1,0:T(8,128)(2,1)S(1)} %get-tuple-element.29), channel_id=1, source_target_pairs={{0,4},{4,8},{8,12},{12,0},{1,5},{5,9},{9,13},{13,1},{2,6},{6,10},{... | collective-permute-start | bytes 294920 | tf_op jit(solution)/shard_map/ppermute | solution.py:64
  18.8 4.0 %collective-permute-start.5 = (bf16[384,128]{1,0:T(8,128)(2,1)S(1)}, bf16[384,128]{1,0:T(8,128)(2,1)S(1)}, u32[]{:S(2)}, u32[]{:S(2)}) collective-permute-start(bf16[384,128]{1,0:T(8,128)(2,1)S(1)} %get-tuple-element.30), channel_id=1, source_target_pairs={{0,12},{4,0},{8,4},{12,8},{1,13},{5,1},{9,5},{13,9},{2,14},{6,2},{... | collective-permute-start | bytes 294920 | tf_op jit(solution)/shard_map/ppermute | solution.py:64
  22.9 5.7 %collective-permute-start.6 = (bf16[112,128]{1,0:T(8,128)(2,1)S(1)}, bf16[112,128]{1,0:T(8,128)(2,1)S(1)}, u32[]{:S(2)}, u32[]{:S(2)}) collective-permute-start(bf16[112,128]{1,0:T(8,128)(2,1)S(1)} %maximum_bitcast_fusion.high_ref), channel_id=1, source_target_pairs={{0,1},{1,2},{2,3},{3,0},{4,5},{5,6},{6,7},{7,4},{8,9},{9,10},{10,1... | collective-permute-start | bytes 86024 | tf_op jit(solution)/shard_map/ppermute | solution.py:64
  22.9 5.6 %collective-permute-start.7 = (bf16[112,128]{1,0:T(8,128)(2,1)S(1)}, bf16[112,128]{1,0:T(8,128)(2,1)S(1)}, u32[]{:S(2)}, u32[]{:S(2)}) collective-permute-start(bf16[112,128]{1,0:T(8,128)(2,1)S(1)} %maximum_bitcast_fusion.1.low_ref), channel_id=1, source_target_pairs={{0,3},{1,0},{2,1},{3,2},{4,7},{5,4},{6,5},{7,6},{8,11},{9,8},{10,9... | collective-permute-start | bytes 86024 | tf_op jit(solution)/shard_map/ppermute | solution.py:64
  26.7 1.8 %copy-start.2 = (bf16[3,16]{1,0:T(4,128)(2,1)S(1)}, bf16[3,16]{1,0:T(4,128)(2,1)}, u32[]{:S(2)}) copy-start(bf16[3,16]{1,0:T(4,128)(2,1)} %self_ref.1) | copy-start | bytes 292

commit v7 on v6

--- a/solution.py
+++ b/solution.py
@@ -122,21 +122,18 @@
     lane = lax.broadcasted_iota(jnp.int32, (1, cap), 1)
     high = high.astype(F32)
     low = low.astype(F32)
-    for bucket in range(buckets):
-        out_ref, place = (
-            (west_ref, bucket)
-            if bucket < 3
-            else (middle_ref, bucket - 3)
-            if bucket < 5
-            else (east_ref, bucket - 5)
-        )
-        at = slice(place * cap, (place + 1) * cap)
-        code = jnp.where(
-            lane < count_ref[bucket], high[bucket : bucket + 1], jnp.full((1, cap), DEAD, F32)
-        )
-        codes = jnp.concatenate([code, low[bucket : bucket + 1]], 0)
-        out_ref[:feat_dim, at] = turned[bucket].astype(BF)
-        out_ref[feat_dim:, at] = codes.astype(BF)
+    blocks = cap // 128
+    step = (feat_dim + 2) * blocks
+    for out_ref, start, end in ((west_ref, 0, 3), (middle_ref, 3, 5), (east_ref, 5, buckets)):
+        for bucket in range(start, end):
+            code = jnp.where(
+                lane < count_ref[bucket], high[bucket : bucket + 1], jnp.full((1, cap), DEAD, F32)
+            )
+            base = (bucket - start) * step
+            pieces = []
+            for value in (turned[bucket], code, low[bucket : bucket + 1]):
+                pieces += [value[:, k * 128 : (k + 1) * 128] for k in range(blocks)]
+            out_ref[base : base + step, :] = jnp.concatenate(pieces, 0).astype(BF)
 
 
 def stay_kernel(feat_in, slot_in, sum_ref, feat_ref, slot_ref, sems):
@@ -206,7 +203,9 @@
 def mean_kernel(
     west_ref, east_ref, down_ref, up_ref, part_ref, mean_ref, first_ref, last_ref, held_ref, total
 ):
-    cap = west_ref.shape[1] // 3
+    cap = held_ref.shape[1] // 8
+    feat_dim = held_ref.shape[0] - 2
+    blocks = cap // 128
     order = [
         (down_ref, 0),
         (west_ref, 1),
@@ -218,10 +217,21 @@
         (up_ref, 2),
     ]
     for place, (ref, which) in enumerate(order):
-        held_ref[:, place * cap : (place + 1) * cap] = ref[:, which * cap : (which + 1) * cap]
+        step = (feat_dim + 2) * blocks
+        block = ref[which * step : (which + 1) * step, :].astype(F32)
+        feats = jnp.concatenate(
+            [block[k * feat_dim : (k + 1) * feat_dim] for k in range(blocks)], 1
+        )
+        codes = block[blocks * feat_dim :]
+        pair = [
+            jnp.concatenate([codes[j * blocks + k][None] for k in range(blocks)], 1)
+            for j in range(2)
+        ]
+        at = slice(place * cap, (place + 1) * cap)
+        held_ref[:feat_dim, at] = feats.astype(BF)
+        held_ref[feat_dim:, at] = jnp.concatenate(pair, 0).astype(BF)
     total[...] = part_ref[...]
     chunk = CHUNK
-    feat_dim = held_ref.shape[0] - 2
 
     def body(step):
         at = aligned(step * chunk, chunk)
@@ -526,9 +536,9 @@
         "pack",
         [hbm()] * 3,
         [
-            (((width, 3 * cap), BF), vmem()),
-            (((width, 3 * cap), BF), vmem()),
-            (((width, 2 * cap), BF), vmem()),
+            (((3 * width * cap // 128, 128), BF), vmem()),
+            (((3 * width * cap // 128, 128), BF), vmem()),
+            (((2 * width * cap // 128, 128), BF), vmem()),
         ],
         [
             pltpu.VMEM((feat_dim, 8, cap), BF),
@@ -560,12 +570,14 @@
         8,
     )(in_hbm(own_feats), in_hbm(own_slots))
     west, east, part = lax.optimization_barrier((west, east, part))
-    down = passed_along(
-        jnp.concatenate([west[:, :cap], middle[:, :cap], east[:, :cap]], 1), "gy", -1
-    )
-    up = passed_along(
-        jnp.concatenate([west[:, 2 * cap :], middle[:, cap:], east[:, 2 * cap :]], 1), "gy", 1
-    )
+    step = width * cap // 128
+
+    def joined(place, inner):
+        pieces = ((west, place), (middle, inner), (east, place))
+        return jnp.concatenate([ref[k * step : (k + 1) * step] for ref, k in pieces], 0)
+
+    down = passed_along(joined(0, 0), "gy", -1)
+    up = passed_along(joined(2, 1), "gy", 1)
     wide = Z * chans
     lanes = Z * feat_dim
     mean, first, last, held = call(

time: 37 us -> 36.4 us (0.984)
  waiting for transfers between devices: 7.17 us -> 6.8 us
where the time goes in v7:
time: 36.4 us; the launch traced here: 36.2 us
  Pallas kernels  17.1 us (47%)
  starting transfers between devices  11.8 us (32%)
  waiting for transfers between devices  6.8 us (19%)
    ppermute x8, starting transfers between devices, passed_along(): lax.ppermute(x, axis, [(i, (i + by) % length) for i in range(length)])  11.8 us
    pallas_call x1, Pallas kernels, on_device(): call(pick_kernel, 'pick', [vmem()] * 11 + [hbm()] * 2 + [vmem()] * 2, [((...  7.85 us
    ppermute x8, waiting for transfers between devices, passed_along(): lax.ppermute(x, axis, [(i, (i + by) % length) for i in range(length)])  6.8 us
    pallas_call x1, Pallas kernels, on_device(): call(stay_kernel, 'stay', [hbm()] * 2, [((sums, F32), vmem())], [pltpu.VM...  2.92 us
    pallas_call x1, Pallas kernels, on_device(): call(core_kernel, 'core', [vmem()] * 5, [(((3, (CX - 2) * PITCH, wide), B...  2.1 us
    pallas_call x1, Pallas kernels, on_device(): call(outer_kernel, 'outer', [vmem()] * 6, [(((3, 2 * HALO * PITCH, wide),...  1.59 us
    pallas_call x1, Pallas kernels, on_device(): call(mean_kernel, 'mean', [vmem()] * 5, [(((CX * CY, lanes), BF), vmem())...  1.52 us
    pallas_call x1, Pallas kernels, on_device(): call(pack_kernel, 'pack', [hbm()] * 3, [(((3 * width * cap // 128, 128),...  1.07 us
  transfers between devices with their start and end apart: 8, of which 5 were waited for; matrix products, arithmetic and copies ran while one was open for 1% of the time, Pallas kernels for 18%

profile of v7, /device:TPU:0, one launch (start us, length us, event | category | flops | bytes accessed | tf_op | source)
XLA Modules:
  0.0 36.2 jit_solution(3260079499598264417)
XLA Ops:
  0.0 1.1 %pack.1 = (bf16[216,128]{1,0:T(8,128)(2,1)S(1)}, bf16[216,128]{1,0:T(8,128)(2,1)S(1)}, bf16[144,128]{1,0:T(8,128)(2,1)S(1)}) custom-call(bf16[16,8,512]{2,1,0:T(8,128)(2,1)} %bitcast.18, s32[8,512]{1,0:T(8,128)} %bitcast.19, s32[8]{0:T(128)} %bitcast.20), custom_call_target="tpu_custom_call" | custom-call | flops 1048576 | bytes 1048576 | tf_op jit(solution)/shard_map/pack/pallas_call | solution.py:534
  1.1 2.5 %collective-permute-start = (bf16[216,128]{1,0:T(8,128)(2,1)S(1)}, bf16[216,128]{1,0:T(8,128)(2,1)S(1)}, u32[]{:S(2)}, u32[]{:S(2)}) collective-permute-start(bf16[216,128]{1,0:T(8,128)(2,1)S(1)} %get-tuple-element.20), channel_id=1, source_target_pairs={{0,12},{4,0},{8,4},{12,8},{1,13},{5,1},{9,5},{13,9},{2,14},{6,2},{... | collective-permute-start | bytes 165896 | tf_op jit(solution)/shard_map/ppermute | solution.py:64
  3.5 0.0 collective-permute-start.1
  3.5 0.0 copy-start.3
  3.5 0.0 copy-start.4
  3.5 2.9 %stay.1.part_ref = f32[544,256]{1,0:T(8,128)S(1)} custom-call(bf16[16,6144]{1,0:T(8,128)(2,1)} %bitcast.21, s32[1,6144]{1,0:T(1,128)} %bitcast.23), custom_call_target="tpu_custom_call" | custom-call | flops 5368709120 | bytes 1048576 | tf_op jit(solution)/shard_map/stay/pallas_call | solution.py:559
  6.5 0.0 collective-permute-done.west_ref
  6.5 0.6 %collective-permute-done.1.east_ref = bf16[216,128]{1,0:T(8,128)(2,1)S(1)} collective-permute-done((bf16[216,128]{1,0:T(8,128)(2,1)S(1)}, bf16[216,128]{1,0:T(8,128)(2,1)S(1)}, u32[]{:S(2)}, u32[]{:S(2)}) %collective-permute-start.1) | collective-permute-done | bytes 55328 | tf_op jit(solution)/shard_map/ppermute | solution.py:64
  7.1 3.7 %collective-permute-start.2 = (bf16[216,128]{1,0:T(8,128)(2,1)S(1)}, bf16[216,128]{1,0:T(8,128)(2,1)S(1)}, u32[]{:S(2)}, u32[]{:S(2)}) collective-permute-start(bf16[216,128]{1,0:T(8,128)(2,1)S(1)} %pad_maximum_fusion), channel_id=1, source_target_pairs={{0,3},{1,0},{2,1},{3,2},{4,7},{5,4},{6,5},{7,6},{8,11},{9,8},{10,9... | collective-permute-start | bytes 165896 | tf_op jit(solution)/shard_map/ppermute | solution.py:64
  10.8 0.0 collective-permute-start.3
  10.8 0.0 copy-done.3
  10.8 0.1 copy.11.encoder_ref
  10.9 0.0 copy-done.4
  10.9 0.1 tile.10.bias_ref
  11.0 0.0 copy-start
  11.0 1.8 %collective-permute-done.2.down_ref = bf16[216,128]{1,0:T(8,128)(2,1)S(1)} collective-permute-done((bf16[216,128]{1,0:T(8,128)(2,1)S(1)}, bf16[216,128]{1,0:T(8,128)(2,1)S(1)}, u32[]{:S(2)}, u32[]{:S(2)}) %collective-permute-start.2) | collective-permute-done | bytes 55328 | tf_op jit(solution)/shard_map/ppermute | solution.py:64
  12.8 3.9 %collective-permute-done.3.up_ref = bf16[216,128]{1,0:T(8,128)(2,1)S(1)} collective-permute-done((bf16[216,128]{1,0:T(8,128)(2,1)S(1)}, bf16[216,128]{1,0:T(8,128)(2,1)S(1)}, u32[]{:S(2)}, u32[]{:S(2)}) %collective-permute-start.3) | collective-permute-done | bytes 55328 | tf_op jit(solution)/shard_map/ppermute | solution.py:64
  16.7 1.5 %mean.1 = (bf16[1024,128]{1,0:T(8,128)(2,1)S(1)}, bf16[384,128]{1,0:T(8,128)(2,1)S(1)}, bf16[384,128]{1,0:T(8,128)(2,1)S(1)}, bf16[18,4096]{1,0:T(8,128)(2,1)S(1)}) custom-call(bf16[216,128]{1,0:T(8,128)(2,1)S(1)} %collective-permute-done.west_ref, bf16[216,128]{1,0:T(8,128)(2,1)S(1)} %collective-permute-done.1.east_ref, ...), custom_call_target="tpu_custom_call" | custom-call | flops 3221225472 | bytes 1048576 | tf_op jit(solution)/shard_map/mean/pallas_call | solution.py:583
  18.3 0.1 collective-permute-start.4
  18.4 1.7 %collective-permute-start.5 = (bf16[384,128]{1,0:T(8,128)(2,1)S(1)}, bf16[384,128]{1,0:T(8,128)(2,1)S(1)}, u32[]{:S(2)}, u32[]{:S(2)}) collective-permute-start(bf16[384,128]{1,0:T(8,128)(2,1)S(1)} %get-tuple-element.30), channel_id=1, source_target_pairs={{0,12},{4,0},{8,4},{12,8},{1,13},{5,1},{9,5},{13,9},{2,14},{6,2},{... | collective-permute-start | bytes 294920 | tf_op jit(solution)/shard_map/ppermute | solution.py:64
  20.1 0.0 copy-done
  20.1 0.0 copy-done.1
  20.1 2.1 %core.1 = (bf16[3,864,256]{2,1,0:T(8,128)(2,1)S(1)}, bf16[1024,256]{1,0:T(8,128)(2,1)S(1)}, bf16[3,256,2304]{2,1,0:T(8,128)(2,1)S(1)}, bf16[256,128]{1,0:T(8,128)(2,1)S(1)}, bf16[24,256]{1,0:T(8,128)(2,1)S(1)}) custom-call(bf16[1024,128]{1,0:T(8,128)(2,1)S(1)} %get-tuple-element.26.mean_ref, bf16[3,32,864]{2,1,0:T(8,128)(2,1)S(1)} %copy-done, ...), custom_call_target="tpu_custom_call" | custom-call | flops 2147483648 | bytes 1048576 | tf_op jit(solution)/shard_map/core/pallas_call | solution.py:611
  22.2 0.2 collective-permute-done.4.before_ref
  22.4 0.0 collective-permute-done.5.after_ref
  22.4 0.1 collective-permute-start.6
  22.5 3.8 %collective-permute-start.7 = (bf16[112,128]{1,0:T(8,128)(2,1)S(1)}, bf16[112,128]{1,0:T(8,128)(2,1)S(1)}, u32[]{:S(2)}, u32[]{:S(2)}) collective-permute-start(bf16[112,128]{1,0:T(8,128)(2,1)S(1)} %maximum_bitcast_fusion.1.low_ref), channel_id=1, source_target_pairs={{0,3},{1,0},{2,1},{3,2},{4,7},{5,4},{6,5},{7,6},{8,11},{9,8},{10,9... | collective-permute-start | bytes 86024 | tf_op jit(solution)/shard_map/ppermute | solution.py:64
  26.3 1.6 %outer.1.outer_ref = bf16[3,864,256]{2,1,0:T(8,128)(2,1)S(1)} custom-call(bf16[1024,256]{1,0:T(8,128)(2,1)S(1)} %get-tuple-element.28.own_ref, bf16[384,128]{1,0:T(8,128)(2,1)S(1)} %collective-permute-done.4.before_ref, bf16[384,128]{1,0:T(8,128)(2,1)S(1)} %collective-permute-done.5.after_ref, bf16[3,256,2304]{2,1,0:T(8,128)(2,1)S(1)} %get-tuple-element.31.band_ref, ...), custom_call_target="tpu_custom_call" | custom-call | flops 2147483648 | bytes 1048576 | tf_op jit(solution)/shard_map/outer/pallas_call | solution.py:626
  27.9 0.2 collective-permute-done.6.below_ref
  28.1 0.0 collective-permute-done.7.above_ref
  28.1 0.0 copy-done.2
  28.1 7.9 %pick.1 = f32[3,1,10240]{2,1,0:T(1,128)} custom-call(bf16[3,864,256]{2,1,0:T(8,128)(2,1)S(1)} %get-tuple-element.27.middle_ref, bf16[3,864,256]{2,1,0:T(8,128)(2,1)S(1)} %outer.1.outer_ref, bf16[1024,256]{1,0:T(8,128)(2,1)S(1)} %get-tuple-element.28.own_ref, bf16[112,128]{1,0:T(8,128)(2,1)S(1)} %collective-permute-done.6.below_ref, ...), custom_call_target="tpu_custom_call" | custom-call | flops 8589934592 | bytes 1048576 | tf_op jit(solution)/shard_map/pick/pallas_call | solution.py:635
  (12 shorter events, 0.1 us)
Async XLA Ops:
  1.1 5.4 %collective-permute-start = (bf16[216,128]{1,0:T(8,128)(2,1)S(1)}, bf16[216,128]{1,0:T(8,128)(2,1)S(1)}, u32[]{:S(2)}, u32[]{:S(2)}) collective-permute-start(bf16[216,128]{1,0:T(8,128)(2,1)S(1)} %get-tuple-element.20), channel_id=1, source_target_pairs={{0,12},{4,0},{8,4},{12,8},{1,13},{5,1},{9,5},{13,9},{2,14},{6,2},{... | collective-permute-start | bytes 165896 | tf_op jit(solution)/shard_map/ppermute | solution.py:64
  3.5 3.6 %collective-permute-start.1 = (bf16[216,128]{1,0:T(8,128)(2,1)S(1)}, bf16[216,128]{1,0:T(8,128)(2,1)S(1)}, u32[]{:S(2)}, u32[]{:S(2)}) collective-permute-start(bf16[216,128]{1,0:T(8,128)(2,1)S(1)} %get-tuple-element.21), channel_id=1, source_target_pairs={{0,4},{4,8},{8,12},{12,0},{1,5},{5,9},{9,13},{13,1},{2,6},{6,10},{... | collective-permute-start | bytes 165896 | tf_op jit(solution)/shard_map/ppermute | solution.py:64
  3.5 7.3 %copy-start.3 = (bf16[32,16]{0,1:T(8,128)(2,1)S(1)}, bf16[32,16]{0,1:T(8,128)(2,1)}, u32[]{:S(2)}) copy-start(bf16[32,16]{0,1:T(8,128)(2,1)} %param.15) | copy-start | bytes 3076
  3.5 7.4 %copy-start.4 = (f32[3,32]{1,0:T(4,128)S(1)}, f32[3,32]{1,0:T(4,128)}, u32[]{:S(2)}) copy-start(f32[3,32]{1,0:T(4,128)} %param.17) | copy-start | bytes 1156
  7.1 5.7 %collective-permute-start.2 = (bf16[216,128]{1,0:T(8,128)(2,1)S(1)}, bf16[216,128]{1,0:T(8,128)(2,1)S(1)}, u32[]{:S(2)}, u32[]{:S(2)}) collective-permute-start(bf16[216,128]{1,0:T(8,128)(2,1)S(1)} %pad_maximum_fusion), channel_id=1, source_target_pairs={{0,3},{1,0},{2,1},{3,2},{4,7},{5,4},{6,5},{7,6},{8,11},{9,8},{10,9... | collective-permute-start | bytes 165896 | tf_op jit(solution)/shard_map/ppermute | solution.py:64
  10.8 6.0 %collective-permute-start.3 = (bf16[216,128]{1,0:T(8,128)(2,1)S(1)}, bf16[216,128]{1,0:T(8,128)(2,1)S(1)}, u32[]{:S(2)}, u32[]{:S(2)}) collective-permute-start(bf16[216,128]{1,0:T(8,128)(2,1)S(1)} %pad_maximum_fusion.1), channel_id=1, source_target_pairs={{0,1},{1,2},{2,3},{3,0},{4,5},{5,6},{6,7},{7,4},{8,9},{9,10},{10,1... | collective-permute-start | bytes 165896 | tf_op jit(solution)/shard_map/ppermute | solution.py:64
  11.0 9.1 %copy-start = (bf16[3,32,864]{2,1,0:T(8,128)(2,1)S(1)}, bf16[3,32,864]{2,1,0:T(8,128)(2,1)}, u32[]{:S(2)}) copy-start(bf16[3,32,864]{2,1,0:T(8,128)(2,1)} %weight_ref.1) | copy-start | bytes 497668
  11.0 9.1 %copy-start.1 = (bf16[3,32]{1,0:T(4,128)(2,1)S(1)}, bf16[3,32]{1,0:T(4,128)(2,1)}, u32[]{:S(2)}) copy-start(bf16[3,32]{1,0:T(4,128)(2,1)} %decoder_ref.1) | copy-start | bytes 580
  18.3 4.1 %collective-permute-start.4 = (bf16[384,128]{1,0:T(8,128)(2,1)S(1)}, bf16[384,128]{1,0:T(8,128)(2,1)S(1)}, u32[]{:S(2)}, u32[]{:S(2)}) collective-permute-start(bf16[384,128]{1,0:T(8,128)(2,1)S(1)} %get-tuple-element.29), channel_id=1, source_target_pairs={{0,4},{4,8},{8,12},{12,0},{1,5},{5,9},{9,13},{13,1},{2,6},{6,10},{... | collective-permute-start | bytes 294920 | tf_op jit(solution)/shard_map/ppermute | solution.py:64
  18.4 4.0 %collective-permute-start.5 = (bf16[384,128]{1,0:T(8,128)(2,1)S(1)}, bf16[384,128]{1,0:T(8,128)(2,1)S(1)}, u32[]{:S(2)}, u32[]{:S(2)}) collective-permute-start(bf16[384,128]{1,0:T(8,128)(2,1)S(1)} %get-tuple-element.30), channel_id=1, source_target_pairs={{0,12},{4,0},{8,4},{12,8},{1,13},{5,1},{9,5},{13,9},{2,14},{6,2},{... | collective-permute-start | bytes 294920 | tf_op jit(solution)/shard_map/ppermute | solution.py:64
  22.4 5.7 %collective-permute-start.6 = (bf16[112,128]{1,0:T(8,128)(2,1)S(1)}, bf16[112,128]{1,0:T(8,128)(2,1)S(1)}, u32[]{:S(2)}, u32[]{:S(2)}) collective-permute-start(bf16[112,128]{1,0:T(8,128)(2,1)S(1)} %maximum_bitcast_fusion.high_ref), channel_id=1, source_target_pairs={{0,1},{1,2},{2,3},{3,0},{4,5},{5,6},{6,7},{7,4},{8,9},{9,10},{10,1... | collective-permute-start | bytes 86024 | tf_op jit(solution)/shard_map/ppermute | solution.py:64
  22.5 5.6 %collective-permute-start.7 = (bf16[112,128]{1,0:T(8,128)(2,1)S(1)}, bf16[112,128]{1,0:T(8,128)(2,1)S(1)}, u32[]{:S(2)}, u32[]{:S(2)}) collective-permute-start(bf16[112,128]{1,0:T(8,128)(2,1)S(1)} %maximum_bitcast_fusion.1.low_ref), channel_id=1, source_target_pairs={{0,3},{1,0},{2,1},{3,2},{4,7},{5,4},{6,5},{7,6},{8,11},{9,8},{10,9... | collective-permute-start | bytes 86024 | tf_op jit(solution)/shard_map/ppermute | solution.py:64
  26.3 1.8 %copy-start.2 = (bf16[3,16]{1,0:T(4,128)(2,1)S(1)}, bf16[3,16]{1,0:T(4,128)(2,1)}, u32[]{:S(2)}) copy-start(bf16[3,16]{1,0:T(4,128)(2,1)} %self_ref.1) | copy-start | bytes 292

commit v8 on v7

--- a/solution.py
+++ b/solution.py
@@ -62,6 +62,18 @@
 def passed_along(x, axis, by):
     length = lax.axis_size(axis)
     return lax.ppermute(x, axis, [(i, (i + by) % length) for i in range(length)])
+
+
+def exchanged(up, down, axis):
+    length = lax.axis_size(axis)
+    if length % 2:
+        return passed_along(down, axis, -1), passed_along(up, axis, 1)
+    even = lax.axis_index(axis) % 2 == 0
+    within = [(i, i + 1 - 2 * (i % 2)) for i in range(length)]
+    between = [(i, (i - 1 + 2 * (i % 2)) % length) for i in range(length)]
+    inner = lax.ppermute(jnp.where(even, up, down), axis, within)
+    outer = lax.ppermute(jnp.where(even, down, up), axis, between)
+    return jnp.where(even, inner, outer), jnp.where(even, outer, inner)
 
 
 def dot(a, b, dims=NN):
@@ -553,8 +565,7 @@
         in_hbm(move_slots.reshape(8, cap)),
         in_hbm(move_counts.reshape(8)),
     )
-    west = passed_along(west, "gx", -1)
-    east = passed_along(east, "gx", 1)
+    west, east = exchanged(east, west, "gx")
     sums = (HI * (feat_dim + 1), LO)
     (part,) = call(
         stay_kernel,
@@ -594,8 +605,7 @@
         3 << 30,
         8,
     )(west, east, down, up, part)
-    after = passed_along(first, "gx", -1)
-    before = passed_along(last, "gx", 1)
+    after, before = exchanged(last, first, "gx")
 
     def edge(start):
         blocks = [

time: 36.4 us -> 37.1 us (1.019)
  waiting for transfers between devices: 6.8 us -> 7.28 us
    ppermute x0 -> x4, starting transfers between devices: none -> 4.4 us  [the longest x2 3.66 us: exchanged(): outer = lax.ppermute(jnp.where(even, down, up), axis, between)]
    ppermute x8 -> x4, starting transfers between devices: 11.8 us -> 7.55 us  [passed_along(): lax.ppermute(x, axis, [(i, (i + by) % length) for i in range(length)])]
    ppermute x0 -> x4, waiting for transfers between devices: none -> 1.28 us  [the longest x2 1.28 us: exchanged(): outer = lax.ppermute(jnp.where(even, down, up), axis, between)]
    ppermute x8 -> x4, waiting for transfers between devices: 6.8 us -> 6 us  [passed_along(): lax.ppermute(x, axis, [(i, (i + by) % length) for i in range(length)])]
  transfers between devices with their start and end apart: 8 -> 8, of which waited for: 5 -> 4; matrix products, arithmetic and copies ran while one was open for 1% -> 1% of each run, Pallas kernels for 18% -> 18%
where the time goes in v8:
time: 37.1 us; the launch traced here: 36.9 us
  Pallas kernels  17 us (46%)
  starting transfers between devices  12 us (32%)
  waiting for transfers between devices  7.28 us (20%)
    pallas_call x1, Pallas kernels, on_device(): call(pick_kernel, 'pick', [vmem()] * 11 + [hbm()] * 2 + [vmem()] * 2, [((...  7.81 us
    ppermute x4, starting transfers between devices, passed_along(): lax.ppermute(x, axis, [(i, (i + by) % length) for i in range(length)])  7.55 us
    ppermute x4, waiting for transfers between devices, passed_along(): lax.ppermute(x, axis, [(i, (i + by) % length) for i in range(length)])  6 us
    ppermute x2, starting transfers between devices, exchanged(): outer = lax.ppermute(jnp.where(even, down, up), axis, between)  3.66 us
    pallas_call x1, Pallas kernels, on_device(): call(stay_kernel, 'stay', [hbm()] * 2, [((sums, F32), vmem())], [pltpu.VM...  2.92 us
    pallas_call x1, Pallas kernels, on_device(): call(core_kernel, 'core', [vmem()] * 5, [(((3, (CX - 2) * PITCH, wide), B...  2.11 us
    pallas_call x1, Pallas kernels, on_device(): call(outer_kernel, 'outer', [vmem()] * 6, [(((3, 2 * HALO * PITCH, wide),...  1.59 us
    pallas_call x1, Pallas kernels, on_device(): call(mean_kernel, 'mean', [vmem()] * 5, [(((CX * CY, lanes), BF), vmem())...  1.52 us
  transfers between devices with their start and end apart: 8, of which 4 were waited for; matrix products, arithmetic and copies ran while one was open for 1% of the time, Pallas kernels for 18%

profile of v8, /device:TPU:0, one launch (start us, length us, event | category | flops | bytes accessed | tf_op | source)
XLA Modules:
  0.0 36.9 jit_solution(10848707895202161208)
XLA Ops:
  0.0 1.1 %pack.1 = (bf16[216,128]{1,0:T(8,128)(2,1)S(1)}, bf16[216,128]{1,0:T(8,128)(2,1)S(1)}, bf16[144,128]{1,0:T(8,128)(2,1)S(1)}) custom-call(bf16[16,8,512]{2,1,0:T(8,128)(2,1)} %bitcast.18, s32[8,512]{1,0:T(8,128)} %bitcast.19, s32[8]{0:T(128)} %bitcast.20), custom_call_target="tpu_custom_call" | custom-call | flops 1048576 | bytes 1048576 | tf_op jit(solution)/shard_map/pack/pallas_call | solution.py:546
  1.1 2.5 %collective-permute-start.1 = (bf16[216,128]{1,0:T(8,128)(2,1)S(1)}, bf16[216,128]{1,0:T(8,128)(2,1)S(1)}, u32[]{:S(2)}, u32[]{:S(2)}) collective-permute-start(bf16[216,128]{1,0:T(8,128)(2,1)S(1)} %get-tuple-element.43), channel_id=1, source_target_pairs={{0,12},{4,8},{8,4},{12,0},{1,13},{5,9},{9,5},{13,1},{2,14},{6,10},... | collective-permute-start | bytes 165896 | tf_op jit(solution)/shard_map/ppermute | solution.py:75
  3.6 0.7 %collective-permute-start = (bf16[216,128]{1,0:T(8,128)(2,1)S(1)}, bf16[216,128]{1,0:T(8,128)(2,1)S(1)}, u32[]{:S(2)}, u32[]{:S(2)}) collective-permute-start(bf16[216,128]{1,0:T(8,128)(2,1)S(1)} %get-tuple-element.44), channel_id=1, source_target_pairs={{0,4},{4,0},{8,12},{12,8},{1,5},{5,1},{9,13},{13,9},{2,6},{6,2},{1... | collective-permute-start | bytes 165896 | tf_op jit(solution)/shard_map/ppermute | solution.py:74
  4.3 0.0 copy-start.3
  4.3 0.0 copy-start.4
  4.3 2.9 %stay.1.part_ref = f32[544,256]{1,0:T(8,128)S(1)} custom-call(bf16[16,6144]{1,0:T(8,128)(2,1)} %bitcast.21, s32[1,6144]{1,0:T(1,128)} %bitcast.23), custom_call_target="tpu_custom_call" | custom-call | flops 5368709120 | bytes 1048576 | tf_op jit(solution)/shard_map/stay/pallas_call | solution.py:570
  7.2 0.0 collective-permute-done.1
  7.2 0.0 collective-permute-done
  7.3 3.7 %collective-permute-start.2 = (bf16[216,128]{1,0:T(8,128)(2,1)S(1)}, bf16[216,128]{1,0:T(8,128)(2,1)S(1)}, u32[]{:S(2)}, u32[]{:S(2)}) collective-permute-start(bf16[216,128]{1,0:T(8,128)(2,1)S(1)} %pad_maximum_fusion), channel_id=1, source_target_pairs={{0,3},{1,0},{2,1},{3,2},{4,7},{5,4},{6,5},{7,6},{8,11},{9,8},{10,9... | collective-permute-start | bytes 165896 | tf_op jit(solution)/shard_map/ppermute | solution.py:64
  11.0 0.0 collective-permute-start.3
  11.0 0.0 copy-done.3
  11.0 0.1 copy.11.encoder_ref
  11.1 0.0 copy-done.4
  11.1 0.1 tile.10.bias_ref
  11.1 0.0 copy-start
  11.1 1.7 %collective-permute-done.2.down_ref = bf16[216,128]{1,0:T(8,128)(2,1)S(1)} collective-permute-done((bf16[216,128]{1,0:T(8,128)(2,1)S(1)}, bf16[216,128]{1,0:T(8,128)(2,1)S(1)}, u32[]{:S(2)}, u32[]{:S(2)}) %collective-permute-start.2) | collective-permute-done | bytes 55328 | tf_op jit(solution)/shard_map/ppermute | solution.py:64
  12.8 4.1 %collective-permute-done.3.up_ref = bf16[216,128]{1,0:T(8,128)(2,1)S(1)} collective-permute-done((bf16[216,128]{1,0:T(8,128)(2,1)S(1)}, bf16[216,128]{1,0:T(8,128)(2,1)S(1)}, u32[]{:S(2)}, u32[]{:S(2)}) %collective-permute-start.3) | collective-permute-done | bytes 55328 | tf_op jit(solution)/shard_map/ppermute | solution.py:64
  16.9 1.5 %mean.1 = (bf16[1024,128]{1,0:T(8,128)(2,1)S(1)}, bf16[384,128]{1,0:T(8,128)(2,1)S(1)}, bf16[384,128]{1,0:T(8,128)(2,1)S(1)}, bf16[18,4096]{1,0:T(8,128)(2,1)S(1)}) custom-call(bf16[216,128]{1,0:T(8,128)(2,1)S(1)} %get-tuple-element.22.west_ref, bf16[216,128]{1,0:T(8,128)(2,1)S(1)} %get-tuple-element.23.east_ref, ...), custom_call_target="tpu_custom_call" | custom-call | flops 3221225472 | bytes 1048576 | tf_op jit(solution)/shard_map/mean/pallas_call | solution.py:594
  18.5 0.1 collective-permute-start.5
  18.6 1.2 %collective-permute-start.4 = (bf16[384,128]{1,0:T(8,128)(2,1)S(1)}, bf16[384,128]{1,0:T(8,128)(2,1)S(1)}, u32[]{:S(2)}, u32[]{:S(2)}) collective-permute-start(bf16[384,128]{1,0:T(8,128)(2,1)S(1)} %get-tuple-element.40), channel_id=1, source_target_pairs={{0,12},{4,8},{8,4},{12,0},{1,13},{5,9},{9,5},{13,1},{2,14},{6,10},... | collective-permute-start | bytes 294920 | tf_op jit(solution)/shard_map/ppermute | solution.py:75
  19.7 0.0 copy-done
  19.7 0.0 copy-done.1
  19.7 2.1 %core.1 = (bf16[3,864,256]{2,1,0:T(8,128)(2,1)S(1)}, bf16[1024,256]{1,0:T(8,128)(2,1)S(1)}, bf16[3,256,2304]{2,1,0:T(8,128)(2,1)S(1)}, bf16[256,128]{1,0:T(8,128)(2,1)S(1)}, bf16[24,256]{1,0:T(8,128)(2,1)S(1)}) custom-call(bf16[1024,128]{1,0:T(8,128)(2,1)S(1)} %get-tuple-element.26.mean_ref, bf16[3,32,864]{2,1,0:T(8,128)(2,1)S(1)} %copy-done, ...), custom_call_target="tpu_custom_call" | custom-call | flops 2147483648 | bytes 1048576 | tf_op jit(solution)/shard_map/core/pallas_call | solution.py:621
  21.9 0.0 collective-permute-done.5
  21.9 1.3 %collective-permute-done.4 = bf16[384,128]{1,0:T(8,128)(2,1)S(1)} collective-permute-done((bf16[384,128]{1,0:T(8,128)(2,1)S(1)}, bf16[384,128]{1,0:T(8,128)(2,1)S(1)}, u32[]{:S(2)}, u32[]{:S(2)}) %collective-permute-start.4) | collective-permute-done | bytes 98336 | tf_op jit(solution)/shard_map/ppermute | solution.py:75
  23.2 0.1 collective-permute-start.6
  23.3 3.8 %collective-permute-start.7 = (bf16[112,128]{1,0:T(8,128)(2,1)S(1)}, bf16[112,128]{1,0:T(8,128)(2,1)S(1)}, u32[]{:S(2)}, u32[]{:S(2)}) collective-permute-start(bf16[112,128]{1,0:T(8,128)(2,1)S(1)} %maximum_bitcast_fusion.1.low_ref), channel_id=1, source_target_pairs={{0,3},{1,0},{2,1},{3,2},{4,7},{5,4},{6,5},{7,6},{8,11},{9,8},{10,9... | collective-permute-start | bytes 86024 | tf_op jit(solution)/shard_map/ppermute | solution.py:64
  27.1 1.6 %outer.1.outer_ref = bf16[3,864,256]{2,1,0:T(8,128)(2,1)S(1)} custom-call(bf16[1024,256]{1,0:T(8,128)(2,1)S(1)} %get-tuple-element.28.own_ref, bf16[384,128]{1,0:T(8,128)(2,1)S(1)} %get-tuple-element.38.before_ref, bf16[384,128]{1,0:T(8,128)(2,1)S(1)} %get-tuple-element.37.after_ref, bf16[3,256,2304]{2,1,0:T(8,128)(2,1)S(1)} %get-tuple-element.31.band_ref, ...), custom_call_target="tpu_custom_call" | custom-call | flops 2147483648 | bytes 1048576 | tf_op jit(solution)/shard_map/outer/pallas_call | solution.py:636
  28.7 0.2 collective-permute-done.6.below_ref
  29.0 0.0 collective-permute-done.7.above_ref
  29.0 0.0 copy-done.2
  29.0 7.8 %pick.1 = f32[3,1,10240]{2,1,0:T(1,128)} custom-call(bf16[3,864,256]{2,1,0:T(8,128)(2,1)S(1)} %get-tuple-element.27.middle_ref, bf16[3,864,256]{2,1,0:T(8,128)(2,1)S(1)} %outer.1.outer_ref, bf16[1024,256]{1,0:T(8,128)(2,1)S(1)} %get-tuple-element.28.own_ref, bf16[112,128]{1,0:T(8,128)(2,1)S(1)} %collective-permute-done.6.below_ref, ...), custom_call_target="tpu_custom_call" | custom-call | flops 8589934592 | bytes 1048576 | tf_op jit(solution)/shard_map/pick/pallas_call | solution.py:645
  (16 shorter events, 0.2 us)
Async XLA Ops:
  1.1 6.1 %collective-permute-start.1 = (bf16[216,128]{1,0:T(8,128)(2,1)S(1)}, bf16[216,128]{1,0:T(8,128)(2,1)S(1)}, u32[]{:S(2)}, u32[]{:S(2)}) collective-permute-start(bf16[216,128]{1,0:T(8,128)(2,1)S(1)} %get-tuple-element.43), channel_id=1, source_target_pairs={{0,12},{4,8},{8,4},{12,0},{1,13},{5,9},{9,5},{13,1},{2,14},{6,10},... | collective-permute-start | bytes 165896 | tf_op jit(solution)/shard_map/ppermute | solution.py:75
  3.6 3.6 %collective-permute-start = (bf16[216,128]{1,0:T(8,128)(2,1)S(1)}, bf16[216,128]{1,0:T(8,128)(2,1)S(1)}, u32[]{:S(2)}, u32[]{:S(2)}) collective-permute-start(bf16[216,128]{1,0:T(8,128)(2,1)S(1)} %get-tuple-element.44), channel_id=1, source_target_pairs={{0,4},{4,0},{8,12},{12,8},{1,5},{5,1},{9,13},{13,9},{2,6},{6,2},{1... | collective-permute-start | bytes 165896 | tf_op jit(solution)/shard_map/ppermute | solution.py:74
  4.3 6.7 %copy-start.3 = (bf16[32,16]{0,1:T(8,128)(2,1)S(1)}, bf16[32,16]{0,1:T(8,128)(2,1)}, u32[]{:S(2)}) copy-start(bf16[32,16]{0,1:T(8,128)(2,1)} %param.15) | copy-start | bytes 3076
  4.3 6.8 %copy-start.4 = (f32[3,32]{1,0:T(4,128)S(1)}, f32[3,32]{1,0:T(4,128)}, u32[]{:S(2)}) copy-start(f32[3,32]{1,0:T(4,128)} %param.17) | copy-start | bytes 1156
  7.3 5.5 %collective-permute-start.2 = (bf16[216,128]{1,0:T(8,128)(2,1)S(1)}, bf16[216,128]{1,0:T(8,128)(2,1)S(1)}, u32[]{:S(2)}, u32[]{:S(2)}) collective-permute-start(bf16[216,128]{1,0:T(8,128)(2,1)S(1)} %pad_maximum_fusion), channel_id=1, source_target_pairs={{0,3},{1,0},{2,1},{3,2},{4,7},{5,4},{6,5},{7,6},{8,11},{9,8},{10,9... | collective-permute-start | bytes 165896 | tf_op jit(solution)/shard_map/ppermute | solution.py:64
  11.0 6.0 %collective-permute-start.3 = (bf16[216,128]{1,0:T(8,128)(2,1)S(1)}, bf16[216,128]{1,0:T(8,128)(2,1)S(1)}, u32[]{:S(2)}, u32[]{:S(2)}) collective-permute-start(bf16[216,128]{1,0:T(8,128)(2,1)S(1)} %pad_maximum_fusion.1), channel_id=1, source_target_pairs={{0,1},{1,2},{2,3},{3,0},{4,5},{5,6},{6,7},{7,4},{8,9},{9,10},{10,1... | collective-permute-start | bytes 165896 | tf_op jit(solution)/shard_map/ppermute | solution.py:64
  11.1 8.6 %copy-start = (bf16[3,32,864]{2,1,0:T(8,128)(2,1)S(1)}, bf16[3,32,864]{2,1,0:T(8,128)(2,1)}, u32[]{:S(2)}) copy-start(bf16[3,32,864]{2,1,0:T(8,128)(2,1)} %weight_ref.1) | copy-start | bytes 497668
  11.1 8.6 %copy-start.1 = (bf16[3,32]{1,0:T(4,128)(2,1)S(1)}, bf16[3,32]{1,0:T(4,128)(2,1)}, u32[]{:S(2)}) copy-start(bf16[3,32]{1,0:T(4,128)(2,1)} %decoder_ref.1) | copy-start | bytes 580
  18.5 3.4 %collective-permute-start.5 = (bf16[384,128]{1,0:T(8,128)(2,1)S(1)}, bf16[384,128]{1,0:T(8,128)(2,1)S(1)}, u32[]{:S(2)}, u32[]{:S(2)}) collective-permute-start(bf16[384,128]{1,0:T(8,128)(2,1)S(1)} %get-tuple-element.39), channel_id=1, source_target_pairs={{0,4},{4,0},{8,12},{12,8},{1,5},{5,1},{9,13},{13,9},{2,6},{6,2},{1... | collective-permute-start | bytes 294920 | tf_op jit(solution)/shard_map/ppermute | solution.py:74
  18.6 4.6 %collective-permute-start.4 = (bf16[384,128]{1,0:T(8,128)(2,1)S(1)}, bf16[384,128]{1,0:T(8,128)(2,1)S(1)}, u32[]{:S(2)}, u32[]{:S(2)}) collective-permute-start(bf16[384,128]{1,0:T(8,128)(2,1)S(1)} %get-tuple-element.40), channel_id=1, source_target_pairs={{0,12},{4,8},{8,4},{12,0},{1,13},{5,9},{9,5},{13,1},{2,14},{6,10},... | collective-permute-start | bytes 294920 | tf_op jit(solution)/shard_map/ppermute | solution.py:75
  23.2 5.8 %collective-permute-start.6 = (bf16[112,128]{1,0:T(8,128)(2,1)S(1)}, bf16[112,128]{1,0:T(8,128)(2,1)S(1)}, u32[]{:S(2)}, u32[]{:S(2)}) collective-permute-start(bf16[112,128]{1,0:T(8,128)(2,1)S(1)} %maximum_bitcast_fusion.high_ref), channel_id=1, source_target_pairs={{0,1},{1,2},{2,3},{3,0},{4,5},{5,6},{6,7},{7,4},{8,9},{9,10},{10,1... | collective-permute-start | bytes 86024 | tf_op jit(solution)/shard_map/ppermute | solution.py:64
  23.3 5.7 %collective-permute-start.7 = (bf16[112,128]{1,0:T(8,128)(2,1)S(1)}, bf16[112,128]{1,0:T(8,128)(2,1)S(1)}, u32[]{:S(2)}, u32[]{:S(2)}) collective-permute-start(bf16[112,128]{1,0:T(8,128)(2,1)S(1)} %maximum_bitcast_fusion.1.low_ref), channel_id=1, source_target_pairs={{0,3},{1,0},{2,1},{3,2},{4,7},{5,4},{6,5},{7,6},{8,11},{9,8},{10,9... | collective-permute-start | bytes 86024 | tf_op jit(solution)/shard_map/ppermute | solution.py:64
  27.1 1.8 %copy-start.2 = (bf16[3,16]{1,0:T(4,128)(2,1)S(1)}, bf16[3,16]{1,0:T(4,128)(2,1)}, u32[]{:S(2)}) copy-start(bf16[3,16]{1,0:T(4,128)(2,1)} %self_ref.1) | copy-start | bytes 292

commit v9 on v7

--- a/solution.py
+++ b/solution.py
@@ -200,47 +200,52 @@
                 band_ref[layer, out_z * chans : (out_z + 1) * chans, lanes : lanes + 128] = tile
 
 
+def unpacked(ref, which, feat_dim, blocks):
+    step = (feat_dim + 2) * blocks
+    block = ref[which * step : (which + 1) * step, :].astype(F32)
+    feats = jnp.concatenate([block[k * feat_dim : (k + 1) * feat_dim] for k in range(blocks)], 1)
+    codes = block[blocks * feat_dim :]
+    pair = [
+        jnp.concatenate([codes[j * blocks + k][None] for k in range(blocks)], 1) for j in range(2)
+    ]
+    return feats.astype(BF), jnp.concatenate(pair, 0).astype(BF)
+
+
+def near_kernel(west_ref, east_ref, part_ref, sum_ref, held_ref):
+    cap = held_ref.shape[1] // 2
+    feat_dim = held_ref.shape[0] - 2
+    for place, ref in enumerate((west_ref, east_ref)):
+        feats, codes = unpacked(ref, 1, feat_dim, cap // 128)
+        at = slice(place * cap, (place + 1) * cap)
+        held_ref[:feat_dim, at] = feats
+        held_ref[feat_dim:, at] = codes
+    rows = held_ref[...]
+    sum_ref[...] = part_ref[...] + scatter_part(
+        rows[:feat_dim], rows[feat_dim : feat_dim + 1], rows[feat_dim + 1 : feat_dim + 2]
+    )
+
+
 def mean_kernel(
-    west_ref, east_ref, down_ref, up_ref, part_ref, mean_ref, first_ref, last_ref, held_ref, total
+    near_ref, down_ref, up_ref, part_ref, mean_ref, first_ref, last_ref, held_ref, total
 ):
     cap = held_ref.shape[1] // 8
     feat_dim = held_ref.shape[0] - 2
-    blocks = cap // 128
-    order = [
-        (down_ref, 0),
-        (west_ref, 1),
-        (up_ref, 0),
-        (down_ref, 1),
-        (up_ref, 1),
-        (down_ref, 2),
-        (east_ref, 1),
-        (up_ref, 2),
-    ]
-    for place, (ref, which) in enumerate(order):
-        step = (feat_dim + 2) * blocks
-        block = ref[which * step : (which + 1) * step, :].astype(F32)
-        feats = jnp.concatenate(
-            [block[k * feat_dim : (k + 1) * feat_dim] for k in range(blocks)], 1
-        )
-        codes = block[blocks * feat_dim :]
-        pair = [
-            jnp.concatenate([codes[j * blocks + k][None] for k in range(blocks)], 1)
-            for j in range(2)
-        ]
+    held_ref[:, cap : 2 * cap] = near_ref[:, :cap]
+    held_ref[:, 6 * cap : 7 * cap] = near_ref[:, cap:]
+    order = ((down_ref, 0, 0), (up_ref, 0, 2), (down_ref, 1, 3))
+    order += ((up_ref, 1, 4), (down_ref, 2, 5), (up_ref, 2, 7))
+    for ref, which, place in order:
+        feats, codes = unpacked(ref, which, feat_dim, cap // 128)
         at = slice(place * cap, (place + 1) * cap)
-        held_ref[:feat_dim, at] = feats.astype(BF)
-        held_ref[feat_dim:, at] = jnp.concatenate(pair, 0).astype(BF)
-    total[...] = part_ref[...]
-    chunk = CHUNK
-
-    def body(step):
-        at = aligned(step * chunk, chunk)
-        rows = held_ref[:, at]
-        total[...] += scatter_part(
+        held_ref[:feat_dim, at] = feats
+        held_ref[feat_dim:, at] = codes
+    for k, (place, count) in enumerate(((0, 1), (2, 2), (4, 2), (7, 1))):
+        rows = held_ref[:, place * cap : (place + count) * cap]
+        part = scatter_part(
             rows[:feat_dim], rows[feat_dim : feat_dim + 1], rows[feat_dim + 1 : feat_dim + 2]
         )
-
-    repeat(held_ref.shape[1] // chunk, body)
+        total[...] = (total[...] if k else part_ref[...]) + part
+
     inverse = 1.0 / jnp.maximum(total[HI * feat_dim :, :], 1.0)
     for pair in range(CX // 2):
         blocks = []
@@ -580,10 +585,19 @@
     up = passed_along(joined(2, 1), "gy", 1)
     wide = Z * chans
     lanes = Z * feat_dim
+    part, near = call(
+        near_kernel,
+        "near",
+        [vmem()] * 3,
+        [((sums, F32), vmem()), (((width, 2 * cap), BF), vmem())],
+        [],
+        1 << 30,
+        8,
+    )(west, east, part)
     mean, first, last, held = call(
         mean_kernel,
         "mean",
-        [vmem()] * 5,
+        [vmem()] * 4,
         [
             (((CX * CY, lanes), BF), vmem()),
             (((HALO * CY, lanes), BF), vmem()),
@@ -593,7 +607,7 @@
         [pltpu.VMEM(sums, F32)],
         3 << 30,
         8,
-    )(west, east, down, up, part)
+    )(near, down, up, part)
     after = passed_along(first, "gx", -1)
     before = passed_along(last, "gx", 1)
 

time: 36.4 us -> 36.1 us (level)
  waiting for transfers between devices: 6.8 us -> 6.29 us
    ppermute x8, waiting for transfers between devices: 6.8 us -> 6.29 us  [passed_along(): lax.ppermute(x, axis, [(i, (i + by) % length) for i in range(length)])]
    pallas_call x1 -> x2, Pallas kernels: 1.52 us -> 1.74 us  [the longest x1 1.24 us: on_device(): call(mean_kernel, 'mean', [vmem()] * 4, [(((CX * CY, lanes), BF), vmem())...]
  transfers between devices with their start and end apart: 8 -> 8, of which waited for: 5 -> 5; matrix products, arithmetic and copies ran while one was open for 1% -> 1% of each run, Pallas kernels for 18% -> 20%
where the time goes in v9:
time: 36.1 us; the launch traced here: 35.9 us
  Pallas kernels  17.3 us (48%)
  starting transfers between devices  11.8 us (33%)
  waiting for transfers between devices  6.29 us (17%)
    ppermute x8, starting transfers between devices, passed_along(): lax.ppermute(x, axis, [(i, (i + by) % length) for i in range(length)])  11.8 us
    pallas_call x1, Pallas kernels, on_device(): call(pick_kernel, 'pick', [vmem()] * 11 + [hbm()] * 2 + [vmem()] * 2, [((...  7.83 us
    ppermute x8, waiting for transfers between devices, passed_along(): lax.ppermute(x, axis, [(i, (i + by) % length) for i in range(length)])  6.29 us
    pallas_call x1, Pallas kernels, on_device(): call(stay_kernel, 'stay', [hbm()] * 2, [((sums, F32), vmem())], [pltpu.VM...  2.92 us
    pallas_call x1, Pallas kernels, on_device(): call(core_kernel, 'core', [vmem()] * 5, [(((3, (CX - 2) * PITCH, wide), B...  2.11 us
    pallas_call x1, Pallas kernels, on_device(): call(outer_kernel, 'outer', [vmem()] * 6, [(((3, 2 * HALO * PITCH, wide),...  1.6 us
    pallas_call x1, Pallas kernels, on_device(): call(mean_kernel, 'mean', [vmem()] * 4, [(((CX * CY, lanes), BF), vmem())...  1.24 us
    pallas_call x1, Pallas kernels, on_device(): call(pack_kernel, 'pack', [hbm()] * 3, [(((3 * width * cap // 128, 128),...  1.07 us
  transfers between devices with their start and end apart: 8, of which 5 were waited for; matrix products, arithmetic and copies ran while one was open for 1% of the time, Pallas kernels for 20%

profile of v9, /device:TPU:0, one launch (start us, length us, event | category | flops | bytes accessed | tf_op | source)
XLA Modules:
  0.0 35.9 jit_solution(11002715042787989973)
XLA Ops:
  0.0 1.1 %pack.1 = (bf16[216,128]{1,0:T(8,128)(2,1)S(1)}, bf16[216,128]{1,0:T(8,128)(2,1)S(1)}, bf16[144,128]{1,0:T(8,128)(2,1)S(1)}) custom-call(bf16[16,8,512]{2,1,0:T(8,128)(2,1)} %bitcast.18, s32[8,512]{1,0:T(8,128)} %bitcast.19, s32[8]{0:T(128)} %bitcast.20), custom_call_target="tpu_custom_call" | custom-call | flops 1048576 | bytes 1048576 | tf_op jit(solution)/shard_map/pack/pallas_call | solution.py:539
  1.1 2.5 %collective-permute-start = (bf16[216,128]{1,0:T(8,128)(2,1)S(1)}, bf16[216,128]{1,0:T(8,128)(2,1)S(1)}, u32[]{:S(2)}, u32[]{:S(2)}) collective-permute-start(bf16[216,128]{1,0:T(8,128)(2,1)S(1)} %get-tuple-element.22), channel_id=1, source_target_pairs={{0,12},{4,0},{8,4},{12,8},{1,13},{5,1},{9,5},{13,9},{2,14},{6,2},{... | collective-permute-start | bytes 165896 | tf_op jit(solution)/shard_map/ppermute | solution.py:64
  3.5 0.0 collective-permute-start.1
  3.5 0.0 copy-start.3
  3.5 0.0 copy-start.4
  3.5 2.9 %stay.1.part_ref = f32[544,256]{1,0:T(8,128)S(1)} custom-call(bf16[16,6144]{1,0:T(8,128)(2,1)} %bitcast.21, s32[1,6144]{1,0:T(1,128)} %bitcast.23), custom_call_target="tpu_custom_call" | custom-call | flops 5368709120 | bytes 1048576 | tf_op jit(solution)/shard_map/stay/pallas_call | solution.py:564
  6.5 0.0 copy-done.3
  6.5 0.1 copy.11.encoder_ref
  6.6 0.0 copy-done.4
  6.6 0.1 tile.10.bias_ref
  6.7 0.0 collective-permute-done.west_ref
  6.7 0.4 %collective-permute-done.1.east_ref = bf16[216,128]{1,0:T(8,128)(2,1)S(1)} collective-permute-done((bf16[216,128]{1,0:T(8,128)(2,1)S(1)}, bf16[216,128]{1,0:T(8,128)(2,1)S(1)}, u32[]{:S(2)}, u32[]{:S(2)}) %collective-permute-start.1) | collective-permute-done | bytes 55328 | tf_op jit(solution)/shard_map/ppermute | solution.py:64
  7.1 3.7 %collective-permute-start.2 = (bf16[216,128]{1,0:T(8,128)(2,1)S(1)}, bf16[216,128]{1,0:T(8,128)(2,1)S(1)}, u32[]{:S(2)}, u32[]{:S(2)}) collective-permute-start(bf16[216,128]{1,0:T(8,128)(2,1)S(1)} %pad_maximum_fusion), channel_id=1, source_target_pairs={{0,3},{1,0},{2,1},{3,2},{4,7},{5,4},{6,5},{7,6},{8,11},{9,8},{10,9... | collective-permute-start | bytes 165896 | tf_op jit(solution)/shard_map/ppermute | solution.py:64
  10.8 0.0 collective-permute-start.3
  10.8 0.5 %near.1 = (f32[544,256]{1,0:T(8,128)S(1)}, bf16[18,1024]{1,0:T(8,128)(2,1)S(1)}) custom-call(bf16[216,128]{1,0:T(8,128)(2,1)S(1)} %collective-permute-done.west_ref, bf16[216,128]{1,0:T(8,128)(2,1)S(1)} %collective-permute-done.1.east_ref, f32[544,256]{1,0:T(8,128)S(1)} %stay.1.part_ref), custom_call_target="tpu_custom_call" | custom-call | flops 1073741824 | bytes 1048576 | tf_op jit(solution)/shard_map/near/pallas_call | solution.py:588
  11.3 1.7 %collective-permute-done.2.down_ref = bf16[216,128]{1,0:T(8,128)(2,1)S(1)} collective-permute-done((bf16[216,128]{1,0:T(8,128)(2,1)S(1)}, bf16[216,128]{1,0:T(8,128)(2,1)S(1)}, u32[]{:S(2)}, u32[]{:S(2)}) %collective-permute-start.2) | collective-permute-done | bytes 55328 | tf_op jit(solution)/shard_map/ppermute | solution.py:64
  13.0 3.7 %collective-permute-done.3.up_ref = bf16[216,128]{1,0:T(8,128)(2,1)S(1)} collective-permute-done((bf16[216,128]{1,0:T(8,128)(2,1)S(1)}, bf16[216,128]{1,0:T(8,128)(2,1)S(1)}, u32[]{:S(2)}, u32[]{:S(2)}) %collective-permute-start.3) | collective-permute-done | bytes 55328 | tf_op jit(solution)/shard_map/ppermute | solution.py:64
  16.8 1.2 %mean.1 = (bf16[1024,128]{1,0:T(8,128)(2,1)S(1)}, bf16[384,128]{1,0:T(8,128)(2,1)S(1)}, bf16[384,128]{1,0:T(8,128)(2,1)S(1)}, bf16[18,4096]{1,0:T(8,128)(2,1)S(1)}) custom-call(bf16[18,1024]{1,0:T(8,128)(2,1)S(1)} %get-tuple-element.27.near_ref, bf16[216,128]{1,0:T(8,128)(2,1)S(1)} %collective-permute-done.2.down_ref, ...), custom_call_target="tpu_custom_call" | custom-call | flops 3221225472 | bytes 1048576 | tf_op jit(solution)/shard_map/mean/pallas_call | solution.py:597
  18.0 0.1 collective-permute-start.4
  18.1 1.7 %collective-permute-start.5 = (bf16[384,128]{1,0:T(8,128)(2,1)S(1)}, bf16[384,128]{1,0:T(8,128)(2,1)S(1)}, u32[]{:S(2)}, u32[]{:S(2)}) collective-permute-start(bf16[384,128]{1,0:T(8,128)(2,1)S(1)} %get-tuple-element.34), channel_id=1, source_target_pairs={{0,12},{4,0},{8,4},{12,8},{1,13},{5,1},{9,5},{13,9},{2,14},{6,2},{... | collective-permute-start | bytes 294920 | tf_op jit(solution)/shard_map/ppermute | solution.py:64
  19.8 0.0 copy-done
  19.8 0.0 copy-done.1
  19.8 2.1 %core.1 = (bf16[3,864,256]{2,1,0:T(8,128)(2,1)S(1)}, bf16[1024,256]{1,0:T(8,128)(2,1)S(1)}, bf16[3,256,2304]{2,1,0:T(8,128)(2,1)S(1)}, bf16[256,128]{1,0:T(8,128)(2,1)S(1)}, bf16[24,256]{1,0:T(8,128)(2,1)S(1)}) custom-call(bf16[1024,128]{1,0:T(8,128)(2,1)S(1)} %get-tuple-element.30.mean_ref, bf16[3,32,864]{2,1,0:T(8,128)(2,1)S(1)} %copy-done, ...), custom_call_target="tpu_custom_call" | custom-call | flops 2147483648 | bytes 1048576 | tf_op jit(solution)/shard_map/core/pallas_call | solution.py:625
  21.9 0.2 collective-permute-done.4.before_ref
  22.1 0.0 collective-permute-done.5.after_ref
  22.1 0.1 collective-permute-start.6
  22.2 3.8 %collective-permute-start.7 = (bf16[112,128]{1,0:T(8,128)(2,1)S(1)}, bf16[112,128]{1,0:T(8,128)(2,1)S(1)}, u32[]{:S(2)}, u32[]{:S(2)}) collective-permute-start(bf16[112,128]{1,0:T(8,128)(2,1)S(1)} %maximum_bitcast_fusion.1.low_ref), channel_id=1, source_target_pairs={{0,3},{1,0},{2,1},{3,2},{4,7},{5,4},{6,5},{7,6},{8,11},{9,8},{10,9... | collective-permute-start | bytes 86024 | tf_op jit(solution)/shard_map/ppermute | solution.py:64
  26.0 1.6 %outer.1.outer_ref = bf16[3,864,256]{2,1,0:T(8,128)(2,1)S(1)} custom-call(bf16[1024,256]{1,0:T(8,128)(2,1)S(1)} %get-tuple-element.32.own_ref, bf16[384,128]{1,0:T(8,128)(2,1)S(1)} %collective-permute-done.4.before_ref, bf16[384,128]{1,0:T(8,128)(2,1)S(1)} %collective-permute-done.5.after_ref, bf16[3,256,2304]{2,1,0:T(8,128)(2,1)S(1)} %get-tuple-element.35.band_ref, ...), custom_call_target="tpu_custom_call" | custom-call | flops 2147483648 | bytes 1048576 | tf_op jit(solution)/shard_map/outer/pallas_call | solution.py:640
  27.6 0.2 collective-permute-done.6.below_ref
  27.9 0.0 collective-permute-done.7.above_ref
  27.9 0.0 copy-done.2
  27.9 7.8 %pick.1 = f32[3,1,10240]{2,1,0:T(1,128)} custom-call(bf16[3,864,256]{2,1,0:T(8,128)(2,1)S(1)} %get-tuple-element.31.middle_ref, bf16[3,864,256]{2,1,0:T(8,128)(2,1)S(1)} %outer.1.outer_ref, bf16[1024,256]{1,0:T(8,128)(2,1)S(1)} %get-tuple-element.32.own_ref, bf16[112,128]{1,0:T(8,128)(2,1)S(1)} %collective-permute-done.6.below_ref, ...), custom_call_target="tpu_custom_call" | custom-call | flops 8589934592 | bytes 1048576 | tf_op jit(solution)/shard_map/pick/pallas_call | solution.py:649
  (13 shorter events, 0.1 us)
Async XLA Ops:
  1.1 5.6 %collective-permute-start = (bf16[216,128]{1,0:T(8,128)(2,1)S(1)}, bf16[216,128]{1,0:T(8,128)(2,1)S(1)}, u32[]{:S(2)}, u32[]{:S(2)}) collective-permute-start(bf16[216,128]{1,0:T(8,128)(2,1)S(1)} %get-tuple-element.22), channel_id=1, source_target_pairs={{0,12},{4,0},{8,4},{12,8},{1,13},{5,1},{9,5},{13,9},{2,14},{6,2},{... | collective-permute-start | bytes 165896 | tf_op jit(solution)/shard_map/ppermute | solution.py:64
  3.5 3.6 %collective-permute-start.1 = (bf16[216,128]{1,0:T(8,128)(2,1)S(1)}, bf16[216,128]{1,0:T(8,128)(2,1)S(1)}, u32[]{:S(2)}, u32[]{:S(2)}) collective-permute-start(bf16[216,128]{1,0:T(8,128)(2,1)S(1)} %get-tuple-element.23), channel_id=1, source_target_pairs={{0,4},{4,8},{8,12},{12,0},{1,5},{5,9},{9,13},{13,1},{2,6},{6,10},{... | collective-permute-start | bytes 165896 | tf_op jit(solution)/shard_map/ppermute | solution.py:64
  3.5 3.0 %copy-start.3 = (bf16[32,16]{0,1:T(8,128)(2,1)S(1)}, bf16[32,16]{0,1:T(8,128)(2,1)}, u32[]{:S(2)}) copy-start(bf16[32,16]{0,1:T(8,128)(2,1)} %param.15) | copy-start | bytes 3076
  3.5 3.0 %copy-start.4 = (f32[3,32]{1,0:T(4,128)S(1)}, f32[3,32]{1,0:T(4,128)}, u32[]{:S(2)}) copy-start(f32[3,32]{1,0:T(4,128)} %param.17) | copy-start | bytes 1156
  7.1 5.9 %collective-permute-start.2 = (bf16[216,128]{1,0:T(8,128)(2,1)S(1)}, bf16[216,128]{1,0:T(8,128)(2,1)S(1)}, u32[]{:S(2)}, u32[]{:S(2)}) collective-permute-start(bf16[216,128]{1,0:T(8,128)(2,1)S(1)} %pad_maximum_fusion), channel_id=1, source_target_pairs={{0,3},{1,0},{2,1},{3,2},{4,7},{5,4},{6,5},{7,6},{8,11},{9,8},{10,9... | collective-permute-start | bytes 165896 | tf_op jit(solution)/shard_map/ppermute | solution.py:64
  10.8 6.0 %collective-permute-start.3 = (bf16[216,128]{1,0:T(8,128)(2,1)S(1)}, bf16[216,128]{1,0:T(8,128)(2,1)S(1)}, u32[]{:S(2)}, u32[]{:S(2)}) collective-permute-start(bf16[216,128]{1,0:T(8,128)(2,1)S(1)} %pad_maximum_fusion.1), channel_id=1, source_target_pairs={{0,1},{1,2},{2,3},{3,0},{4,5},{5,6},{6,7},{7,4},{8,9},{9,10},{10,1... | collective-permute-start | bytes 165896 | tf_op jit(solution)/shard_map/ppermute | solution.py:64
  16.7 3.1 %copy-start = (bf16[3,32,864]{2,1,0:T(8,128)(2,1)S(1)}, bf16[3,32,864]{2,1,0:T(8,128)(2,1)}, u32[]{:S(2)}) copy-start(bf16[3,32,864]{2,1,0:T(8,128)(2,1)} %weight_ref.1) | copy-start | bytes 497668
  16.7 3.1 %copy-start.1 = (bf16[3,32]{1,0:T(4,128)(2,1)S(1)}, bf16[3,32]{1,0:T(4,128)(2,1)}, u32[]{:S(2)}) copy-start(bf16[3,32]{1,0:T(4,128)(2,1)} %decoder_ref.1) | copy-start | bytes 580
  18.0 4.1 %collective-permute-start.4 = (bf16[384,128]{1,0:T(8,128)(2,1)S(1)}, bf16[384,128]{1,0:T(8,128)(2,1)S(1)}, u32[]{:S(2)}, u32[]{:S(2)}) collective-permute-start(bf16[384,128]{1,0:T(8,128)(2,1)S(1)} %get-tuple-element.33), channel_id=1, source_target_pairs={{0,4},{4,8},{8,12},{12,0},{1,5},{5,9},{9,13},{13,1},{2,6},{6,10},{... | collective-permute-start | bytes 294920 | tf_op jit(solution)/shard_map/ppermute | solution.py:64
  18.1 4.0 %collective-permute-start.5 = (bf16[384,128]{1,0:T(8,128)(2,1)S(1)}, bf16[384,128]{1,0:T(8,128)(2,1)S(1)}, u32[]{:S(2)}, u32[]{:S(2)}) collective-permute-start(bf16[384,128]{1,0:T(8,128)(2,1)S(1)} %get-tuple-element.34), channel_id=1, source_target_pairs={{0,12},{4,0},{8,4},{12,8},{1,13},{5,1},{9,5},{13,9},{2,14},{6,2},{... | collective-permute-start | bytes 294920 | tf_op jit(solution)/shard_map/ppermute | solution.py:64
  22.1 5.7 %collective-permute-start.6 = (bf16[112,128]{1,0:T(8,128)(2,1)S(1)}, bf16[112,128]{1,0:T(8,128)(2,1)S(1)}, u32[]{:S(2)}, u32[]{:S(2)}) collective-permute-start(bf16[112,128]{1,0:T(8,128)(2,1)S(1)} %maximum_bitcast_fusion.high_ref), channel_id=1, source_target_pairs={{0,1},{1,2},{2,3},{3,0},{4,5},{5,6},{6,7},{7,4},{8,9},{9,10},{10,1... | collective-permute-start | bytes 86024 | tf_op jit(solution)/shard_map/ppermute | solution.py:64
  22.2 5.7 %collective-permute-start.7 = (bf16[112,128]{1,0:T(8,128)(2,1)S(1)}, bf16[112,128]{1,0:T(8,128)(2,1)S(1)}, u32[]{:S(2)}, u32[]{:S(2)}) collective-permute-start(bf16[112,128]{1,0:T(8,128)(2,1)S(1)} %maximum_bitcast_fusion.1.low_ref), channel_id=1, source_target_pairs={{0,3},{1,0},{2,1},{3,2},{4,7},{5,4},{6,5},{7,6},{8,11},{9,8},{10,9... | collective-permute-start | bytes 86024 | tf_op jit(solution)/shard_map/ppermute | solution.py:64
  26.0 1.9 %copy-start.2 = (bf16[3,16]{1,0:T(4,128)(2,1)S(1)}, bf16[3,16]{1,0:T(4,128)(2,1)}, u32[]{:S(2)}) copy-start(bf16[3,16]{1,0:T(4,128)(2,1)} %self_ref.1) | copy-start | bytes 292

commit v10 on v9

--- a/solution.py
+++ b/solution.py
@@ -108,7 +108,7 @@
 
 
 def pack_kernel(
-    feat_in, slot_in, count_in, west_ref, east_ref, middle_ref, feat_ref, slot_ref, count_ref, sems
+    feat_in, slot_in, count_in, down_ref, up_ref, middle_ref, feat_ref, slot_ref, count_ref, sems
 ):
     pairs = ((count_in, count_ref), (slot_in, slot_ref), (feat_in, feat_ref))
     copies = [pltpu.make_async_copy(a, b, sems.at[k]) for k, (a, b) in enumerate(pairs)]
@@ -124,12 +124,12 @@
     low = low.astype(F32)
     blocks = cap // 128
     step = (feat_dim + 2) * blocks
-    for out_ref, start, end in ((west_ref, 0, 3), (middle_ref, 3, 5), (east_ref, 5, buckets)):
-        for bucket in range(start, end):
+    for out_ref, chosen in ((down_ref, (0, 3, 5)), (up_ref, (2, 4, 7)), (middle_ref, (1, 6))):
+        for place, bucket in enumerate(chosen):
             code = jnp.where(
                 lane < count_ref[bucket], high[bucket : bucket + 1], jnp.full((1, cap), DEAD, F32)
             )
-            base = (bucket - start) * step
+            base = place * step
             pieces = []
             for value in (turned[bucket], code, low[bucket : bucket + 1]):
                 pieces += [value[:, k * 128 : (k + 1) * 128] for k in range(blocks)]
@@ -211,10 +211,10 @@
     return feats.astype(BF), jnp.concatenate(pair, 0).astype(BF)
 
 
-def near_kernel(west_ref, east_ref, part_ref, sum_ref, held_ref):
+def near_kernel(down_ref, up_ref, part_ref, sum_ref, held_ref):
     cap = held_ref.shape[1] // 2
     feat_dim = held_ref.shape[0] - 2
-    for place, ref in enumerate((west_ref, east_ref)):
+    for place, ref in enumerate((down_ref, up_ref)):
         feats, codes = unpacked(ref, 1, feat_dim, cap // 128)
         at = slice(place * cap, (place + 1) * cap)
         held_ref[:feat_dim, at] = feats
@@ -226,20 +226,18 @@
 
 
 def mean_kernel(
-    near_ref, down_ref, up_ref, part_ref, mean_ref, first_ref, last_ref, held_ref, total
+    near_ref, west_ref, east_ref, part_ref, mean_ref, first_ref, last_ref, held_ref, total
 ):
     cap = held_ref.shape[1] // 8
     feat_dim = held_ref.shape[0] - 2
-    held_ref[:, cap : 2 * cap] = near_ref[:, :cap]
-    held_ref[:, 6 * cap : 7 * cap] = near_ref[:, cap:]
-    order = ((down_ref, 0, 0), (up_ref, 0, 2), (down_ref, 1, 3))
-    order += ((up_ref, 1, 4), (down_ref, 2, 5), (up_ref, 2, 7))
+    held_ref[:, 3 * cap : 5 * cap] = near_ref[...]
+    order = [(west_ref, k, k) for k in range(3)] + [(east_ref, k, 5 + k) for k in range(3)]
     for ref, which, place in order:
         feats, codes = unpacked(ref, which, feat_dim, cap // 128)
         at = slice(place * cap, (place + 1) * cap)
         held_ref[:feat_dim, at] = feats
         held_ref[feat_dim:, at] = codes
-    for k, (place, count) in enumerate(((0, 1), (2, 2), (4, 2), (7, 1))):
+    for k, (place, count) in enumerate(((0, 2), (2, 1), (5, 1), (6, 2))):
         rows = held_ref[:, place * cap : (place + count) * cap]
         part = scatter_part(
             rows[:feat_dim], rows[feat_dim : feat_dim + 1], rows[feat_dim + 1 : feat_dim + 2]
@@ -536,7 +534,7 @@
     own_slots = stay_slots.reshape(1, stay)
 
     width = feat_dim + 2
-    west, east, middle = call(
+    down, up, middle = call(
         pack_kernel,
         "pack",
         [hbm()] * 3,
@@ -558,8 +556,8 @@
         in_hbm(move_slots.reshape(8, cap)),
         in_hbm(move_counts.reshape(8)),
     )
-    west = passed_along(west, "gx", -1)
-    east = passed_along(east, "gx", 1)
+    down = passed_along(down, "gy", -1)
+    up = passed_along(up, "gy", 1)
     sums = (HI * (feat_dim + 1), LO)
     (part,) = call(
         stay_kernel,
@@ -574,15 +572,15 @@
         5 << 30,
         8,
     )(in_hbm(own_feats), in_hbm(own_slots))
-    west, east, part = lax.optimization_barrier((west, east, part))
+    down, up, part = lax.optimization_barrier((down, up, part))
     step = width * cap // 128
 
     def joined(place, inner):
-        pieces = ((west, place), (middle, inner), (east, place))
+        pieces = ((down, place), (middle, inner), (up, place))
         return jnp.concatenate([ref[k * step : (k + 1) * step] for ref, k in pieces], 0)
 
-    down = passed_along(joined(0, 0), "gy", -1)
-    up = passed_along(joined(2, 1), "gy", 1)
+    west = passed_along(joined(0, 0), "gx", -1)
+    east = passed_along(joined(2, 1), "gx", 1)
     wide = Z * chans
     lanes = Z * feat_dim
     part, near = call(
@@ -593,7 +591,7 @@
         [],
         1 << 30,
         8,
-    )(west, east, part)
+    )(down, up, part)
     mean, first, last, held = call(
         mean_kernel,
         "mean",
@@ -607,7 +605,7 @@
         [pltpu.VMEM(sums, F32)],
         3 << 30,
         8,
-    )(near, down, up, part)
+    )(near, west, east, part)
     after = passed_along(first, "gx", -1)
     before = passed_along(last, "gx", 1)
 

time: 36.1 us -> 35.9 us (level)
  starting transfers between devices: 11.8 us -> 11.3 us
  waiting for transfers between devices: 6.29 us -> 6.7 us
    ppermute x8, starting transfers between devices: 11.8 us -> 11.3 us  [passed_along(): lax.ppermute(x, axis, [(i, (i + by) % length) for i in range(length)])]
    ppermute x8, waiting for transfers between devices: 6.29 us -> 6.7 us  [passed_along(): lax.ppermute(x, axis, [(i, (i + by) % length) for i in range(length)])]
where the time goes in v10:
time: 35.9 us; the launch traced here: 35.8 us
  Pallas kernels  17.2 us (48%)
  starting transfers between devices  11.3 us (31%)
  waiting for transfers between devices  6.7 us (19%)
    ppermute x8, starting transfers between devices, passed_along(): lax.ppermute(x, axis, [(i, (i + by) % length) for i in range(length)])  11.3 us
    pallas_call x1, Pallas kernels, on_device(): call(pick_kernel, 'pick', [vmem()] * 11 + [hbm()] * 2 + [vmem()] * 2, [((...  7.83 us
    ppermute x8, waiting for transfers between devices, passed_along(): lax.ppermute(x, axis, [(i, (i + by) % length) for i in range(length)])  6.7 us
    pallas_call x1, Pallas kernels, on_device(): call(stay_kernel, 'stay', [hbm()] * 2, [((sums, F32), vmem())], [pltpu.VM...  2.92 us
    pallas_call x1, Pallas kernels, on_device(): call(core_kernel, 'core', [vmem()] * 5, [(((3, (CX - 2) * PITCH, wide), B...  2.11 us
    pallas_call x1, Pallas kernels, on_device(): call(outer_kernel, 'outer', [vmem()] * 6, [(((3, 2 * HALO * PITCH, wide),...  1.58 us
    pallas_call x1, Pallas kernels, on_device(): call(mean_kernel, 'mean', [vmem()] * 4, [(((CX * CY, lanes), BF), vmem())...  1.23 us
    pallas_call x1, Pallas kernels, on_device(): call(pack_kernel, 'pack', [hbm()] * 3, [(((3 * width * cap // 128, 128),...  1.06 us
  transfers between devices with their start and end apart: 8, of which 5 were waited for; matrix products, arithmetic and copies ran while one was open for 1% of the time, Pallas kernels for 20%

profile of v10, /device:TPU:0, one launch (start us, length us, event | category | flops | bytes accessed | tf_op | source)
XLA Modules:
  0.0 35.8 jit_solution(17061836792350260652)
XLA Ops:
  0.0 1.1 %pack.1 = (bf16[216,128]{1,0:T(8,128)(2,1)S(1)}, bf16[216,128]{1,0:T(8,128)(2,1)S(1)}, bf16[144,128]{1,0:T(8,128)(2,1)S(1)}) custom-call(bf16[16,8,512]{2,1,0:T(8,128)(2,1)} %bitcast.18, s32[8,512]{1,0:T(8,128)} %bitcast.19, s32[8]{0:T(128)} %bitcast.20), custom_call_target="tpu_custom_call" | custom-call | flops 1048576 | bytes 1048576 | tf_op jit(solution)/shard_map/pack/pallas_call | solution.py:537
  1.1 5.1 %collective-permute-start = (bf16[216,128]{1,0:T(8,128)(2,1)S(1)}, bf16[216,128]{1,0:T(8,128)(2,1)S(1)}, u32[]{:S(2)}, u32[]{:S(2)}) collective-permute-start(bf16[216,128]{1,0:T(8,128)(2,1)S(1)} %get-tuple-element.22), channel_id=1, source_target_pairs={{0,3},{1,0},{2,1},{3,2},{4,7},{5,4},{6,5},{7,6},{8,11},{9,8},{10,9... | collective-permute-start | bytes 165896 | tf_op jit(solution)/shard_map/ppermute | solution.py:64
  6.2 0.0 collective-permute-start.1
  6.2 0.0 copy-start.3
  6.2 0.0 copy-start.4
  6.2 2.9 %stay.1.part_ref = f32[544,256]{1,0:T(8,128)S(1)} custom-call(bf16[16,6144]{1,0:T(8,128)(2,1)} %bitcast.21, s32[1,6144]{1,0:T(1,128)} %bitcast.23), custom_call_target="tpu_custom_call" | custom-call | flops 5368709120 | bytes 1048576 | tf_op jit(solution)/shard_map/stay/pallas_call | solution.py:562
  9.1 0.0 copy-done.3
  9.1 0.1 copy.11.encoder_ref
  9.2 0.0 copy-done.4
  9.2 0.1 tile.10.bias_ref
  9.3 0.0 collective-permute-done.down_ref
  9.3 2.8 %collective-permute-done.1.up_ref = bf16[216,128]{1,0:T(8,128)(2,1)S(1)} collective-permute-done((bf16[216,128]{1,0:T(8,128)(2,1)S(1)}, bf16[216,128]{1,0:T(8,128)(2,1)S(1)}, u32[]{:S(2)}, u32[]{:S(2)}) %collective-permute-start.1) | collective-permute-done | bytes 55328 | tf_op jit(solution)/shard_map/ppermute | solution.py:64
  12.1 0.1 collective-permute-start.2
  12.2 0.5 %collective-permute-start.3 = (bf16[216,128]{1,0:T(8,128)(2,1)S(1)}, bf16[216,128]{1,0:T(8,128)(2,1)S(1)}, u32[]{:S(2)}, u32[]{:S(2)}) collective-permute-start(bf16[216,128]{1,0:T(8,128)(2,1)S(1)} %pad_maximum_fusion.1), channel_id=1, source_target_pairs={{0,4},{4,8},{8,12},{12,0},{1,5},{5,9},{9,13},{13,1},{2,6},{6,10},{... | collective-permute-start | bytes 165896 | tf_op jit(solution)/shard_map/ppermute | solution.py:64
  12.7 0.5 %near.1 = (f32[544,256]{1,0:T(8,128)S(1)}, bf16[18,1024]{1,0:T(8,128)(2,1)S(1)}) custom-call(bf16[216,128]{1,0:T(8,128)(2,1)S(1)} %collective-permute-done.down_ref, bf16[216,128]{1,0:T(8,128)(2,1)S(1)} %collective-permute-done.1.up_ref, f32[544,256]{1,0:T(8,128)S(1)} %stay.1.part_ref), custom_call_target="tpu_custom_call" | custom-call | flops 1073741824 | bytes 1048576 | tf_op jit(solution)/shard_map/near/pallas_call | solution.py:586
  13.2 0.8 %collective-permute-done.2.west_ref = bf16[216,128]{1,0:T(8,128)(2,1)S(1)} collective-permute-done((bf16[216,128]{1,0:T(8,128)(2,1)S(1)}, bf16[216,128]{1,0:T(8,128)(2,1)S(1)}, u32[]{:S(2)}, u32[]{:S(2)}) %collective-permute-start.2) | collective-permute-done | bytes 55328 | tf_op jit(solution)/shard_map/ppermute | solution.py:64
  14.0 2.4 %collective-permute-done.3.east_ref = bf16[216,128]{1,0:T(8,128)(2,1)S(1)} collective-permute-done((bf16[216,128]{1,0:T(8,128)(2,1)S(1)}, bf16[216,128]{1,0:T(8,128)(2,1)S(1)}, u32[]{:S(2)}, u32[]{:S(2)}) %collective-permute-start.3) | collective-permute-done | bytes 55328 | tf_op jit(solution)/shard_map/ppermute | solution.py:64
  16.4 1.2 %mean.1 = (bf16[1024,128]{1,0:T(8,128)(2,1)S(1)}, bf16[384,128]{1,0:T(8,128)(2,1)S(1)}, bf16[384,128]{1,0:T(8,128)(2,1)S(1)}, bf16[18,4096]{1,0:T(8,128)(2,1)S(1)}) custom-call(bf16[18,1024]{1,0:T(8,128)(2,1)S(1)} %get-tuple-element.27.near_ref, bf16[216,128]{1,0:T(8,128)(2,1)S(1)} %collective-permute-done.2.west_ref, ...), custom_call_target="tpu_custom_call" | custom-call | flops 3221225472 | bytes 1048576 | tf_op jit(solution)/shard_map/mean/pallas_call | solution.py:595
  17.7 0.2 collective-permute-start.4
  17.9 1.6 %collective-permute-start.5 = (bf16[384,128]{1,0:T(8,128)(2,1)S(1)}, bf16[384,128]{1,0:T(8,128)(2,1)S(1)}, u32[]{:S(2)}, u32[]{:S(2)}) collective-permute-start(bf16[384,128]{1,0:T(8,128)(2,1)S(1)} %get-tuple-element.34), channel_id=1, source_target_pairs={{0,12},{4,0},{8,4},{12,8},{1,13},{5,1},{9,5},{13,9},{2,14},{6,2},{... | collective-permute-start | bytes 294920 | tf_op jit(solution)/shard_map/ppermute | solution.py:64
  19.5 0.0 copy-done
  19.5 0.0 copy-done.1
  19.5 2.1 %core.1 = (bf16[3,864,256]{2,1,0:T(8,128)(2,1)S(1)}, bf16[1024,256]{1,0:T(8,128)(2,1)S(1)}, bf16[3,256,2304]{2,1,0:T(8,128)(2,1)S(1)}, bf16[256,128]{1,0:T(8,128)(2,1)S(1)}, bf16[24,256]{1,0:T(8,128)(2,1)S(1)}) custom-call(bf16[1024,128]{1,0:T(8,128)(2,1)S(1)} %get-tuple-element.30.mean_ref, bf16[3,32,864]{2,1,0:T(8,128)(2,1)S(1)} %copy-done, ...), custom_call_target="tpu_custom_call" | custom-call | flops 2147483648 | bytes 1048576 | tf_op jit(solution)/shard_map/core/pallas_call | solution.py:623
  21.6 0.2 collective-permute-done.4.before_ref
  21.8 0.0 collective-permute-done.5.after_ref
  21.8 0.1 collective-permute-start.6
  21.9 3.8 %collective-permute-start.7 = (bf16[112,128]{1,0:T(8,128)(2,1)S(1)}, bf16[112,128]{1,0:T(8,128)(2,1)S(1)}, u32[]{:S(2)}, u32[]{:S(2)}) collective-permute-start(bf16[112,128]{1,0:T(8,128)(2,1)S(1)} %maximum_bitcast_fusion.1.low_ref), channel_id=1, source_target_pairs={{0,3},{1,0},{2,1},{3,2},{4,7},{5,4},{6,5},{7,6},{8,11},{9,8},{10,9... | collective-permute-start | bytes 86024 | tf_op jit(solution)/shard_map/ppermute | solution.py:64
  25.7 1.6 %outer.1.outer_ref = bf16[3,864,256]{2,1,0:T(8,128)(2,1)S(1)} custom-call(bf16[1024,256]{1,0:T(8,128)(2,1)S(1)} %get-tuple-element.32.own_ref, bf16[384,128]{1,0:T(8,128)(2,1)S(1)} %collective-permute-done.4.before_ref, bf16[384,128]{1,0:T(8,128)(2,1)S(1)} %collective-permute-done.5.after_ref, bf16[3,256,2304]{2,1,0:T(8,128)(2,1)S(1)} %get-tuple-element.35.band_ref, ...), custom_call_target="tpu_custom_call" | custom-call | flops 2147483648 | bytes 1048576 | tf_op jit(solution)/shard_map/outer/pallas_call | solution.py:638
  27.3 0.5 %collective-permute-done.6.below_ref = bf16[112,128]{1,0:T(8,128)(2,1)S(1)} collective-permute-done((bf16[112,128]{1,0:T(8,128)(2,1)S(1)}, bf16[112,128]{1,0:T(8,128)(2,1)S(1)}, u32[]{:S(2)}, u32[]{:S(2)}) %collective-permute-start.6) | collective-permute-done | bytes 28704 | tf_op jit(solution)/shard_map/ppermute | solution.py:64
  27.8 0.0 collective-permute-done.7.above_ref
  27.8 0.0 copy-done.2
  27.8 7.8 %pick.1 = f32[3,1,10240]{2,1,0:T(1,128)} custom-call(bf16[3,864,256]{2,1,0:T(8,128)(2,1)S(1)} %get-tuple-element.31.middle_ref, bf16[3,864,256]{2,1,0:T(8,128)(2,1)S(1)} %outer.1.outer_ref, bf16[1024,256]{1,0:T(8,128)(2,1)S(1)} %get-tuple-element.32.own_ref, bf16[112,128]{1,0:T(8,128)(2,1)S(1)} %collective-permute-done.6.below_ref, ...), custom_call_target="tpu_custom_call" | custom-call | flops 8589934592 | bytes 1048576 | tf_op jit(solution)/shard_map/pick/pallas_call | solution.py:647
  (13 shorter events, 0.1 us)
Async XLA Ops:
  1.1 8.2 %collective-permute-start = (bf16[216,128]{1,0:T(8,128)(2,1)S(1)}, bf16[216,128]{1,0:T(8,128)(2,1)S(1)}, u32[]{:S(2)}, u32[]{:S(2)}) collective-permute-start(bf16[216,128]{1,0:T(8,128)(2,1)S(1)} %get-tuple-element.22), channel_id=1, source_target_pairs={{0,3},{1,0},{2,1},{3,2},{4,7},{5,4},{6,5},{7,6},{8,11},{9,8},{10,9... | collective-permute-start | bytes 165896 | tf_op jit(solution)/shard_map/ppermute | solution.py:64
  6.2 6.0 %collective-permute-start.1 = (bf16[216,128]{1,0:T(8,128)(2,1)S(1)}, bf16[216,128]{1,0:T(8,128)(2,1)S(1)}, u32[]{:S(2)}, u32[]{:S(2)}) collective-permute-start(bf16[216,128]{1,0:T(8,128)(2,1)S(1)} %get-tuple-element.23), channel_id=1, source_target_pairs={{0,1},{1,2},{2,3},{3,0},{4,5},{5,6},{6,7},{7,4},{8,9},{9,10},{10,1... | collective-permute-start | bytes 165896 | tf_op jit(solution)/shard_map/ppermute | solution.py:64
  6.2 3.0 %copy-start.3 = (bf16[32,16]{0,1:T(8,128)(2,1)S(1)}, bf16[32,16]{0,1:T(8,128)(2,1)}, u32[]{:S(2)}) copy-start(bf16[32,16]{0,1:T(8,128)(2,1)} %param.15) | copy-start | bytes 3076
  6.2 3.0 %copy-start.4 = (f32[3,32]{1,0:T(4,128)S(1)}, f32[3,32]{1,0:T(4,128)}, u32[]{:S(2)}) copy-start(f32[3,32]{1,0:T(4,128)} %param.17) | copy-start | bytes 1156
  12.1 1.9 %collective-permute-start.2 = (bf16[216,128]{1,0:T(8,128)(2,1)S(1)}, bf16[216,128]{1,0:T(8,128)(2,1)S(1)}, u32[]{:S(2)}, u32[]{:S(2)}) collective-permute-start(bf16[216,128]{1,0:T(8,128)(2,1)S(1)} %pad_maximum_fusion), channel_id=1, source_target_pairs={{0,12},{4,0},{8,4},{12,8},{1,13},{5,1},{9,5},{13,9},{2,14},{6,2},{... | collective-permute-start | bytes 165896 | tf_op jit(solution)/shard_map/ppermute | solution.py:64
  12.2 4.2 %collective-permute-start.3 = (bf16[216,128]{1,0:T(8,128)(2,1)S(1)}, bf16[216,128]{1,0:T(8,128)(2,1)S(1)}, u32[]{:S(2)}, u32[]{:S(2)}) collective-permute-start(bf16[216,128]{1,0:T(8,128)(2,1)S(1)} %pad_maximum_fusion.1), channel_id=1, source_target_pairs={{0,4},{4,8},{8,12},{12,0},{1,5},{5,9},{9,13},{13,1},{2,6},{6,10},{... | collective-permute-start | bytes 165896 | tf_op jit(solution)/shard_map/ppermute | solution.py:64
  16.4 3.1 %copy-start = (bf16[3,32,864]{2,1,0:T(8,128)(2,1)S(1)}, bf16[3,32,864]{2,1,0:T(8,128)(2,1)}, u32[]{:S(2)}) copy-start(bf16[3,32,864]{2,1,0:T(8,128)(2,1)} %weight_ref.1) | copy-start | bytes 497668
  16.4 3.1 %copy-start.1 = (bf16[3,32]{1,0:T(4,128)(2,1)S(1)}, bf16[3,32]{1,0:T(4,128)(2,1)}, u32[]{:S(2)}) copy-start(bf16[3,32]{1,0:T(4,128)(2,1)} %decoder_ref.1) | copy-start | bytes 580
  17.7 4.1 %collective-permute-start.4 = (bf16[384,128]{1,0:T(8,128)(2,1)S(1)}, bf16[384,128]{1,0:T(8,128)(2,1)S(1)}, u32[]{:S(2)}, u32[]{:S(2)}) collective-permute-start(bf16[384,128]{1,0:T(8,128)(2,1)S(1)} %get-tuple-element.33), channel_id=1, source_target_pairs={{0,4},{4,8},{8,12},{12,0},{1,5},{5,9},{9,13},{13,1},{2,6},{6,10},{... | collective-permute-start | bytes 294920 | tf_op jit(solution)/shard_map/ppermute | solution.py:64
  17.9 3.9 %collective-permute-start.5 = (bf16[384,128]{1,0:T(8,128)(2,1)S(1)}, bf16[384,128]{1,0:T(8,128)(2,1)S(1)}, u32[]{:S(2)}, u32[]{:S(2)}) collective-permute-start(bf16[384,128]{1,0:T(8,128)(2,1)S(1)} %get-tuple-element.34), channel_id=1, source_target_pairs={{0,12},{4,0},{8,4},{12,8},{1,13},{5,1},{9,5},{13,9},{2,14},{6,2},{... | collective-permute-start | bytes 294920 | tf_op jit(solution)/shard_map/ppermute | solution.py:64
  21.8 6.0 %collective-permute-start.6 = (bf16[112,128]{1,0:T(8,128)(2,1)S(1)}, bf16[112,128]{1,0:T(8,128)(2,1)S(1)}, u32[]{:S(2)}, u32[]{:S(2)}) collective-permute-start(bf16[112,128]{1,0:T(8,128)(2,1)S(1)} %maximum_bitcast_fusion.high_ref), channel_id=1, source_target_pairs={{0,1},{1,2},{2,3},{3,0},{4,5},{5,6},{6,7},{7,4},{8,9},{9,10},{10,1... | collective-permute-start | bytes 86024 | tf_op jit(solution)/shard_map/ppermute | solution.py:64
  21.9 5.9 %collective-permute-start.7 = (bf16[112,128]{1,0:T(8,128)(2,1)S(1)}, bf16[112,128]{1,0:T(8,128)(2,1)S(1)}, u32[]{:S(2)}, u32[]{:S(2)}) collective-permute-start(bf16[112,128]{1,0:T(8,128)(2,1)S(1)} %maximum_bitcast_fusion.1.low_ref), channel_id=1, source_target_pairs={{0,3},{1,0},{2,1},{3,2},{4,7},{5,4},{6,5},{7,6},{8,11},{9,8},{10,9... | collective-permute-start | bytes 86024 | tf_op jit(solution)/shard_map/ppermute | solution.py:64
  25.7 2.1 %copy-start.2 = (bf16[3,16]{1,0:T(4,128)(2,1)S(1)}, bf16[3,16]{1,0:T(4,128)(2,1)}, u32[]{:S(2)}) copy-start(bf16[3,16]{1,0:T(4,128)(2,1)} %self_ref.1) | copy-start | bytes 292

commit v11 on v10

--- a/solution.py
+++ b/solution.py
@@ -62,6 +62,18 @@
 def passed_along(x, axis, by):
     length = lax.axis_size(axis)
     return lax.ppermute(x, axis, [(i, (i + by) % length) for i in range(length)])
+
+
+def exchanged(up, down, axis):
+    length = lax.axis_size(axis)
+    if length % 2:
+        return passed_along(down, axis, -1), passed_along(up, axis, 1)
+    even = lax.axis_index(axis) % 2 == 0
+    within = [(i, i + 1 - 2 * (i % 2)) for i in range(length)]
+    between = [(i, (i - 1 + 2 * (i % 2)) % length) for i in range(length)]
+    inner = lax.ppermute(jnp.where(even, up, down), axis, within)
+    outer = lax.ppermute(jnp.where(even, down, up), axis, between)
+    return jnp.where(even, inner, outer), jnp.where(even, outer, inner)
 
 
 def dot(a, b, dims=NN):
@@ -579,8 +591,7 @@
         pieces = ((down, place), (middle, inner), (up, place))
         return jnp.concatenate([ref[k * step : (k + 1) * step] for ref, k in pieces], 0)
 
-    west = passed_along(joined(0, 0), "gx", -1)
-    east = passed_along(joined(2, 1), "gx", 1)
+    west, east = exchanged(joined(2, 1), joined(0, 0), "gx")
     wide = Z * chans
     lanes = Z * feat_dim
     part, near = call(

time: 35.9 us -> 35.8 us (level)
  waiting for transfers between devices: 6.7 us -> 5.33 us
  starting transfers between devices: 11.3 us -> 12.5 us
    ppermute x8 -> x6, waiting for transfers between devices: 6.7 us -> 3.38 us  [passed_along(): lax.ppermute(x, axis, [(i, (i + by) % length) for i in range(length)])]
    ppermute x0 -> x2, waiting for transfers between devices: none -> 1.95 us  [the longest x1 1.95 us: exchanged(): outer = lax.ppermute(jnp.where(even, down, up), axis, between)]
    ppermute x0 -> x2, starting transfers between devices: none -> 1.69 us  [the longest x1 1.62 us: exchanged(): inner = lax.ppermute(jnp.where(even, up, down), axis, within)]
    ppermute x8 -> x6, starting transfers between devices: 11.3 us -> 10.8 us  [passed_along(): lax.ppermute(x, axis, [(i, (i + by) % length) for i in range(length)])]
  transfers between devices with their start and end apart: 8 -> 8, of which waited for: 5 -> 4; matrix products, arithmetic and copies ran while one was open for 1% -> 1% of each run, Pallas kernels for 20% -> 20%
where the time goes in v11:
time: 35.8 us; the launch traced here: 35.7 us
  Pallas kernels  17.3 us (48%)
  starting transfers between devices  12.5 us (35%)
  waiting for transfers between devices  5.33 us (15%)
    ppermute x6, starting transfers between devices, passed_along(): lax.ppermute(x, axis, [(i, (i + by) % length) for i in range(length)])  10.8 us
    pallas_call x1, Pallas kernels, on_device(): call(pick_kernel, 'pick', [vmem()] * 11 + [hbm()] * 2 + [vmem()] * 2, [((...  7.84 us
    ppermute x6, waiting for transfers between devices, passed_along(): lax.ppermute(x, axis, [(i, (i + by) % length) for i in range(length)])  3.38 us
    pallas_call x1, Pallas kernels, on_device(): call(stay_kernel, 'stay', [hbm()] * 2, [((sums, F32), vmem())], [pltpu.VM...  2.92 us
    pallas_call x1, Pallas kernels, on_device(): call(core_kernel, 'core', [vmem()] * 5, [(((3, (CX - 2) * PITCH, wide), B...  2.11 us
    ppermute x1, waiting for transfers between devices, exchanged(): outer = lax.ppermute(jnp.where(even, down, up), axis, between)  1.95 us
    ppermute x1, starting transfers between devices, exchanged(): inner = lax.ppermute(jnp.where(even, up, down), axis, within)  1.62 us
    pallas_call x1, Pallas kernels, on_device(): call(outer_kernel, 'outer', [vmem()] * 6, [(((3, 2 * HALO * PITCH, wide),...  1.6 us
  transfers between devices with their start and end apart: 8, of which 4 were waited for; matrix products, arithmetic and copies ran while one was open for 1% of the time, Pallas kernels for 20%

profile of v11, /device:TPU:0, one launch (start us, length us, event | category | flops | bytes accessed | tf_op | source)
XLA Modules:
  0.0 35.7 jit_solution(15970547186876016438)
XLA Ops:
  0.0 1.1 %pack.1 = (bf16[216,128]{1,0:T(8,128)(2,1)S(1)}, bf16[216,128]{1,0:T(8,128)(2,1)S(1)}, bf16[144,128]{1,0:T(8,128)(2,1)S(1)}) custom-call(bf16[16,8,512]{2,1,0:T(8,128)(2,1)} %bitcast.18, s32[8,512]{1,0:T(8,128)} %bitcast.19, s32[8]{0:T(128)} %bitcast.20), custom_call_target="tpu_custom_call" | custom-call | flops 1048576 | bytes 1048576 | tf_op jit(solution)/shard_map/pack/pallas_call | solution.py:549
  1.1 5.1 %collective-permute-start = (bf16[216,128]{1,0:T(8,128)(2,1)S(1)}, bf16[216,128]{1,0:T(8,128)(2,1)S(1)}, u32[]{:S(2)}, u32[]{:S(2)}) collective-permute-start(bf16[216,128]{1,0:T(8,128)(2,1)S(1)} %get-tuple-element.22), channel_id=1, source_target_pairs={{0,3},{1,0},{2,1},{3,2},{4,7},{5,4},{6,5},{7,6},{8,11},{9,8},{10,9... | collective-permute-start | bytes 165896 | tf_op jit(solution)/shard_map/ppermute | solution.py:64
  6.2 0.0 collective-permute-start.1
  6.2 2.9 %stay.1.part_ref = f32[544,256]{1,0:T(8,128)S(1)} custom-call(bf16[16,6144]{1,0:T(8,128)(2,1)} %bitcast.21, s32[1,6144]{1,0:T(1,128)} %bitcast.23), custom_call_target="tpu_custom_call" | custom-call | flops 5368709120 | bytes 1048576 | tf_op jit(solution)/shard_map/stay/pallas_call | solution.py:574
  9.1 0.0 copy-done.3
  9.1 0.1 copy.11.encoder_ref
  9.2 0.0 copy-done.4
  9.2 0.1 tile.10.bias_ref
  9.3 0.0 collective-permute-done.down_ref
  9.3 2.8 %collective-permute-done.1.up_ref = bf16[216,128]{1,0:T(8,128)(2,1)S(1)} collective-permute-done((bf16[216,128]{1,0:T(8,128)(2,1)S(1)}, bf16[216,128]{1,0:T(8,128)(2,1)S(1)}, u32[]{:S(2)}, u32[]{:S(2)}) %collective-permute-start.1) | collective-permute-done | bytes 55328 | tf_op jit(solution)/shard_map/ppermute | solution.py:64
  12.2 0.1 collective-permute-start.3
  12.2 1.6 %collective-permute-start.2 = (bf16[216,128]{1,0:T(8,128)(2,1)S(1)}, bf16[216,128]{1,0:T(8,128)(2,1)S(1)}, u32[]{:S(2)}, u32[]{:S(2)}) collective-permute-start(bf16[216,128]{1,0:T(8,128)(2,1)S(1)} %get-tuple-element.44), channel_id=1, source_target_pairs={{0,4},{4,0},{8,12},{12,8},{1,5},{5,1},{9,13},{13,9},{2,6},{6,2},{1... | collective-permute-start | bytes 165896 | tf_op jit(solution)/shard_map/ppermute | solution.py:74
  13.9 0.5 %near.1 = (f32[544,256]{1,0:T(8,128)S(1)}, bf16[18,1024]{1,0:T(8,128)(2,1)S(1)}) custom-call(bf16[216,128]{1,0:T(8,128)(2,1)S(1)} %collective-permute-done.down_ref, bf16[216,128]{1,0:T(8,128)(2,1)S(1)} %collective-permute-done.1.up_ref, f32[544,256]{1,0:T(8,128)S(1)} %stay.1.part_ref), custom_call_target="tpu_custom_call" | custom-call | flops 1073741824 | bytes 1048576 | tf_op jit(solution)/shard_map/near/pallas_call | solution.py:597
  14.4 2.0 %collective-permute-done.3 = bf16[216,128]{1,0:T(8,128)(2,1)S(1)} collective-permute-done((bf16[216,128]{1,0:T(8,128)(2,1)S(1)}, bf16[216,128]{1,0:T(8,128)(2,1)S(1)}, u32[]{:S(2)}, u32[]{:S(2)}) %collective-permute-start.3) | collective-permute-done | bytes 55328 | tf_op jit(solution)/shard_map/ppermute | solution.py:75
  16.3 0.0 collective-permute-done.2
  16.4 0.0 copy-start
  16.4 0.0 copy-start.1
  16.4 1.2 %mean.1 = (bf16[1024,128]{1,0:T(8,128)(2,1)S(1)}, bf16[384,128]{1,0:T(8,128)(2,1)S(1)}, bf16[384,128]{1,0:T(8,128)(2,1)S(1)}, bf16[18,4096]{1,0:T(8,128)(2,1)S(1)}) custom-call(bf16[18,1024]{1,0:T(8,128)(2,1)S(1)} %get-tuple-element.27.near_ref, bf16[216,128]{1,0:T(8,128)(2,1)S(1)} %get-tuple-element.42.west_ref, ...), custom_call_target="tpu_custom_call" | custom-call | flops 3221225472 | bytes 1048576 | tf_op jit(solution)/shard_map/mean/pallas_call | solution.py:606
  17.6 0.2 collective-permute-start.4
  17.8 1.6 %collective-permute-start.5 = (bf16[384,128]{1,0:T(8,128)(2,1)S(1)}, bf16[384,128]{1,0:T(8,128)(2,1)S(1)}, u32[]{:S(2)}, u32[]{:S(2)}) collective-permute-start(bf16[384,128]{1,0:T(8,128)(2,1)S(1)} %get-tuple-element.34), channel_id=1, source_target_pairs={{0,12},{4,0},{8,4},{12,8},{1,13},{5,1},{9,5},{13,9},{2,14},{6,2},{... | collective-permute-start | bytes 294920 | tf_op jit(solution)/shard_map/ppermute | solution.py:64
  19.4 0.0 copy-done
  19.4 0.0 copy-done.1
  19.4 2.1 %core.1 = (bf16[3,864,256]{2,1,0:T(8,128)(2,1)S(1)}, bf16[1024,256]{1,0:T(8,128)(2,1)S(1)}, bf16[3,256,2304]{2,1,0:T(8,128)(2,1)S(1)}, bf16[256,128]{1,0:T(8,128)(2,1)S(1)}, bf16[24,256]{1,0:T(8,128)(2,1)S(1)}) custom-call(bf16[1024,128]{1,0:T(8,128)(2,1)S(1)} %get-tuple-element.30.mean_ref, bf16[3,32,864]{2,1,0:T(8,128)(2,1)S(1)} %copy-done, ...), custom_call_target="tpu_custom_call" | custom-call | flops 2147483648 | bytes 1048576 | tf_op jit(solution)/shard_map/core/pallas_call | solution.py:634
  21.6 0.2 collective-permute-done.4.before_ref
  21.7 0.0 collective-permute-done.5.after_ref
  21.8 0.1 collective-permute-start.6
  21.8 3.8 %collective-permute-start.7 = (bf16[112,128]{1,0:T(8,128)(2,1)S(1)}, bf16[112,128]{1,0:T(8,128)(2,1)S(1)}, u32[]{:S(2)}, u32[]{:S(2)}) collective-permute-start(bf16[112,128]{1,0:T(8,128)(2,1)S(1)} %maximum_bitcast_fusion.1.low_ref), channel_id=1, source_target_pairs={{0,3},{1,0},{2,1},{3,2},{4,7},{5,4},{6,5},{7,6},{8,11},{9,8},{10,9... | collective-permute-start | bytes 86024 | tf_op jit(solution)/shard_map/ppermute | solution.py:64
  25.6 1.6 %outer.1.outer_ref = bf16[3,864,256]{2,1,0:T(8,128)(2,1)S(1)} custom-call(bf16[1024,256]{1,0:T(8,128)(2,1)S(1)} %get-tuple-element.32.own_ref, bf16[384,128]{1,0:T(8,128)(2,1)S(1)} %collective-permute-done.4.before_ref, bf16[384,128]{1,0:T(8,128)(2,1)S(1)} %collective-permute-done.5.after_ref, bf16[3,256,2304]{2,1,0:T(8,128)(2,1)S(1)} %get-tuple-element.35.band_ref, ...), custom_call_target="tpu_custom_call" | custom-call | flops 2147483648 | bytes 1048576 | tf_op jit(solution)/shard_map/outer/pallas_call | solution.py:649
  27.3 0.4 %collective-permute-done.6.below_ref = bf16[112,128]{1,0:T(8,128)(2,1)S(1)} collective-permute-done((bf16[112,128]{1,0:T(8,128)(2,1)S(1)}, bf16[112,128]{1,0:T(8,128)(2,1)S(1)}, u32[]{:S(2)}, u32[]{:S(2)}) %collective-permute-start.6) | collective-permute-done | bytes 28704 | tf_op jit(solution)/shard_map/ppermute | solution.py:64
  27.7 0.0 collective-permute-done.7.above_ref
  27.7 0.0 copy-done.2
  27.7 7.8 %pick.1 = f32[3,1,10240]{2,1,0:T(1,128)} custom-call(bf16[3,864,256]{2,1,0:T(8,128)(2,1)S(1)} %get-tuple-element.31.middle_ref, bf16[3,864,256]{2,1,0:T(8,128)(2,1)S(1)} %outer.1.outer_ref, bf16[1024,256]{1,0:T(8,128)(2,1)S(1)} %get-tuple-element.32.own_ref, bf16[112,128]{1,0:T(8,128)(2,1)S(1)} %collective-permute-done.6.below_ref, ...), custom_call_target="tpu_custom_call" | custom-call | flops 8589934592 | bytes 1048576 | tf_op jit(solution)/shard_map/pick/pallas_call | solution.py:658
  (13 shorter events, 0.1 us)
Async XLA Ops:
  1.1 8.3 %collective-permute-start = (bf16[216,128]{1,0:T(8,128)(2,1)S(1)}, bf16[216,128]{1,0:T(8,128)(2,1)S(1)}, u32[]{:S(2)}, u32[]{:S(2)}) collective-permute-start(bf16[216,128]{1,0:T(8,128)(2,1)S(1)} %get-tuple-element.22), channel_id=1, source_target_pairs={{0,3},{1,0},{2,1},{3,2},{4,7},{5,4},{6,5},{7,6},{8,11},{9,8},{10,9... | collective-permute-start | bytes 165896 | tf_op jit(solution)/shard_map/ppermute | solution.py:64
  6.2 6.0 %collective-permute-start.1 = (bf16[216,128]{1,0:T(8,128)(2,1)S(1)}, bf16[216,128]{1,0:T(8,128)(2,1)S(1)}, u32[]{:S(2)}, u32[]{:S(2)}) collective-permute-start(bf16[216,128]{1,0:T(8,128)(2,1)S(1)} %get-tuple-element.23), channel_id=1, source_target_pairs={{0,1},{1,2},{2,3},{3,0},{4,5},{5,6},{6,7},{7,4},{8,9},{9,10},{10,1... | collective-permute-start | bytes 165896 | tf_op jit(solution)/shard_map/ppermute | solution.py:64
  6.2 3.0 %copy-start.3 = (bf16[32,16]{0,1:T(8,128)(2,1)S(1)}, bf16[32,16]{0,1:T(8,128)(2,1)}, u32[]{:S(2)}) copy-start(bf16[32,16]{0,1:T(8,128)(2,1)} %param.15) | copy-start | bytes 3076
  6.2 3.1 %copy-start.4 = (f32[3,32]{1,0:T(4,128)S(1)}, f32[3,32]{1,0:T(4,128)}, u32[]{:S(2)}) copy-start(f32[3,32]{1,0:T(4,128)} %param.17) | copy-start | bytes 1156
  12.2 4.2 %collective-permute-start.3 = (bf16[216,128]{1,0:T(8,128)(2,1)S(1)}, bf16[216,128]{1,0:T(8,128)(2,1)S(1)}, u32[]{:S(2)}, u32[]{:S(2)}) collective-permute-start(bf16[216,128]{1,0:T(8,128)(2,1)S(1)} %get-tuple-element.43), channel_id=1, source_target_pairs={{0,12},{4,8},{8,4},{12,0},{1,13},{5,9},{9,5},{13,1},{2,14},{6,10},... | collective-permute-start | bytes 165896 | tf_op jit(solution)/shard_map/ppermute | solution.py:75
  12.2 4.1 %collective-permute-start.2 = (bf16[216,128]{1,0:T(8,128)(2,1)S(1)}, bf16[216,128]{1,0:T(8,128)(2,1)S(1)}, u32[]{:S(2)}, u32[]{:S(2)}) collective-permute-start(bf16[216,128]{1,0:T(8,128)(2,1)S(1)} %get-tuple-element.44), channel_id=1, source_target_pairs={{0,4},{4,0},{8,12},{12,8},{1,5},{5,1},{9,13},{13,9},{2,6},{6,2},{1... | collective-permute-start | bytes 165896 | tf_op jit(solution)/shard_map/ppermute | solution.py:74
  16.4 3.1 %copy-start = (bf16[3,32,864]{2,1,0:T(8,128)(2,1)S(1)}, bf16[3,32,864]{2,1,0:T(8,128)(2,1)}, u32[]{:S(2)}) copy-start(bf16[3,32,864]{2,1,0:T(8,128)(2,1)} %weight_ref.1) | copy-start | bytes 497668
  16.4 3.1 %copy-start.1 = (bf16[3,32]{1,0:T(4,128)(2,1)S(1)}, bf16[3,32]{1,0:T(4,128)(2,1)}, u32[]{:S(2)}) copy-start(bf16[3,32]{1,0:T(4,128)(2,1)} %decoder_ref.1) | copy-start | bytes 580
  17.6 4.1 %collective-permute-start.4 = (bf16[384,128]{1,0:T(8,128)(2,1)S(1)}, bf16[384,128]{1,0:T(8,128)(2,1)S(1)}, u32[]{:S(2)}, u32[]{:S(2)}) collective-permute-start(bf16[384,128]{1,0:T(8,128)(2,1)S(1)} %get-tuple-element.33), channel_id=1, source_target_pairs={{0,4},{4,8},{8,12},{12,0},{1,5},{5,9},{9,13},{13,1},{2,6},{6,10},{... | collective-permute-start | bytes 294920 | tf_op jit(solution)/shard_map/ppermute | solution.py:64
  17.8 3.9 %collective-permute-start.5 = (bf16[384,128]{1,0:T(8,128)(2,1)S(1)}, bf16[384,128]{1,0:T(8,128)(2,1)S(1)}, u32[]{:S(2)}, u32[]{:S(2)}) collective-permute-start(bf16[384,128]{1,0:T(8,128)(2,1)S(1)} %get-tuple-element.34), channel_id=1, source_target_pairs={{0,12},{4,0},{8,4},{12,8},{1,13},{5,1},{9,5},{13,9},{2,14},{6,2},{... | collective-permute-start | bytes 294920 | tf_op jit(solution)/shard_map/ppermute | solution.py:64
  21.8 5.9 %collective-permute-start.6 = (bf16[112,128]{1,0:T(8,128)(2,1)S(1)}, bf16[112,128]{1,0:T(8,128)(2,1)S(1)}, u32[]{:S(2)}, u32[]{:S(2)}) collective-permute-start(bf16[112,128]{1,0:T(8,128)(2,1)S(1)} %maximum_bitcast_fusion.high_ref), channel_id=1, source_target_pairs={{0,1},{1,2},{2,3},{3,0},{4,5},{5,6},{6,7},{7,4},{8,9},{9,10},{10,1... | collective-permute-start | bytes 86024 | tf_op jit(solution)/shard_map/ppermute | solution.py:64
  21.8 5.8 %collective-permute-start.7 = (bf16[112,128]{1,0:T(8,128)(2,1)S(1)}, bf16[112,128]{1,0:T(8,128)(2,1)S(1)}, u32[]{:S(2)}, u32[]{:S(2)}) collective-permute-start(bf16[112,128]{1,0:T(8,128)(2,1)S(1)} %maximum_bitcast_fusion.1.low_ref), channel_id=1, source_target_pairs={{0,3},{1,0},{2,1},{3,2},{4,7},{5,4},{6,5},{7,6},{8,11},{9,8},{10,9... | collective-permute-start | bytes 86024 | tf_op jit(solution)/shard_map/ppermute | solution.py:64
  25.6 2.0 %copy-start.2 = (bf16[3,16]{1,0:T(4,128)(2,1)S(1)}, bf16[3,16]{1,0:T(4,128)(2,1)}, u32[]{:S(2)}) copy-start(bf16[3,16]{1,0:T(4,128)(2,1)} %self_ref.1) | copy-start | bytes 292

commit v12 on v11

--- a/solution.py
+++ b/solution.py
@@ -126,16 +126,17 @@
     copies = [pltpu.make_async_copy(a, b, sems.at[k]) for k, (a, b) in enumerate(pairs)]
     for copy in copies:
         copy.start()
-    for copy in copies:
+    for copy in copies[:2]:
         copy.wait()
     feat_dim, buckets, cap = feat_ref.shape
-    turned = jnp.swapaxes(feat_ref[...].astype(F32), 0, 1)
     high, low = cell_codes(slot_ref[...])
     lane = lax.broadcasted_iota(jnp.int32, (1, cap), 1)
     high = high.astype(F32)
     low = low.astype(F32)
     blocks = cap // 128
     step = (feat_dim + 2) * blocks
+    copies[2].wait()
+    turned = jnp.swapaxes(feat_ref[...].astype(F32), 0, 1)
     for out_ref, chosen in ((down_ref, (0, 3, 5)), (up_ref, (2, 4, 7)), (middle_ref, (1, 6))):
         for place, bucket in enumerate(chosen):
             code = jnp.where(

time: 35.8 us -> 35.8 us (level)
  no operation moved by 1% of the time
where the time goes in v12:
time: 35.8 us; the launch traced here: 35.7 us
  Pallas kernels  17.2 us (48%)
  starting transfers between devices  12.5 us (35%)
  waiting for transfers between devices  5.35 us (15%)
    ppermute x6, starting transfers between devices, passed_along(): lax.ppermute(x, axis, [(i, (i + by) % length) for i in range(length)])  10.8 us
    pallas_call x1, Pallas kernels, on_device(): call(pick_kernel, 'pick', [vmem()] * 11 + [hbm()] * 2 + [vmem()] * 2, [((...  7.85 us
    ppermute x6, waiting for transfers between devices, passed_along(): lax.ppermute(x, axis, [(i, (i + by) % length) for i in range(length)])  3.4 us
    pallas_call x1, Pallas kernels, on_device(): call(stay_kernel, 'stay', [hbm()] * 2, [((sums, F32), vmem())], [pltpu.VM...  2.92 us
    pallas_call x1, Pallas kernels, on_device(): call(core_kernel, 'core', [vmem()] * 5, [(((3, (CX - 2) * PITCH, wide), B...  2.11 us
    ppermute x1, waiting for transfers between devices, exchanged(): outer = lax.ppermute(jnp.where(even, down, up), axis, between)  1.95 us
    ppermute x1, starting transfers between devices, exchanged(): inner = lax.ppermute(jnp.where(even, up, down), axis, within)  1.62 us
    pallas_call x1, Pallas kernels, on_device(): call(outer_kernel, 'outer', [vmem()] * 6, [(((3, 2 * HALO * PITCH, wide),...  1.58 us
  transfers between devices with their start and end apart: 8, of which 4 were waited for; matrix products, arithmetic and copies ran while one was open for 1% of the time, Pallas kernels for 20%

profile of v12, /device:TPU:0, one launch (start us, length us, event | category | flops | bytes accessed | tf_op | source)
XLA Modules:
  0.0 35.7 jit_solution(14496026614796516940)
XLA Ops:
  0.0 1.0 %pack.1 = (bf16[216,128]{1,0:T(8,128)(2,1)S(1)}, bf16[216,128]{1,0:T(8,128)(2,1)S(1)}, bf16[144,128]{1,0:T(8,128)(2,1)S(1)}) custom-call(bf16[16,8,512]{2,1,0:T(8,128)(2,1)} %bitcast.18, s32[8,512]{1,0:T(8,128)} %bitcast.19, s32[8]{0:T(128)} %bitcast.20), custom_call_target="tpu_custom_call" | custom-call | flops 1048576 | bytes 1048576 | tf_op jit(solution)/shard_map/pack/pallas_call | solution.py:550
  1.0 5.1 %collective-permute-start = (bf16[216,128]{1,0:T(8,128)(2,1)S(1)}, bf16[216,128]{1,0:T(8,128)(2,1)S(1)}, u32[]{:S(2)}, u32[]{:S(2)}) collective-permute-start(bf16[216,128]{1,0:T(8,128)(2,1)S(1)} %get-tuple-element.22), channel_id=1, source_target_pairs={{0,3},{1,0},{2,1},{3,2},{4,7},{5,4},{6,5},{7,6},{8,11},{9,8},{10,9... | collective-permute-start | bytes 165896 | tf_op jit(solution)/shard_map/ppermute | solution.py:64
  6.2 0.0 collective-permute-start.1
  6.2 2.9 %stay.1.part_ref = f32[544,256]{1,0:T(8,128)S(1)} custom-call(bf16[16,6144]{1,0:T(8,128)(2,1)} %bitcast.21, s32[1,6144]{1,0:T(1,128)} %bitcast.23), custom_call_target="tpu_custom_call" | custom-call | flops 5368709120 | bytes 1048576 | tf_op jit(solution)/shard_map/stay/pallas_call | solution.py:575
  9.1 0.0 copy-done.3
  9.1 0.1 copy.11.encoder_ref
  9.2 0.0 copy-done.4
  9.2 0.1 tile.10.bias_ref
  9.3 0.0 collective-permute-done.down_ref
  9.3 2.8 %collective-permute-done.1.up_ref = bf16[216,128]{1,0:T(8,128)(2,1)S(1)} collective-permute-done((bf16[216,128]{1,0:T(8,128)(2,1)S(1)}, bf16[216,128]{1,0:T(8,128)(2,1)S(1)}, u32[]{:S(2)}, u32[]{:S(2)}) %collective-permute-start.1) | collective-permute-done | bytes 55328 | tf_op jit(solution)/shard_map/ppermute | solution.py:64
  12.1 0.1 collective-permute-start.3
  12.2 1.6 %collective-permute-start.2 = (bf16[216,128]{1,0:T(8,128)(2,1)S(1)}, bf16[216,128]{1,0:T(8,128)(2,1)S(1)}, u32[]{:S(2)}, u32[]{:S(2)}) collective-permute-start(bf16[216,128]{1,0:T(8,128)(2,1)S(1)} %get-tuple-element.44), channel_id=1, source_target_pairs={{0,4},{4,0},{8,12},{12,8},{1,5},{5,1},{9,13},{13,9},{2,6},{6,2},{1... | collective-permute-start | bytes 165896 | tf_op jit(solution)/shard_map/ppermute | solution.py:74
  13.8 0.5 %near.1 = (f32[544,256]{1,0:T(8,128)S(1)}, bf16[18,1024]{1,0:T(8,128)(2,1)S(1)}) custom-call(bf16[216,128]{1,0:T(8,128)(2,1)S(1)} %collective-permute-done.down_ref, bf16[216,128]{1,0:T(8,128)(2,1)S(1)} %collective-permute-done.1.up_ref, f32[544,256]{1,0:T(8,128)S(1)} %stay.1.part_ref), custom_call_target="tpu_custom_call" | custom-call | flops 1073741824 | bytes 1048576 | tf_op jit(solution)/shard_map/near/pallas_call | solution.py:598
  14.4 2.0 %collective-permute-done.3 = bf16[216,128]{1,0:T(8,128)(2,1)S(1)} collective-permute-done((bf16[216,128]{1,0:T(8,128)(2,1)S(1)}, bf16[216,128]{1,0:T(8,128)(2,1)S(1)}, u32[]{:S(2)}, u32[]{:S(2)}) %collective-permute-start.3) | collective-permute-done | bytes 55328 | tf_op jit(solution)/shard_map/ppermute | solution.py:75
  16.3 0.0 collective-permute-done.2
  16.3 0.0 copy-start
  16.4 0.0 copy-start.1
  16.4 1.2 %mean.1 = (bf16[1024,128]{1,0:T(8,128)(2,1)S(1)}, bf16[384,128]{1,0:T(8,128)(2,1)S(1)}, bf16[384,128]{1,0:T(8,128)(2,1)S(1)}, bf16[18,4096]{1,0:T(8,128)(2,1)S(1)}) custom-call(bf16[18,1024]{1,0:T(8,128)(2,1)S(1)} %get-tuple-element.27.near_ref, bf16[216,128]{1,0:T(8,128)(2,1)S(1)} %get-tuple-element.42.west_ref, ...), custom_call_target="tpu_custom_call" | custom-call | flops 3221225472 | bytes 1048576 | tf_op jit(solution)/shard_map/mean/pallas_call | solution.py:607
  17.6 0.2 collective-permute-start.4
  17.8 1.6 %collective-permute-start.5 = (bf16[384,128]{1,0:T(8,128)(2,1)S(1)}, bf16[384,128]{1,0:T(8,128)(2,1)S(1)}, u32[]{:S(2)}, u32[]{:S(2)}) collective-permute-start(bf16[384,128]{1,0:T(8,128)(2,1)S(1)} %get-tuple-element.34), channel_id=1, source_target_pairs={{0,12},{4,0},{8,4},{12,8},{1,13},{5,1},{9,5},{13,9},{2,14},{6,2},{... | collective-permute-start | bytes 294920 | tf_op jit(solution)/shard_map/ppermute | solution.py:64
  19.4 0.0 copy-done
  19.4 0.0 copy-done.1
  19.4 2.1 %core.1 = (bf16[3,864,256]{2,1,0:T(8,128)(2,1)S(1)}, bf16[1024,256]{1,0:T(8,128)(2,1)S(1)}, bf16[3,256,2304]{2,1,0:T(8,128)(2,1)S(1)}, bf16[256,128]{1,0:T(8,128)(2,1)S(1)}, bf16[24,256]{1,0:T(8,128)(2,1)S(1)}) custom-call(bf16[1024,128]{1,0:T(8,128)(2,1)S(1)} %get-tuple-element.30.mean_ref, bf16[3,32,864]{2,1,0:T(8,128)(2,1)S(1)} %copy-done, ...), custom_call_target="tpu_custom_call" | custom-call | flops 2147483648 | bytes 1048576 | tf_op jit(solution)/shard_map/core/pallas_call | solution.py:635
  21.5 0.2 collective-permute-done.4.before_ref
  21.7 0.0 collective-permute-done.5.after_ref
  21.7 0.1 collective-permute-start.6
  21.8 3.8 %collective-permute-start.7 = (bf16[112,128]{1,0:T(8,128)(2,1)S(1)}, bf16[112,128]{1,0:T(8,128)(2,1)S(1)}, u32[]{:S(2)}, u32[]{:S(2)}) collective-permute-start(bf16[112,128]{1,0:T(8,128)(2,1)S(1)} %maximum_bitcast_fusion.1.low_ref), channel_id=1, source_target_pairs={{0,3},{1,0},{2,1},{3,2},{4,7},{5,4},{6,5},{7,6},{8,11},{9,8},{10,9... | collective-permute-start | bytes 86024 | tf_op jit(solution)/shard_map/ppermute | solution.py:64
  25.6 1.6 %outer.1.outer_ref = bf16[3,864,256]{2,1,0:T(8,128)(2,1)S(1)} custom-call(bf16[1024,256]{1,0:T(8,128)(2,1)S(1)} %get-tuple-element.32.own_ref, bf16[384,128]{1,0:T(8,128)(2,1)S(1)} %collective-permute-done.4.before_ref, bf16[384,128]{1,0:T(8,128)(2,1)S(1)} %collective-permute-done.5.after_ref, bf16[3,256,2304]{2,1,0:T(8,128)(2,1)S(1)} %get-tuple-element.35.band_ref, ...), custom_call_target="tpu_custom_call" | custom-call | flops 2147483648 | bytes 1048576 | tf_op jit(solution)/shard_map/outer/pallas_call | solution.py:650
  27.2 0.4 %collective-permute-done.6.below_ref = bf16[112,128]{1,0:T(8,128)(2,1)S(1)} collective-permute-done((bf16[112,128]{1,0:T(8,128)(2,1)S(1)}, bf16[112,128]{1,0:T(8,128)(2,1)S(1)}, u32[]{:S(2)}, u32[]{:S(2)}) %collective-permute-start.6) | collective-permute-done | bytes 28704 | tf_op jit(solution)/shard_map/ppermute | solution.py:64
  27.6 0.0 collective-permute-done.7.above_ref
  27.6 0.0 copy-done.2
  27.6 7.9 %pick.1 = f32[3,1,10240]{2,1,0:T(1,128)} custom-call(bf16[3,864,256]{2,1,0:T(8,128)(2,1)S(1)} %get-tuple-element.31.middle_ref, bf16[3,864,256]{2,1,0:T(8,128)(2,1)S(1)} %outer.1.outer_ref, bf16[1024,256]{1,0:T(8,128)(2,1)S(1)} %get-tuple-element.32.own_ref, bf16[112,128]{1,0:T(8,128)(2,1)S(1)} %collective-permute-done.6.below_ref, ...), custom_call_target="tpu_custom_call" | custom-call | flops 8589934592 | bytes 1048576 | tf_op jit(solution)/shard_map/pick/pallas_call | solution.py:659
  (13 shorter events, 0.1 us)
Async XLA Ops:
  1.0 8.3 %collective-permute-start = (bf16[216,128]{1,0:T(8,128)(2,1)S(1)}, bf16[216,128]{1,0:T(8,128)(2,1)S(1)}, u32[]{:S(2)}, u32[]{:S(2)}) collective-permute-start(bf16[216,128]{1,0:T(8,128)(2,1)S(1)} %get-tuple-element.22), channel_id=1, source_target_pairs={{0,3},{1,0},{2,1},{3,2},{4,7},{5,4},{6,5},{7,6},{8,11},{9,8},{10,9... | collective-permute-start | bytes 165896 | tf_op jit(solution)/shard_map/ppermute | solution.py:64
  6.2 6.0 %collective-permute-start.1 = (bf16[216,128]{1,0:T(8,128)(2,1)S(1)}, bf16[216,128]{1,0:T(8,128)(2,1)S(1)}, u32[]{:S(2)}, u32[]{:S(2)}) collective-permute-start(bf16[216,128]{1,0:T(8,128)(2,1)S(1)} %get-tuple-element.23), channel_id=1, source_target_pairs={{0,1},{1,2},{2,3},{3,0},{4,5},{5,6},{6,7},{7,4},{8,9},{9,10},{10,1... | collective-permute-start | bytes 165896 | tf_op jit(solution)/shard_map/ppermute | solution.py:64
  6.2 3.0 %copy-start.3 = (bf16[32,16]{0,1:T(8,128)(2,1)S(1)}, bf16[32,16]{0,1:T(8,128)(2,1)}, u32[]{:S(2)}) copy-start(bf16[32,16]{0,1:T(8,128)(2,1)} %param.15) | copy-start | bytes 3076
  6.2 3.1 %copy-start.4 = (f32[3,32]{1,0:T(4,128)S(1)}, f32[3,32]{1,0:T(4,128)}, u32[]{:S(2)}) copy-start(f32[3,32]{1,0:T(4,128)} %param.17) | copy-start | bytes 1156
  12.1 4.2 %collective-permute-start.3 = (bf16[216,128]{1,0:T(8,128)(2,1)S(1)}, bf16[216,128]{1,0:T(8,128)(2,1)S(1)}, u32[]{:S(2)}, u32[]{:S(2)}) collective-permute-start(bf16[216,128]{1,0:T(8,128)(2,1)S(1)} %get-tuple-element.43), channel_id=1, source_target_pairs={{0,12},{4,8},{8,4},{12,0},{1,13},{5,9},{9,5},{13,1},{2,14},{6,10},... | collective-permute-start | bytes 165896 | tf_op jit(solution)/shard_map/ppermute | solution.py:75
  12.2 4.1 %collective-permute-start.2 = (bf16[216,128]{1,0:T(8,128)(2,1)S(1)}, bf16[216,128]{1,0:T(8,128)(2,1)S(1)}, u32[]{:S(2)}, u32[]{:S(2)}) collective-permute-start(bf16[216,128]{1,0:T(8,128)(2,1)S(1)} %get-tuple-element.44), channel_id=1, source_target_pairs={{0,4},{4,0},{8,12},{12,8},{1,5},{5,1},{9,13},{13,9},{2,6},{6,2},{1... | collective-permute-start | bytes 165896 | tf_op jit(solution)/shard_map/ppermute | solution.py:74
  16.3 3.1 %copy-start = (bf16[3,32,864]{2,1,0:T(8,128)(2,1)S(1)}, bf16[3,32,864]{2,1,0:T(8,128)(2,1)}, u32[]{:S(2)}) copy-start(bf16[3,32,864]{2,1,0:T(8,128)(2,1)} %weight_ref.1) | copy-start | bytes 497668
  16.4 3.1 %copy-start.1 = (bf16[3,32]{1,0:T(4,128)(2,1)S(1)}, bf16[3,32]{1,0:T(4,128)(2,1)}, u32[]{:S(2)}) copy-start(bf16[3,32]{1,0:T(4,128)(2,1)} %decoder_ref.1) | copy-start | bytes 580
  17.6 4.1 %collective-permute-start.4 = (bf16[384,128]{1,0:T(8,128)(2,1)S(1)}, bf16[384,128]{1,0:T(8,128)(2,1)S(1)}, u32[]{:S(2)}, u32[]{:S(2)}) collective-permute-start(bf16[384,128]{1,0:T(8,128)(2,1)S(1)} %get-tuple-element.33), channel_id=1, source_target_pairs={{0,4},{4,8},{8,12},{12,0},{1,5},{5,9},{9,13},{13,1},{2,6},{6,10},{... | collective-permute-start | bytes 294920 | tf_op jit(solution)/shard_map/ppermute | solution.py:64
  17.8 3.9 %collective-permute-start.5 = (bf16[384,128]{1,0:T(8,128)(2,1)S(1)}, bf16[384,128]{1,0:T(8,128)(2,1)S(1)}, u32[]{:S(2)}, u32[]{:S(2)}) collective-permute-start(bf16[384,128]{1,0:T(8,128)(2,1)S(1)} %get-tuple-element.34), channel_id=1, source_target_pairs={{0,12},{4,0},{8,4},{12,8},{1,13},{5,1},{9,5},{13,9},{2,14},{6,2},{... | collective-permute-start | bytes 294920 | tf_op jit(solution)/shard_map/ppermute | solution.py:64
  21.7 5.9 %collective-permute-start.6 = (bf16[112,128]{1,0:T(8,128)(2,1)S(1)}, bf16[112,128]{1,0:T(8,128)(2,1)S(1)}, u32[]{:S(2)}, u32[]{:S(2)}) collective-permute-start(bf16[112,128]{1,0:T(8,128)(2,1)S(1)} %maximum_bitcast_fusion.high_ref), channel_id=1, source_target_pairs={{0,1},{1,2},{2,3},{3,0},{4,5},{5,6},{6,7},{7,4},{8,9},{9,10},{10,1... | collective-permute-start | bytes 86024 | tf_op jit(solution)/shard_map/ppermute | solution.py:64
  21.8 5.8 %collective-permute-start.7 = (bf16[112,128]{1,0:T(8,128)(2,1)S(1)}, bf16[112,128]{1,0:T(8,128)(2,1)S(1)}, u32[]{:S(2)}, u32[]{:S(2)}) collective-permute-start(bf16[112,128]{1,0:T(8,128)(2,1)S(1)} %maximum_bitcast_fusion.1.low_ref), channel_id=1, source_target_pairs={{0,3},{1,0},{2,1},{3,2},{4,7},{5,4},{6,5},{7,6},{8,11},{9,8},{10,9... | collective-permute-start | bytes 86024 | tf_op jit(solution)/shard_map/ppermute | solution.py:64
  25.6 2.0 %copy-start.2 = (bf16[3,16]{1,0:T(4,128)(2,1)S(1)}, bf16[3,16]{1,0:T(4,128)(2,1)}, u32[]{:S(2)}) copy-start(bf16[3,16]{1,0:T(4,128)(2,1)} %self_ref.1) | copy-start | bytes 292

commit v13 on v11

--- a/solution.py
+++ b/solution.py
@@ -27,7 +27,7 @@
 
 CHUNK = 1024
 GRANT = 24
-CORE_PARTS = ((0, 3), (3, 3))
+CORE_PARTS = ((0, 2), (2, 2), (4, 2))
 ORDER = (
     (0, 0, 4),
     (0, 4, 4),

time: 35.8 us -> 35.8 us (level)
  no operation moved by 1% of the time
where the time goes in v13:
time: 35.8 us; the launch traced here: 35.7 us
  Pallas kernels  17.1 us (48%)
  starting transfers between devices  12.5 us (35%)
  waiting for transfers between devices  5.49 us (15%)
    ppermute x6, starting transfers between devices, passed_along(): lax.ppermute(x, axis, [(i, (i + by) % length) for i in range(length)])  10.8 us
    pallas_call x1, Pallas kernels, on_device(): call(pick_kernel, 'pick', [vmem()] * 11 + [hbm()] * 2 + [vmem()] * 2, [((...  7.84 us
    ppermute x6, waiting for transfers between devices, passed_along(): lax.ppermute(x, axis, [(i, (i + by) % length) for i in range(length)])  3.53 us
    pallas_call x1, Pallas kernels, on_device(): call(stay_kernel, 'stay', [hbm()] * 2, [((sums, F32), vmem())], [pltpu.VM...  2.92 us
    pallas_call x1, Pallas kernels, on_device(): call(core_kernel, 'core', [vmem()] * 5, [(((3, (CX - 2) * PITCH, wide), B...  1.96 us
    ppermute x1, waiting for transfers between devices, exchanged(): outer = lax.ppermute(jnp.where(even, down, up), axis, between)  1.95 us
    ppermute x1, starting transfers between devices, exchanged(): inner = lax.ppermute(jnp.where(even, up, down), axis, within)  1.62 us
    pallas_call x1, Pallas kernels, on_device(): call(outer_kernel, 'outer', [vmem()] * 6, [(((3, 2 * HALO * PITCH, wide),...  1.6 us
  transfers between devices with their start and end apart: 8, of which 4 were waited for; matrix products, arithmetic and copies ran while one was open for 1% of the time, Pallas kernels for 20%

profile of v13, /device:TPU:0, one launch (start us, length us, event | category | flops | bytes accessed | tf_op | source)
XLA Modules:
  0.0 35.7 jit_solution(4777986222634592276)
XLA Ops:
  0.0 1.1 %pack.1 = (bf16[216,128]{1,0:T(8,128)(2,1)S(1)}, bf16[216,128]{1,0:T(8,128)(2,1)S(1)}, bf16[144,128]{1,0:T(8,128)(2,1)S(1)}) custom-call(bf16[16,8,512]{2,1,0:T(8,128)(2,1)} %bitcast.18, s32[8,512]{1,0:T(8,128)} %bitcast.19, s32[8]{0:T(128)} %bitcast.20), custom_call_target="tpu_custom_call" | custom-call | flops 1048576 | bytes 1048576 | tf_op jit(solution)/shard_map/pack/pallas_call | solution.py:549
  1.1 5.1 %collective-permute-start = (bf16[216,128]{1,0:T(8,128)(2,1)S(1)}, bf16[216,128]{1,0:T(8,128)(2,1)S(1)}, u32[]{:S(2)}, u32[]{:S(2)}) collective-permute-start(bf16[216,128]{1,0:T(8,128)(2,1)S(1)} %get-tuple-element.22), channel_id=1, source_target_pairs={{0,3},{1,0},{2,1},{3,2},{4,7},{5,4},{6,5},{7,6},{8,11},{9,8},{10,9... | collective-permute-start | bytes 165896 | tf_op jit(solution)/shard_map/ppermute | solution.py:64
  6.2 0.0 collective-permute-start.1
  6.2 2.9 %stay.1.part_ref = f32[544,256]{1,0:T(8,128)S(1)} custom-call(bf16[16,6144]{1,0:T(8,128)(2,1)} %bitcast.21, s32[1,6144]{1,0:T(1,128)} %bitcast.23), custom_call_target="tpu_custom_call" | custom-call | flops 5368709120 | bytes 1048576 | tf_op jit(solution)/shard_map/stay/pallas_call | solution.py:574
  9.1 0.0 copy-done.3
  9.1 0.1 copy.11.encoder_ref
  9.2 0.0 copy-done.4
  9.2 0.1 tile.10.bias_ref
  9.3 0.0 collective-permute-done.down_ref
  9.3 2.8 %collective-permute-done.1.up_ref = bf16[216,128]{1,0:T(8,128)(2,1)S(1)} collective-permute-done((bf16[216,128]{1,0:T(8,128)(2,1)S(1)}, bf16[216,128]{1,0:T(8,128)(2,1)S(1)}, u32[]{:S(2)}, u32[]{:S(2)}) %collective-permute-start.1) | collective-permute-done | bytes 55328 | tf_op jit(solution)/shard_map/ppermute | solution.py:64
  12.2 0.1 collective-permute-start.3
  12.2 1.6 %collective-permute-start.2 = (bf16[216,128]{1,0:T(8,128)(2,1)S(1)}, bf16[216,128]{1,0:T(8,128)(2,1)S(1)}, u32[]{:S(2)}, u32[]{:S(2)}) collective-permute-start(bf16[216,128]{1,0:T(8,128)(2,1)S(1)} %get-tuple-element.44), channel_id=1, source_target_pairs={{0,4},{4,0},{8,12},{12,8},{1,5},{5,1},{9,13},{13,9},{2,6},{6,2},{1... | collective-permute-start | bytes 165896 | tf_op jit(solution)/shard_map/ppermute | solution.py:74
  13.9 0.5 %near.1 = (f32[544,256]{1,0:T(8,128)S(1)}, bf16[18,1024]{1,0:T(8,128)(2,1)S(1)}) custom-call(bf16[216,128]{1,0:T(8,128)(2,1)S(1)} %collective-permute-done.down_ref, bf16[216,128]{1,0:T(8,128)(2,1)S(1)} %collective-permute-done.1.up_ref, f32[544,256]{1,0:T(8,128)S(1)} %stay.1.part_ref), custom_call_target="tpu_custom_call" | custom-call | flops 1073741824 | bytes 1048576 | tf_op jit(solution)/shard_map/near/pallas_call | solution.py:597
  14.4 2.0 %collective-permute-done.3 = bf16[216,128]{1,0:T(8,128)(2,1)S(1)} collective-permute-done((bf16[216,128]{1,0:T(8,128)(2,1)S(1)}, bf16[216,128]{1,0:T(8,128)(2,1)S(1)}, u32[]{:S(2)}, u32[]{:S(2)}) %collective-permute-start.3) | collective-permute-done | bytes 55328 | tf_op jit(solution)/shard_map/ppermute | solution.py:75
  16.3 0.0 collective-permute-done.2
  16.4 0.0 copy-start
  16.4 0.0 copy-start.1
  16.4 1.2 %mean.1 = (bf16[1024,128]{1,0:T(8,128)(2,1)S(1)}, bf16[384,128]{1,0:T(8,128)(2,1)S(1)}, bf16[384,128]{1,0:T(8,128)(2,1)S(1)}, bf16[18,4096]{1,0:T(8,128)(2,1)S(1)}) custom-call(bf16[18,1024]{1,0:T(8,128)(2,1)S(1)} %get-tuple-element.27.near_ref, bf16[216,128]{1,0:T(8,128)(2,1)S(1)} %get-tuple-element.42.west_ref, ...), custom_call_target="tpu_custom_call" | custom-call | flops 3221225472 | bytes 1048576 | tf_op jit(solution)/shard_map/mean/pallas_call | solution.py:606
  17.6 0.2 collective-permute-start.4
  17.8 1.6 %collective-permute-start.5 = (bf16[384,128]{1,0:T(8,128)(2,1)S(1)}, bf16[384,128]{1,0:T(8,128)(2,1)S(1)}, u32[]{:S(2)}, u32[]{:S(2)}) collective-permute-start(bf16[384,128]{1,0:T(8,128)(2,1)S(1)} %get-tuple-element.34), channel_id=1, source_target_pairs={{0,12},{4,0},{8,4},{12,8},{1,13},{5,1},{9,5},{13,9},{2,14},{6,2},{... | collective-permute-start | bytes 294920 | tf_op jit(solution)/shard_map/ppermute | solution.py:64
  19.4 0.0 copy-done
  19.4 0.0 copy-done.1
  19.4 2.0 %core.1 = (bf16[3,864,256]{2,1,0:T(8,128)(2,1)S(1)}, bf16[1024,256]{1,0:T(8,128)(2,1)S(1)}, bf16[3,256,2304]{2,1,0:T(8,128)(2,1)S(1)}, bf16[256,128]{1,0:T(8,128)(2,1)S(1)}, bf16[24,256]{1,0:T(8,128)(2,1)S(1)}) custom-call(bf16[1024,128]{1,0:T(8,128)(2,1)S(1)} %get-tuple-element.30.mean_ref, bf16[3,32,864]{2,1,0:T(8,128)(2,1)S(1)} %copy-done, ...), custom_call_target="tpu_custom_call" | custom-call | flops 2147483648 | bytes 1048576 | tf_op jit(solution)/shard_map/core/pallas_call | solution.py:634
  21.4 0.3 collective-permute-done.4.before_ref
  21.7 0.0 collective-permute-done.5.after_ref
  21.8 0.1 collective-permute-start.6
  21.8 3.8 %collective-permute-start.7 = (bf16[112,128]{1,0:T(8,128)(2,1)S(1)}, bf16[112,128]{1,0:T(8,128)(2,1)S(1)}, u32[]{:S(2)}, u32[]{:S(2)}) collective-permute-start(bf16[112,128]{1,0:T(8,128)(2,1)S(1)} %maximum_bitcast_fusion.1.low_ref), channel_id=1, source_target_pairs={{0,3},{1,0},{2,1},{3,2},{4,7},{5,4},{6,5},{7,6},{8,11},{9,8},{10,9... | collective-permute-start | bytes 86024 | tf_op jit(solution)/shard_map/ppermute | solution.py:64
  25.6 1.6 %outer.1.outer_ref = bf16[3,864,256]{2,1,0:T(8,128)(2,1)S(1)} custom-call(bf16[1024,256]{1,0:T(8,128)(2,1)S(1)} %get-tuple-element.32.own_ref, bf16[384,128]{1,0:T(8,128)(2,1)S(1)} %collective-permute-done.4.before_ref, bf16[384,128]{1,0:T(8,128)(2,1)S(1)} %collective-permute-done.5.after_ref, bf16[3,256,2304]{2,1,0:T(8,128)(2,1)S(1)} %get-tuple-element.35.band_ref, ...), custom_call_target="tpu_custom_call" | custom-call | flops 2147483648 | bytes 1048576 | tf_op jit(solution)/shard_map/outer/pallas_call | solution.py:649
  27.3 0.4 %collective-permute-done.6.below_ref = bf16[112,128]{1,0:T(8,128)(2,1)S(1)} collective-permute-done((bf16[112,128]{1,0:T(8,128)(2,1)S(1)}, bf16[112,128]{1,0:T(8,128)(2,1)S(1)}, u32[]{:S(2)}, u32[]{:S(2)}) %collective-permute-start.6) | collective-permute-done | bytes 28704 | tf_op jit(solution)/shard_map/ppermute | solution.py:64
  27.7 0.0 collective-permute-done.7.above_ref
  27.7 0.0 copy-done.2
  27.7 7.8 %pick.1 = f32[3,1,10240]{2,1,0:T(1,128)} custom-call(bf16[3,864,256]{2,1,0:T(8,128)(2,1)S(1)} %get-tuple-element.31.middle_ref, bf16[3,864,256]{2,1,0:T(8,128)(2,1)S(1)} %outer.1.outer_ref, bf16[1024,256]{1,0:T(8,128)(2,1)S(1)} %get-tuple-element.32.own_ref, bf16[112,128]{1,0:T(8,128)(2,1)S(1)} %collective-permute-done.6.below_ref, ...), custom_call_target="tpu_custom_call" | custom-call | flops 8589934592 | bytes 1048576 | tf_op jit(solution)/shard_map/pick/pallas_call | solution.py:658
  (13 shorter events, 0.1 us)
Async XLA Ops:
  1.1 8.3 %collective-permute-start = (bf16[216,128]{1,0:T(8,128)(2,1)S(1)}, bf16[216,128]{1,0:T(8,128)(2,1)S(1)}, u32[]{:S(2)}, u32[]{:S(2)}) collective-permute-start(bf16[216,128]{1,0:T(8,128)(2,1)S(1)} %get-tuple-element.22), channel_id=1, source_target_pairs={{0,3},{1,0},{2,1},{3,2},{4,7},{5,4},{6,5},{7,6},{8,11},{9,8},{10,9... | collective-permute-start | bytes 165896 | tf_op jit(solution)/shard_map/ppermute | solution.py:64
  6.2 6.0 %collective-permute-start.1 = (bf16[216,128]{1,0:T(8,128)(2,1)S(1)}, bf16[216,128]{1,0:T(8,128)(2,1)S(1)}, u32[]{:S(2)}, u32[]{:S(2)}) collective-permute-start(bf16[216,128]{1,0:T(8,128)(2,1)S(1)} %get-tuple-element.23), channel_id=1, source_target_pairs={{0,1},{1,2},{2,3},{3,0},{4,5},{5,6},{6,7},{7,4},{8,9},{9,10},{10,1... | collective-permute-start | bytes 165896 | tf_op jit(solution)/shard_map/ppermute | solution.py:64
  6.2 3.0 %copy-start.3 = (bf16[32,16]{0,1:T(8,128)(2,1)S(1)}, bf16[32,16]{0,1:T(8,128)(2,1)}, u32[]{:S(2)}) copy-start(bf16[32,16]{0,1:T(8,128)(2,1)} %param.15) | copy-start | bytes 3076
  6.2 3.1 %copy-start.4 = (f32[3,32]{1,0:T(4,128)S(1)}, f32[3,32]{1,0:T(4,128)}, u32[]{:S(2)}) copy-start(f32[3,32]{1,0:T(4,128)} %param.17) | copy-start | bytes 1156
  12.2 4.2 %collective-permute-start.3 = (bf16[216,128]{1,0:T(8,128)(2,1)S(1)}, bf16[216,128]{1,0:T(8,128)(2,1)S(1)}, u32[]{:S(2)}, u32[]{:S(2)}) collective-permute-start(bf16[216,128]{1,0:T(8,128)(2,1)S(1)} %get-tuple-element.43), channel_id=1, source_target_pairs={{0,12},{4,8},{8,4},{12,0},{1,13},{5,9},{9,5},{13,1},{2,14},{6,10},... | collective-permute-start | bytes 165896 | tf_op jit(solution)/shard_map/ppermute | solution.py:75
  12.2 4.1 %collective-permute-start.2 = (bf16[216,128]{1,0:T(8,128)(2,1)S(1)}, bf16[216,128]{1,0:T(8,128)(2,1)S(1)}, u32[]{:S(2)}, u32[]{:S(2)}) collective-permute-start(bf16[216,128]{1,0:T(8,128)(2,1)S(1)} %get-tuple-element.44), channel_id=1, source_target_pairs={{0,4},{4,0},{8,12},{12,8},{1,5},{5,1},{9,13},{13,9},{2,6},{6,2},{1... | collective-permute-start | bytes 165896 | tf_op jit(solution)/shard_map/ppermute | solution.py:74
  16.4 3.1 %copy-start = (bf16[3,32,864]{2,1,0:T(8,128)(2,1)S(1)}, bf16[3,32,864]{2,1,0:T(8,128)(2,1)}, u32[]{:S(2)}) copy-start(bf16[3,32,864]{2,1,0:T(8,128)(2,1)} %weight_ref.1) | copy-start | bytes 497668
  16.4 3.1 %copy-start.1 = (bf16[3,32]{1,0:T(4,128)(2,1)S(1)}, bf16[3,32]{1,0:T(4,128)(2,1)}, u32[]{:S(2)}) copy-start(bf16[3,32]{1,0:T(4,128)(2,1)} %decoder_ref.1) | copy-start | bytes 580
  17.6 4.1 %collective-permute-start.4 = (bf16[384,128]{1,0:T(8,128)(2,1)S(1)}, bf16[384,128]{1,0:T(8,128)(2,1)S(1)}, u32[]{:S(2)}, u32[]{:S(2)}) collective-permute-start(bf16[384,128]{1,0:T(8,128)(2,1)S(1)} %get-tuple-element.33), channel_id=1, source_target_pairs={{0,4},{4,8},{8,12},{12,0},{1,5},{5,9},{9,13},{13,1},{2,6},{6,10},{... | collective-permute-start | bytes 294920 | tf_op jit(solution)/shard_map/ppermute | solution.py:64
  17.8 3.9 %collective-permute-start.5 = (bf16[384,128]{1,0:T(8,128)(2,1)S(1)}, bf16[384,128]{1,0:T(8,128)(2,1)S(1)}, u32[]{:S(2)}, u32[]{:S(2)}) collective-permute-start(bf16[384,128]{1,0:T(8,128)(2,1)S(1)} %get-tuple-element.34), channel_id=1, source_target_pairs={{0,12},{4,0},{8,4},{12,8},{1,13},{5,1},{9,5},{13,9},{2,14},{6,2},{... | collective-permute-start | bytes 294920 | tf_op jit(solution)/shard_map/ppermute | solution.py:64
  21.8 5.9 %collective-permute-start.6 = (bf16[112,128]{1,0:T(8,128)(2,1)S(1)}, bf16[112,128]{1,0:T(8,128)(2,1)S(1)}, u32[]{:S(2)}, u32[]{:S(2)}) collective-permute-start(bf16[112,128]{1,0:T(8,128)(2,1)S(1)} %maximum_bitcast_fusion.high_ref), channel_id=1, source_target_pairs={{0,1},{1,2},{2,3},{3,0},{4,5},{5,6},{6,7},{7,4},{8,9},{9,10},{10,1... | collective-permute-start | bytes 86024 | tf_op jit(solution)/shard_map/ppermute | solution.py:64
  21.8 5.8 %collective-permute-start.7 = (bf16[112,128]{1,0:T(8,128)(2,1)S(1)}, bf16[112,128]{1,0:T(8,128)(2,1)S(1)}, u32[]{:S(2)}, u32[]{:S(2)}) collective-permute-start(bf16[112,128]{1,0:T(8,128)(2,1)S(1)} %maximum_bitcast_fusion.1.low_ref), channel_id=1, source_target_pairs={{0,3},{1,0},{2,1},{3,2},{4,7},{5,4},{6,5},{7,6},{8,11},{9,8},{10,9... | collective-permute-start | bytes 86024 | tf_op jit(solution)/shard_map/ppermute | solution.py:64
  25.6 2.0 %copy-start.2 = (bf16[3,16]{1,0:T(4,128)(2,1)S(1)}, bf16[3,16]{1,0:T(4,128)(2,1)}, u32[]{:S(2)}) copy-start(bf16[3,16]{1,0:T(4,128)(2,1)} %self_ref.1) | copy-start | bytes 292
